TPU v7x, 32 devices: a whole 2x2x4 slice. The times are simulated.
32 devices in a mesh: fsdp: 16 (over z, x, core), seq: 2 (over y).
Axes of the slice: x: 2, y: 2, z: 4, core: 2. Of those that a mesh axis runs over, the one named last changes fastest.
Arguments:
- tokens: bfloat16 [16, 256, 1024], P('fsdp', 'seq'), may hold values from -6 to 6
- visible: int32 [16], P('fsdp'), may hold values from 157 to 250, as said below
- first_gain: bfloat16 [1024], P('fsdp'), may hold values from 0.25 to 1.75
- first_shift: bfloat16 [1024], P('fsdp'), may hold values from -3 to 3
- inward_weight: bfloat16 [1024, 3072], P('fsdp'), may hold values from -0.1875 to 0.1875
- query_bias: bfloat16 [1024], P('fsdp'), may hold values from -3 to 3
- value_bias: bfloat16 [1024], P('fsdp'), may hold values from -3 to 3
- outward_weight: bfloat16 [1024, 1024], P('fsdp'), may hold values from -2 to 2
- outward_bias: bfloat16 [1024], P('fsdp'), may hold values from -3 to 3
- second_gain: bfloat16 [1024], P('fsdp'), may hold values from 0.25 to 1.75
- second_shift: bfloat16 [1024], P('fsdp'), may hold values from -3 to 3
- expand_weight: bfloat16 [1024, 4096], P('fsdp'), may hold values from -0.1875 to 0.1875
- expand_bias: bfloat16 [4096], P('fsdp'), may hold values from -3 to 3
- shrink_weight: bfloat16 [4096, 1024], P('fsdp'), may hold values from -0.09375 to 0.09375
- shrink_bias: bfloat16 [1024], P('fsdp'), may hold values from -3 to 3
- upstream: bfloat16 [16, 256, 1024], P('fsdp', 'seq'), may hold values from -6 to 6
Outputs:
- layer_out: bfloat16 [16, 256, 1024], P('fsdp', 'seq')
- tokens_grad: float32 [16, 256, 1024], P('fsdp', 'seq')
- first_gain_grad: float32 [1024], P(('fsdp', 'seq'))
- first_shift_grad: float32 [1024], P(('fsdp', 'seq'))
- inward_weight_grad: float32 [1024, 3072], P(('fsdp', 'seq'))
- query_bias_grad: float32 [1024], P(('fsdp', 'seq'))
- value_bias_grad: float32 [1024], P(('fsdp', 'seq'))
- outward_weight_grad: float32 [1024, 1024], P(('fsdp', 'seq'))
- outward_bias_grad: float32 [1024], P(('fsdp', 'seq'))
- second_gain_grad: float32 [1024], P(('fsdp', 'seq'))
- second_shift_grad: float32 [1024], P(('fsdp', 'seq'))
- expand_weight_grad: float32 [1024, 4096], P(('fsdp', 'seq'))
- expand_bias_grad: float32 [4096], P(('fsdp', 'seq'))
- shrink_weight_grad: float32 [4096, 1024], P(('fsdp', 'seq'))
- shrink_bias_grad: float32 [1024], P(('fsdp', 'seq'))
Inputs may be any that keep to these rules, and one draw needn't show every extreme that they name: Clip i's visible tokens fill its first visible[i] slots; the remaining slots are padding. Some clip has exactly 250 and some exactly 157 visible tokens.
All inputs are finite; a program needn't handle non-finite values.
Results may differ from a plain program's by a relative error of at most 0.012.
Values may be sent and summed in bfloat16 or wider, within the bound.
A program may use at most 192 MiB of HBM per device.

v0:
```python
import jax
import jax.numpy as jnp
from jax import lax
from jax.sharding import PartitionSpec as P

HEADS = 16


epsilon = 1e-06


def norm_rows(inputs, norm_gain, norm_shift):
    row_mean = jnp.mean(inputs, axis=-1, keepdims=True)
    centered = inputs - row_mean
    variance = jnp.mean(centered * centered, axis=-1, keepdims=True)
    inverse = lax.rsqrt(variance + epsilon)
    normed = centered * inverse
    return (normed * norm_gain + norm_shift, normed, inverse)


def norm_back(grad_out, normed, inverse, norm_gain):
    scaled = grad_out * norm_gain
    first_mean = jnp.mean(scaled, axis=-1, keepdims=True)
    second_mean = jnp.mean(scaled * normed, axis=-1, keepdims=True)
    return inverse * (scaled - first_mean - normed * second_mean)


def gather_weights(
    first_gain,
    first_shift,
    inward_weight,
    query_bias,
    value_bias,
    outward_weight,
    outward_bias,
    second_gain,
    second_shift,
    expand_weight,
    expand_bias,
    shrink_weight,
    shrink_bias,
):
    return (
        lax.all_gather(first_gain, "fsdp", axis=0, tiled=True),
        lax.all_gather(first_shift, "fsdp", axis=0, tiled=True),
        lax.all_gather(inward_weight, "fsdp", axis=0, tiled=True),
        lax.all_gather(query_bias, "fsdp", axis=0, tiled=True),
        lax.all_gather(value_bias, "fsdp", axis=0, tiled=True),
        lax.all_gather(outward_weight, "fsdp", axis=0, tiled=True),
        lax.all_gather(outward_bias, "fsdp", axis=0, tiled=True),
        lax.all_gather(second_gain, "fsdp", axis=0, tiled=True),
        lax.all_gather(second_shift, "fsdp", axis=0, tiled=True),
        lax.all_gather(expand_weight, "fsdp", axis=0, tiled=True),
        lax.all_gather(expand_bias, "fsdp", axis=0, tiled=True),
        lax.all_gather(shrink_weight, "fsdp", axis=0, tiled=True),
        lax.all_gather(shrink_bias, "fsdp", axis=0, tiled=True),
    )


def attend_scores(query_heads, key_heads, key_valid, scale):
    scores = (
        jnp.einsum("cqhe,ckhe->chqk", query_heads, key_heads, preferred_element_type=jnp.float32)
        * scale
    )
    return jnp.where(key_valid[:, None, None, :], scores, -1e30)


def forward(tokens32, key_valid, row_valid, gathered):
    (
        first_gain,
        first_shift,
        inward_weight,
        query_bias,
        value_bias,
        outward_weight,
        outward_bias,
        second_gain,
        second_shift,
        expand_weight,
        expand_bias,
        shrink_weight,
        shrink_bias,
    ) = gathered
    clip_count, seg_rows, model_width = tokens32.shape
    head_size = model_width // HEADS
    scale = head_size ** (-0.5)
    affine_first, normed_first, inverse_first = norm_rows(
        tokens32, first_gain.astype(jnp.float32), first_shift.astype(jnp.float32)
    )
    lowered_first = affine_first.astype(jnp.bfloat16)
    merged_bias = jnp.concatenate([query_bias, jnp.zeros_like(query_bias), value_bias]).astype(
        jnp.float32
    )
    project = (
        jnp.einsum("csd,de->cse", lowered_first, inward_weight, preferred_element_type=jnp.float32)
        + merged_bias
    )
    queries = project[..., :model_width].astype(jnp.bfloat16)
    key_local = project[..., model_width : 2 * model_width].astype(jnp.bfloat16)
    value_local = project[..., 2 * model_width :].astype(jnp.bfloat16)
    key_all, value_all = (
        lax.all_gather(key_local, "seq", axis=1, tiled=True),
        lax.all_gather(value_local, "seq", axis=1, tiled=True),
    )
    slot_count = key_all.shape[1]
    query_heads = queries.reshape(clip_count, seg_rows, HEADS, head_size)
    key_heads = key_all.reshape(clip_count, slot_count, HEADS, head_size)
    value_heads = value_all.reshape(clip_count, slot_count, HEADS, head_size)
    scores = attend_scores(query_heads, key_heads, key_valid, scale)
    row_top = jnp.max(scores, axis=-1, keepdims=True)
    row_total = jnp.sum(jnp.exp(scores - row_top), axis=-1, keepdims=True)
    log_total = row_top + jnp.log(row_total)
    soft_low = jnp.exp(scores - log_total).astype(jnp.bfloat16)
    blended = jnp.einsum(
        "chqk,ckhe->cqhe", soft_low, value_heads, preferred_element_type=jnp.float32
    )
    blended = blended.reshape(clip_count, seg_rows, model_width).astype(jnp.bfloat16)
    branch = jnp.einsum(
        "csd,de->cse", blended, outward_weight, preferred_element_type=jnp.float32
    ) + outward_bias.astype(jnp.float32)
    middle = tokens32 + branch
    affine_second, normed_second, inverse_second = norm_rows(
        middle, second_gain.astype(jnp.float32), second_shift.astype(jnp.float32)
    )
    lowered_second = affine_second.astype(jnp.bfloat16)
    hidden = jnp.einsum(
        "csd,df->csf", lowered_second, expand_weight, preferred_element_type=jnp.float32
    ) + expand_bias.astype(jnp.float32)
    active = jax.nn.gelu(hidden, approximate=False).astype(jnp.bfloat16)
    branch_second = jnp.einsum(
        "csf,fd->csd", active, shrink_weight, preferred_element_type=jnp.float32
    ) + shrink_bias.astype(jnp.float32)
    result = middle + branch_second
    output = jnp.where(row_valid, result, 0.0).astype(jnp.bfloat16)
    return {
        "normed_first": normed_first,
        "inverse_first": inverse_first,
        "lowered_first": lowered_first,
        "query_heads": query_heads,
        "key_heads": key_heads,
        "value_heads": value_heads,
        "log_total": log_total,
        "blended": blended,
        "normed_second": normed_second,
        "inverse_second": inverse_second,
        "lowered_second": lowered_second,
        "hidden": hidden,
        "active": active,
        "output": output,
    }


def gelu_exact(inputs):
    return jax.nn.gelu(inputs, approximate=False)


def backward(saved, gathered, upstream32, key_valid, row_valid):
    (
        first_gain,
        first_shift,
        inward_weight,
        query_bias,
        value_bias,
        outward_weight,
        outward_bias,
        second_gain,
        second_shift,
        expand_weight,
        expand_bias,
        shrink_weight,
        shrink_bias,
    ) = gathered
    clip_count, seg_rows, model_width = upstream32.shape
    head_size = model_width // HEADS
    scale = head_size ** (-0.5)
    grad_result = jnp.where(row_valid, upstream32, 0.0)
    grad_low_second = grad_result.astype(jnp.bfloat16)
    shrink_weight_grad = jnp.einsum(
        "csf,csd->fd", saved["active"], grad_low_second, preferred_element_type=jnp.float32
    )
    shrink_bias_grad = jnp.sum(grad_low_second.astype(jnp.float32), axis=(0, 1))
    grad_active = jnp.einsum(
        "csd,fd->csf", grad_low_second, shrink_weight, preferred_element_type=jnp.float32
    )
    gelu_value, gelu_pull = jax.vjp(gelu_exact, saved["hidden"])
    grad_hidden = gelu_pull(grad_active)[0].astype(jnp.bfloat16)
    expand_weight_grad = jnp.einsum(
        "csd,csf->df", saved["lowered_second"], grad_hidden, preferred_element_type=jnp.float32
    )
    expand_bias_grad = jnp.sum(grad_hidden.astype(jnp.float32), axis=(0, 1))
    grad_second = jnp.einsum(
        "csf,df->csd", grad_hidden, expand_weight, preferred_element_type=jnp.float32
    )
    second_gain_grad = jnp.sum(grad_second * saved["normed_second"], axis=(0, 1))
    second_shift_grad = jnp.sum(grad_second, axis=(0, 1))
    grad_middle = grad_result + norm_back(
        grad_second,
        saved["normed_second"],
        saved["inverse_second"],
        second_gain.astype(jnp.float32),
    )
    grad_low_first = grad_middle.astype(jnp.bfloat16)
    outward_weight_grad = jnp.einsum(
        "csd,cse->de", saved["blended"], grad_low_first, preferred_element_type=jnp.float32
    )
    outward_bias_grad = jnp.sum(grad_low_first.astype(jnp.float32), axis=(0, 1))
    grad_blended = jnp.einsum(
        "cse,de->csd", grad_low_first, outward_weight, preferred_element_type=jnp.float32
    )
    grad_blended = grad_blended.astype(jnp.bfloat16).reshape(clip_count, seg_rows, HEADS, head_size)
    query_heads = saved["query_heads"]
    key_heads = saved["key_heads"]
    value_heads = saved["value_heads"]
    slot_count = key_heads.shape[1]
    scores = attend_scores(query_heads, key_heads, key_valid, scale)
    soft = jnp.exp(scores - saved["log_total"])
    soft_low = soft.astype(jnp.bfloat16)
    grad_soft = jnp.einsum(
        "cqhe,ckhe->chqk", grad_blended, value_heads, preferred_element_type=jnp.float32
    )
    grad_scores = soft * (grad_soft - jnp.sum(grad_soft * soft, axis=-1, keepdims=True))
    grad_scores = grad_scores.astype(jnp.bfloat16)
    grad_queries = (
        jnp.einsum("chqk,ckhe->cqhe", grad_scores, key_heads, preferred_element_type=jnp.float32)
        * scale
    )
    grad_queries = grad_queries.astype(jnp.bfloat16).reshape(clip_count, seg_rows, model_width)
    grad_keys_part = (
        jnp.einsum("chqk,cqhe->ckhe", grad_scores, query_heads, preferred_element_type=jnp.float32)
        * scale
    )
    grad_values_part = jnp.einsum(
        "chqk,cqhe->ckhe", soft_low, grad_blended, preferred_element_type=jnp.float32
    )
    grad_keys_part = grad_keys_part.reshape(clip_count, slot_count, model_width)
    grad_values_part = grad_values_part.reshape(clip_count, slot_count, model_width)
    grad_keys, grad_values = (
        lax.psum_scatter(
            grad_keys_part.astype(jnp.bfloat16), "seq", scatter_dimension=1, tiled=True
        ).astype(jnp.float32),
        lax.psum_scatter(
            grad_values_part.astype(jnp.bfloat16), "seq", scatter_dimension=1, tiled=True
        ).astype(jnp.float32),
    )
    grad_keys = grad_keys.astype(jnp.bfloat16)
    grad_values = grad_values.astype(jnp.bfloat16)
    grad_project = jnp.concatenate([grad_queries, grad_keys, grad_values], axis=-1)
    inward_weight_grad = jnp.einsum(
        "csd,cse->de", saved["lowered_first"], grad_project, preferred_element_type=jnp.float32
    )
    query_bias_grad = jnp.sum(grad_queries.astype(jnp.float32), axis=(0, 1))
    value_bias_grad = jnp.sum(grad_values.astype(jnp.float32), axis=(0, 1))
    grad_first = jnp.einsum(
        "cse,de->csd", grad_project, inward_weight, preferred_element_type=jnp.float32
    )
    first_gain_grad = jnp.sum(grad_first * saved["normed_first"], axis=(0, 1))
    first_shift_grad = jnp.sum(grad_first, axis=(0, 1))
    tokens_grad = grad_middle + norm_back(
        grad_first, saved["normed_first"], saved["inverse_first"], first_gain.astype(jnp.float32)
    )
    weight_shares = (
        lax.psum_scatter(first_gain_grad, ("fsdp", "seq"), scatter_dimension=0, tiled=True),
        lax.psum_scatter(first_shift_grad, ("fsdp", "seq"), scatter_dimension=0, tiled=True),
        lax.psum_scatter(inward_weight_grad, ("fsdp", "seq"), scatter_dimension=0, tiled=True),
        lax.psum_scatter(query_bias_grad, ("fsdp", "seq"), scatter_dimension=0, tiled=True),
        lax.psum_scatter(value_bias_grad, ("fsdp", "seq"), scatter_dimension=0, tiled=True),
        lax.psum_scatter(outward_weight_grad, ("fsdp", "seq"), scatter_dimension=0, tiled=True),
        lax.psum_scatter(outward_bias_grad, ("fsdp", "seq"), scatter_dimension=0, tiled=True),
        lax.psum_scatter(second_gain_grad, ("fsdp", "seq"), scatter_dimension=0, tiled=True),
        lax.psum_scatter(second_shift_grad, ("fsdp", "seq"), scatter_dimension=0, tiled=True),
        lax.psum_scatter(expand_weight_grad, ("fsdp", "seq"), scatter_dimension=0, tiled=True),
        lax.psum_scatter(expand_bias_grad, ("fsdp", "seq"), scatter_dimension=0, tiled=True),
        lax.psum_scatter(shrink_weight_grad, ("fsdp", "seq"), scatter_dimension=0, tiled=True),
        lax.psum_scatter(shrink_bias_grad, ("fsdp", "seq"), scatter_dimension=0, tiled=True),
    )
    return (tokens_grad, weight_shares)


def shards(
    tokens,
    visible,
    first_gain,
    first_shift,
    inward_weight,
    query_bias,
    value_bias,
    outward_weight,
    outward_bias,
    second_gain,
    second_shift,
    expand_weight,
    expand_bias,
    shrink_weight,
    shrink_bias,
    upstream,
):
    clip_count, seg_rows, model_width = tokens.shape
    slot_count = seg_rows * lax.axis_size("seq")
    local_start = lax.axis_index("seq") * seg_rows
    row_positions = local_start + jnp.arange(seg_rows, dtype=jnp.int32)
    row_valid = (row_positions[None, :] < visible[:, None])[..., None]
    key_valid = jnp.arange(slot_count, dtype=jnp.int32)[None, :] < visible[:, None]
    tokens32 = tokens.astype(jnp.float32)
    upstream32 = upstream.astype(jnp.float32)
    gathered = gather_weights(
        first_gain,
        first_shift,
        inward_weight,
        query_bias,
        value_bias,
        outward_weight,
        outward_bias,
        second_gain,
        second_shift,
        expand_weight,
        expand_bias,
        shrink_weight,
        shrink_bias,
    )
    saved = forward(tokens32, key_valid, row_valid, gathered)
    layer_out = saved["output"]
    gathered = gather_weights(
        first_gain,
        first_shift,
        inward_weight,
        query_bias,
        value_bias,
        outward_weight,
        outward_bias,
        second_gain,
        second_shift,
        expand_weight,
        expand_bias,
        shrink_weight,
        shrink_bias,
    )
    saved = forward(tokens32, key_valid, row_valid, gathered)
    tokens_grad, shares = backward(saved, gathered, upstream32, key_valid, row_valid)
    return (
        layer_out,
        tokens_grad,
        shares[0],
        shares[1],
        shares[2],
        shares[3],
        shares[4],
        shares[5],
        shares[6],
        shares[7],
        shares[8],
        shares[9],
        shares[10],
        shares[11],
        shares[12],
    )


def solution(mesh):
    in_specs = (
        P("fsdp", "seq", None),
        P("fsdp"),
        P("fsdp"),
        P("fsdp"),
        P("fsdp", None),
        P("fsdp"),
        P("fsdp"),
        P("fsdp", None),
        P("fsdp"),
        P("fsdp"),
        P("fsdp"),
        P("fsdp", None),
        P("fsdp"),
        P("fsdp", None),
        P("fsdp"),
        P("fsdp", "seq", None),
    )
    out_specs = (
        P("fsdp", "seq", None),
        P("fsdp", "seq", None),
        P(("fsdp", "seq")),
        P(("fsdp", "seq")),
        P(("fsdp", "seq"), None),
        P(("fsdp", "seq")),
        P(("fsdp", "seq")),
        P(("fsdp", "seq"), None),
        P(("fsdp", "seq")),
        P(("fsdp", "seq")),
        P(("fsdp", "seq")),
        P(("fsdp", "seq"), None),
        P(("fsdp", "seq")),
        P(("fsdp", "seq"), None),
        P(("fsdp", "seq")),
    )
    return jax.shard_map(shards, mesh=mesh, in_specs=in_specs, out_specs=out_specs, check_vma=False)
```

profile of v0, /device:TPU:0, one launch (start us, length us, event | category | flops | bytes accessed | tf_op | source)
XLA Modules:
  0.0 1356.3 jit_solution(4544401787546621798)
XLA Ops:
  7.2 0.7 all-gather.6.cloned.1.call-update
  8.0 0.7 all-gather.8.cloned.1.call-update
  8.7 0.7 all-gather.10.cloned.1.call-update
  10.0 1.2 dynamic-slice
  11.9 0.8 dynamic-update-slice.3
  12.8 0.8 dynamic-update-slice.2
  13.6 0.8 dynamic-update-slice.1
  14.5 0.8 dynamic-update-slice
  15.3 0.8 dynamic-update-slice.4
  16.1 0.8 dynamic-update-slice.7
  17.0 0.8 dynamic-update-slice.6
  17.8 0.8 dynamic-update-slice.5
  18.6 65.1 %all-reduce.18 = (bf16[1024]{0:T(1024)(128)(2,1)S(1)}, bf16[1024]{0:T(1024)(128)(2,1)S(1)}, bf16[1024]{0:T(1024)(128)(2,1)S(1)}, bf16[1024]{0:T(1024)(128)(2,1)S...) all-reduce(bf16[1024]{0:T(1024)(128)(2,1)S(1)} %dynamic-update-slic, ...), channel_id=1, replica_groups=mesh['fsdp'=16,'seq'=2] {'fsdp'}, use_global_device_ids=true, to_apply=%add.3 | all-reduce | flops 8192 | bytes 32768
  84.4 0.7 reshape.468
  85.0 17.1 %all-gather = bf16[16,1,256]{2,1,0:T(2,128)(2,1)S(1)} all-gather(bf16[1,1,256]{2,1,0:T(2,128)(2,1)S(1)} %reshape.468), channel_id=1, replica_groups=mesh['fsdp'=16,'seq'=2] {'fsdp'}, dimensions={0}, use_global_device_ids=true | all-gather | bytes 8704 | tf_op jit(solution)/shard_map/all_gather | solution.py:54
  102.3 1.1 convert_reduce_fusion.1
  103.6 3.9 fusion.1
  107.6 9.2 all_gather.64
  117.0 0.9 copy.44
  117.9 8.8 all_gather.65
  126.9 1.7 fusion.66
  128.7 0.7 exponential_reduce_fusion
  129.3 1.3 convolution_convert_fusion.2
  130.6 2.2 fusion.67
  133.1 59.7 %all-gather.10.cloned.1.call-done = bf16[1024,4096]{1,0:T(8,128)(2,1)} async-done(((bf16[64,4096]{1,0:T(8,128)(2,1)}), bf16[1024,4096]{1,0:T(8,128)(2,1)}) %all-gather.10.cloned.1.call-update) | async-done | bytes 8388624 | tf_op jit(solution)/shard_map/all_gather | solution.py:53
  192.8 6.1 convolution_add_fusion
  198.8 68.9 %all-gather.12.cloned.1.call-done = bf16[4096,1024]{1,0:T(8,128)(2,1)} async-done(((bf16[256,1024]{1,0:T(8,128)(2,1)}), bf16[4096,1024]{1,0:T(8,128)(2,1)}) %all-gather.12.cloned.1.call-update) | async-done | bytes 8388624 | tf_op jit(solution)/shard_map/all_gather | solution.py:55
  267.7 9.9 convert_reduce_fusion
  277.6 3.0 fusion.31
  281.1 1.1 copy-done.4
  282.2 1.5 convolution_convert_fusion.1
  283.8 1.8 copy.46
  285.6 2.3 convolution_convert_fusion
  287.9 3.6 copy.49
  291.5 2.2 copy.55
  293.9 2.0 multiply_reduce_fusion
  295.9 0.8 multiply_convert_fusion
  296.7 1.0 copy-done.2
  298.0 1.0 copy.47
  299.0 1.0 copy.56
  300.1 2.8 fusion.42
  302.9 1.2 copy-done.3
  304.8 2.3 reduce-scatter.21.cloned.1.call-done
  307.1 1.2 reshape_bitcast_fusion
  308.7 15.6 %reduce-scatter.19.cloned.1.call-done = bf16[128,1024]{1,0:T(8,128)(2,1)} async-done(((bf16[256,1024]{1,0:T(8,128)(2,1)}), bf16[128,1024]{1,0:T(8,128)(2,1)}) %reduce-scatter.19.cloned.1.call-update) | async-done | bytes 262160
  324.4 1.2 reshape_bitcast_fusion.1
  326.1 6.4 fusion.36
  332.6 1.2 copy-done.9
  333.8 8.2 fusion.59
  342.2 0.7 copy-done.14
  342.9 10.9 fusion.45
  354.0 10.1 fusion.16
  364.2 5.1 fusion.29
  369.5 40.5 %all-reduce.17 = (f32[1024]{0:T(1024)S(1)}, f32[1024]{0:T(1024)S(1)}, f32[1024]{0:T(1024)S(1)}, f32[1024]{0:T(1024)S(1)}, f32[1024]{0:T(1024)S(1)}, /*index=5*/f...) all-reduce(f32[1024]{0:T(1024)S(1)} %get-tuple-element.17, ...), channel_id=4, replica_groups=mesh['fsdp'=16,'seq'=2] {'fsdp','seq'}, use_global_device_ids=true, to_apply=%region_14.15.clone | all-reduce | flops 12288 | bytes 98304
  410.0 0.6 dynamic-slice.8
  410.6 0.6 dynamic-slice.9
  411.1 0.6 dynamic-slice.10
  412.9 0.6 dynamic-slice.13
  414.6 0.6 dynamic-slice.15
  415.2 1.0 fusion.28
  416.3 54.3 %reduce-scatter.13.cloned.1.call-done = f32[32,1024]{1,0:T(8,128)} async-done(((f32[1024,1024]{1,0:T(8,128)}), f32[32,1024]{1,0:T(8,128)}) %reduce-scatter.13.cloned.1.call-update) | async-done | bytes 131088 | tf_op jit(solution)/shard_map/reduce_scatter | solution.py:267
  470.6 158.2 %reduce-scatter.11.cloned.1.call-done = f32[32,3072]{1,0:T(8,128)} async-done(((f32[1024,3072]{1,0:T(8,128)}), f32[32,3072]{1,0:T(8,128)}) %reduce-scatter.11.cloned.1.call-update) | async-done | bytes 393232 | tf_op jit(solution)/shard_map/reduce_scatter | solution.py:264
  628.8 359.2 %reduce-scatter.15.cloned.1.call-done = f32[32,4096]{1,0:T(8,128)} async-done(((f32[1024,4096]{1,0:T(8,128)}), f32[32,4096]{1,0:T(8,128)}) %reduce-scatter.15.cloned.1.call-update) | async-done | bytes 524304 | tf_op jit(solution)/shard_map/reduce_scatter | solution.py:271
  988.0 361.3 %reduce-scatter.17.cloned.1.call-done = f32[128,1024]{1,0:T(8,128)} async-done(((f32[4096,1024]{1,0:T(8,128)}), f32[128,1024]{1,0:T(8,128)}) %reduce-scatter.17.cloned.1.call-update) | async-done | bytes 524304 | tf_op jit(solution)/shard_map/reduce_scatter | solution.py:273
  (89 shorter events, 7.5 us)
Async XLA Ops:
  7.2 96.2 %copy-start.1 = (bf16[1,128,1024]{2,1,0:T(8,128)(2,1)S(1)}, bf16[1,128,1024]{2,1,0:T(8,128)(2,1)}, u32[]{:S(2)}) copy-start(bf16[1,128,1024]{2,1,0:T(8,128)(2,1)} %param.16) | copy-start | bytes 786436
  7.2 96.4 %all-gather.6.cloned.1.call-start = ((), (), s32[]{:S(2)}) async-start(), calls=%async_computation.6 | async-start | bytes 6684672 | tf_op jit(solution)/shard_map/all_gather | solution.py:46
  7.9 122.7 %all-gather.8.cloned.1.call-start = ((), (), s32[]{:S(2)}) async-start(), calls=%async_computation.7 | async-start | bytes 2228224 | tf_op jit(solution)/shard_map/all_gather | solution.py:49
  8.7 184.1 %all-gather.10.cloned.1.call-start = ((), (), s32[]{:S(2)}) async-start(), calls=%async_computation.8 | async-start | bytes 8912896 | tf_op jit(solution)/shard_map/all_gather | solution.py:53
  9.4 258.3 %all-gather.12.cloned.1.call-start = ((), (), s32[]{:S(2)}) async-start(), calls=%async_computation.9 | async-start | bytes 8912896 | tf_op jit(solution)/shard_map/all_gather | solution.py:55
  10.0 297.1 %reduce-scatter.21.cloned.1.call-start = ((), (), s32[]{:S(2)}) async-start(), calls=%async_computation.15 | async-start | bytes 786432
  117.0 12.3 copy-start.7
  126.9 2.4 copy-start.5
  192.8 74.9 %copy-start.12 = (bf16[1,128,1024]{2,1,0:T(8,128)(2,1)S(1)}, bf16[1,128,1024]{2,1,0:T(8,128)(2,1)}, u32[]{:S(2)}) copy-start(bf16[1,128,1024]{2,1,0:T(8,128)(2,1)} %param.31) | copy-start | bytes 786436
  267.7 9.9 copy-start
  277.6 3.0 copy-start.8
  277.6 3.2 copy-start.13
  280.6 1.6 copy-start.4
  293.7 30.7 %reduce-scatter.19.cloned.1.call-start = ((), (), s32[]{:S(2)}) async-start(), calls=%async_computation.14 | async-start | bytes 786432
  295.9 1.8 copy-start.10
  296.7 1.0 copy-start.2
  298.0 2.1 copy-start.11
  300.0 170.6 %reduce-scatter.13.cloned.1.call-start = ((), (), s32[]{:S(2)}) async-start(), calls=%async_computation.11 | async-start | bytes 4325376 | tf_op jit(solution)/shard_map/reduce_scatter | solution.py:267
  302.8 1.2 copy-start.3
  302.8 1.4 copy-start.6
  302.9 325.9 %reduce-scatter.11.cloned.1.call-start = ((), (), s32[]{:S(2)}) async-start(), calls=%async_computation.10 | async-start | bytes 12976128 | tf_op jit(solution)/shard_map/reduce_scatter | solution.py:264
  332.5 1.3 copy-start.9
  332.5 655.4 %reduce-scatter.15.cloned.1.call-start = ((), (), s32[]{:S(2)}) async-start(), calls=%async_computation.12 | async-start | bytes 17301504 | tf_op jit(solution)/shard_map/reduce_scatter | solution.py:271
  341.9 0.9 copy-start.14
  342.0 1007.3 %reduce-scatter.17.cloned.1.call-start = ((), (), s32[]{:S(2)}) async-start(), calls=%async_computation.13 | async-start | bytes 17301504 | tf_op jit(solution)/shard_map/reduce_scatter | solution.py:273
Sparse Core Ops, SparseCore 0:
  10.3 64.7 all-gather.5
  77.2 40.1 all-gather.7
  119.6 73.0 all-gather.9
  194.8 72.8 all-gather.11
  293.8 13.2 reduce-scatter.20
  309.7 14.6 reduce-scatter.18
  327.2 143.3 reduce-scatter.12
  477.2 151.5 reduce-scatter.10
  631.7 356.2 reduce-scatter.14
  990.7 358.5 reduce-scatter.16
where the time goes:
time: 1360 us
  waiting for transfers between devices  1080 us (79%)
  blocking collectives  141 us (10%)
  matrix products  78.4 us (6%)
  local copies, waits for them, and re-layouts  33.4 us (2%)
  between operations  16.1 us (1%)
    reduce_scatter x1, waiting for transfers between devices, backward(): lax.psum_scatter(shrink_weight_grad, ('fsdp', 'seq'), scatter_dimension=0...  361 us
    reduce_scatter x1, waiting for transfers between devices, backward(): lax.psum_scatter(expand_weight_grad, ('fsdp', 'seq'), scatter_dimension=0...  359 us
    reduce_scatter x1, waiting for transfers between devices, backward(): lax.psum_scatter(inward_weight_grad, ('fsdp', 'seq'), scatter_dimension=0...  158 us
    unnamed x2, blocking collectives  106 us
    all_gather x1, waiting for transfers between devices, gather_weights(): lax.all_gather(shrink_weight, 'fsdp', axis=0, tiled=True)  68.9 us
    all_gather x1, waiting for transfers between devices, gather_weights(): lax.all_gather(expand_weight, 'fsdp', axis=0, tiled=True)  59.7 us
    reduce_scatter x1, waiting for transfers between devices, backward(): lax.psum_scatter(outward_weight_grad, ('fsdp', 'seq'), scatter_dimension=...  54.3 us
    unnamed x66, local copies, waits for them, and re-layouts  30.2 us
  transfers between devices with their start and end apart: 10, of which 8 were waited for; matrix products, arithmetic and copies ran while one was open for 6% of the time, Pallas kernels for 0%

commit v1 on v0

--- a/solution.py
+++ b/solution.py
@@ -1,6 +1,10 @@
+import functools
+
 import jax
 import jax.numpy as jnp
 from jax import lax
+from jax.experimental import pallas as pl
+from jax.experimental.pallas import tpu as pltpu
 from jax.sharding import PartitionSpec as P
 
 HEADS = 16
@@ -355,6 +359,879 @@
     )
 
 
+F32 = jnp.float32
+BF16 = jnp.bfloat16
+MESH = pl.DeviceIdType.MESH
+SLAB = 8
+
+
+def matmul(a, b):
+    return lax.dot_general(a, b, (((1,), (0,)), ((), ())), preferred_element_type=F32)
+
+
+def matmul_bt(a, b):
+    return lax.dot_general(a, b, (((1,), (1,)), ((), ())), preferred_element_type=F32)
+
+
+def matmul_at(a, b):
+    return lax.dot_general(a, b, (((0,), (0,)), ((), ())), preferred_element_type=F32)
+
+
+def row_stats(x):
+    mean = jnp.mean(x, axis=-1, keepdims=True)
+    centered = x - mean
+    inverse = lax.rsqrt(jnp.mean(centered * centered, axis=-1, keepdims=True) + epsilon)
+    return centered * inverse, inverse
+
+
+def row_norm_back(grad, normed, inverse, gain):
+    scaled = grad * gain
+    first_mean = jnp.mean(scaled, axis=-1, keepdims=True)
+    second_mean = jnp.mean(scaled * normed, axis=-1, keepdims=True)
+    return inverse * (scaled - first_mean - normed * second_mean)
+
+
+class Place:
+    def __init__(self, groups):
+        self.groups = groups
+        self.f = lax.axis_index("fsdp")
+        self.y = lax.axis_index("seq")
+        self.r = self.f // 4
+        self.xc = self.f % 4
+        self.t = self.xc * 2 + self.y
+        x, c = self.xc // 2, self.xc % 2
+        self.step = {4: 4 - 8 * x, 2: 2 - 4 * c, 1: 1 - 2 * self.y}
+
+    def peer(self, mask):
+        at = self.t
+        for bit in (4, 2, 1):
+            if mask & bit:
+                at = at + self.step[bit]
+        return at
+
+    def device(self, r, t):
+        return (r * 4 + t // 2, t % 2)
+
+
+def rows(ref, index, size):
+    return ref.at[pl.ds(pl.multiple_of(index * size, size), size), :]
+
+
+def cols(ref, index, size):
+    return ref.at[:, pl.ds(pl.multiple_of(index * size, size), size)]
+
+
+class Wire:
+    def __init__(self, place, send_sems, recv_sems, local_sems):
+        self.place = place
+        self.send_sems, self.recv_sems, self.local_sems = send_sems, recv_sems, local_sems
+        self.sends = self.recvs = self.locals = 0
+        self.open_sends = []
+
+    def recv_slots(self, count):
+        first = self.recvs
+        self.recvs += count
+        return [self.recv_sems.at[first + i] for i in range(count)]
+
+    def send(self, src, dst, slot, to):
+        copy = pltpu.make_async_remote_copy(
+            src_ref=src,
+            dst_ref=dst,
+            send_sem=self.send_sems.at[self.sends],
+            recv_sem=slot,
+            device_id=self.place.device(*to),
+            device_id_type=MESH,
+        )
+        self.sends += 1
+        copy.start()
+        self.open_sends.append(copy)
+
+    def arrived(self, dst, slot):
+        pltpu.make_async_remote_copy(
+            src_ref=dst,
+            dst_ref=dst,
+            send_sem=self.send_sems.at[0],
+            recv_sem=slot,
+            device_id=self.place.device(self.place.r, self.place.peer(2)),
+            device_id_type=MESH,
+        ).wait_recv()
+
+    def local(self, src, dst):
+        copy = pltpu.make_async_copy(src, dst, self.local_sems.at[self.locals])
+        self.locals += 1
+        copy.start()
+        return copy
+
+    def finish(self):
+        for copy in self.open_sends:
+            copy.wait_send()
+
+
+class SlabGather:
+    def __init__(self, wire, at):
+        self.wire, self.at = wire, at
+        self.slots = wire.recv_slots(8)
+
+    def start(self, src):
+        place = self.wire.place
+        for mask in (5, 4, 1, 2):
+            self.wire.send(src, self.at(place.t), self.slots[mask], (place.r, place.peer(mask)))
+
+    def forward(self):
+        place = self.wire.place
+        for mask in (4, 1, 5):
+            block = self.at(place.peer(mask))
+            self.wire.arrived(block, self.slots[mask])
+            self.wire.send(block, block, self.slots[mask ^ 2], (place.r, place.peer(2)))
+
+    def wait(self):
+        place = self.wire.place
+        for mask in (2, 6, 3, 7):
+            self.wire.arrived(self.at(place.peer(mask)), self.slots[mask])
+
+
+class SlabScatter:
+    def __init__(self, wire, part, core_in, chip_in, block):
+        self.wire, self.part, self.core_in, self.chip_in, self.block = wire, part, core_in, chip_in, block
+        self.core_slots = wire.recv_slots(4)
+        self.chip_slots = wire.recv_slots(3)
+        self.order = (5, 4, 1, 0)
+
+    def cores(self):
+        place = self.wire.place
+        for i, mask in enumerate(self.order):
+            self.wire.send(
+                rows(self.part, place.peer(mask ^ 2), self.block),
+                self.core_in.at[i],
+                self.core_slots[i],
+                (place.r, place.peer(2)),
+            )
+
+    def chips(self):
+        place = self.wire.place
+        for i, mask in enumerate(self.order[:3]):
+            self.wire.arrived(self.core_in.at[i], self.core_slots[i])
+            mine = rows(self.part, place.peer(mask), self.block)
+            mine[...] = (mine[...].astype(F32) + self.core_in[i].astype(F32)).astype(BF16)
+            self.wire.send(mine, self.chip_in.at[i], self.chip_slots[i], (place.r, place.peer(mask)))
+        self.wire.arrived(self.core_in.at[3], self.core_slots[3])
+
+    def wait(self):
+        for i in range(3):
+            self.wire.arrived(self.chip_in.at[i], self.chip_slots[i])
+
+    def total(self, first, size):
+        mine = self.part[pl.ds(pl.multiple_of(self.wire.place.t * self.block + first, size), size), :].astype(F32)
+        mine = mine + self.core_in[3, pl.ds(first, size), :].astype(F32)
+        for i in range(3):
+            mine = mine + self.chip_in[i, pl.ds(first, size), :].astype(F32)
+        return mine
+
+
+class SlabSwap:
+    def __init__(self, wire, source, target):
+        self.wire, self.source, self.target = wire, source, target
+        self.slots = wire.recv_slots(8)
+
+    def start(self):
+        place = self.wire.place
+        self.own = self.wire.local(self.source(place.t), self.target(place.t))
+        for i in (4, 5, 3, 6, 2, 7, 1):
+            to = (place.t + i) % SLAB
+            self.wire.send(self.source(to), self.target(place.t), self.slots[i], (place.r, to))
+
+    def wait(self):
+        place = self.wire.place
+        for i in range(1, SLAB):
+            self.wire.arrived(self.target((place.t + SLAB - i) % SLAB), self.slots[i])
+        self.own.wait()
+
+
+class GroupGather:
+    def __init__(self, wire, at):
+        self.wire, self.at = wire, at
+        self.slots = wire.recv_slots(wire.place.groups)
+
+    def start(self, src):
+        place = self.wire.place
+        for i in range(1, place.groups):
+            self.wire.send(src, self.at(place.r), self.slots[i], ((place.r + i) % place.groups, place.t))
+
+    def wait(self):
+        place = self.wire.place
+        for i in range(1, place.groups):
+            self.wire.arrived(self.at((place.r + place.groups - i) % place.groups), self.slots[i])
+
+
+class GroupScatter:
+    def __init__(self, wire, out, into, own):
+        self.wire, self.out, self.into, self.own = wire, out, into, own
+        self.slots = wire.recv_slots(wire.place.groups)
+
+    def start(self, make):
+        place = self.wire.place
+        for i in range(1, place.groups):
+            to = (place.r + i) % place.groups
+            self.out[i - 1] = make(to).astype(BF16)
+            self.wire.send(self.out.at[i - 1], self.into.at[i - 1], self.slots[i], (to, place.t))
+        self.own[...] = make(place.r)
+
+    def total(self):
+        total = self.own[...]
+        for i in range(1, self.wire.place.groups):
+            self.wire.arrived(self.into.at[i - 1], self.slots[i])
+            total = total + self.into[i - 1].astype(F32)
+        return total
+
+
+def layer_kernel(
+    groups,
+    scale,
+    tokens,
+    upstream,
+    pack,
+    w_in,
+    w_out,
+    w_exp,
+    w_shr,
+    layer_out,
+    tokens_grad,
+    in_grad,
+    out_grad,
+    exp_grad,
+    shr_grad,
+    vec_grad,
+    packs,
+    tok_all,
+    first_all,
+    win,
+    wex,
+    wsh,
+    wo,
+    gls,
+    gls_all,
+    vecs,
+    ebias,
+    qkv,
+    gqkv,
+    soft_all,
+    blend_t,
+    blend,
+    middle,
+    normed,
+    inverses,
+    second,
+    second_all,
+    active,
+    ghid,
+    part_a,
+    part_b,
+    part_c,
+    part_d,
+    core_a,
+    core_b,
+    core_c,
+    core_d,
+    chip_a,
+    chip_b,
+    chip_c,
+    chip_d,
+    gsec,
+    glow,
+    gblend,
+    gblend_t,
+    sh_out,
+    sh_in,
+    sh_own,
+    ex_out,
+    ex_in,
+    ex_own,
+    ex_sum,
+    ex_all,
+    in_out,
+    in_in,
+    in_own,
+    in_sum,
+    in_all,
+    ou_out,
+    ou_in,
+    ou_own,
+    gvec,
+    gvec_exp,
+    gvec_out,
+    gvec_in,
+    send_sems,
+    recv_sems,
+    local_sems,
+):
+    place = Place(groups)
+    wire = Wire(place, send_sems, recv_sems, local_sems)
+    f, y, r, xc, t = place.f, place.y, place.r, place.xc, place.t
+    devices = groups * SLAB
+    me = r * SLAB + t
+    seg, width = tokens.shape
+    clips = SLAB // 2
+    slots = seg * 2
+    total_rows = SLAB * seg
+    head2 = qkv.shape[1] // 3
+    own_rows = w_in.shape[0]
+    slab_rows = own_rows * 4
+    share = width // devices
+    chunk = wsh.shape[1]
+
+    barrier = pltpu.get_barrier_semaphore()
+    for i in range(1, devices):
+        to = (me + i) % devices
+        pl.semaphore_signal(barrier, inc=1, device_id=place.device(to // SLAB, to % SLAB), device_id_type=MESH)
+    pl.semaphore_wait(barrier, devices - 1)
+
+    pack_slots = wire.recv_slots(groups * 4)
+    for i in range(1, groups * 4):
+        to = (f + i) % (groups * 4)
+        wire.send(pack, packs.at[f], pack_slots[i], (to // 4, (to % 4) * 2 + y))
+    own_pack = wire.local(pack, packs.at[f])
+
+    in_slots = wire.recv_slots(12)
+    ex_slots = wire.recv_slots(4 * groups)
+
+    def in_piece(index, c):
+        return win.at[pl.ds(pl.multiple_of(index * own_rows, own_rows), own_rows), pl.ds(c * head2, head2)]
+
+    def ex_piece(index, c):
+        return wex.at[pl.ds(pl.multiple_of(index * own_rows, own_rows), own_rows), pl.ds(c * chunk, chunk)]
+
+    own_in = []
+    for i in (2, 3, 1, 0):
+        to = ((xc + i) % 4) * 2 + y
+        for c in range(3):
+            src = w_in.at[:, pl.ds(pl.multiple_of(c * width + to * head2, head2), head2)]
+            if i == 0:
+                own_in.append(wire.local(src, in_piece(f, c)))
+            else:
+                wire.send(src, in_piece(f, c), in_slots[i * 3 + c], (r, to))
+    gather_tok = SlabGather(wire, lambda at: rows(tok_all, at, seg))
+    gather_tok.start(tokens)
+    own_tok = wire.local(tokens, rows(tok_all, t, seg))
+
+    out_share = w_out.at[pl.ds(pl.multiple_of(y * share, share), share), :]
+    own_out = wire.local(out_share, wo.at[r, t])
+    group_wo = GroupGather(wire, lambda at: wo.at[at, t])
+    group_wo.start(out_share)
+
+    own_ex = []
+    for i in (2, 3, 1, 0):
+        to = ((xc + i) % 4) * 2 + y
+        for c in range(groups):
+            src = w_exp.at[:, pl.ds(pl.multiple_of((c * SLAB + to) * chunk, chunk), chunk)]
+            if i == 0:
+                own_ex.append(wire.local(src, ex_piece(f, c)))
+            else:
+                wire.send(src, ex_piece(f, c), ex_slots[i * groups + c], (r, to))
+
+    row_at = y * seg + lax.broadcasted_iota(jnp.int32, (seg, 1), 0)
+    row_valid = row_at.astype(F32) < pack[10:11, 0:1].astype(F32)
+    gls[...] = jnp.where(row_valid, upstream[...].astype(F32), 0.0).astype(BF16)
+
+    for i in range(1, 4):
+        frm = r * 4 + (xc + 4 - i) % 4
+        for c in range(3):
+            wire.arrived(in_piece(frm, c), in_slots[i * 3 + c])
+    for copy in own_in:
+        copy.wait()
+    group_in = GroupGather(wire, lambda at: rows(win, at, slab_rows))
+    group_in.start(rows(win, r, slab_rows))
+
+    gather_tok.forward()
+    own_tok.wait()
+
+    shr_share = w_shr.at[pl.ds(pl.multiple_of(y * chunk, chunk), chunk), :]
+    own_shr = wire.local(shr_share, wsh.at[r])
+    for i in range(1, 4):
+        frm = r * 4 + (xc + 4 - i) % 4
+        for c in range(groups):
+            wire.arrived(ex_piece(frm, c), ex_slots[i * groups + c])
+    for copy in own_ex:
+        copy.wait()
+    group_ex = GroupGather(wire, lambda at: rows(wex, at, slab_rows))
+    group_ex.start(rows(wex, r, slab_rows))
+    group_sh = GroupGather(wire, lambda at: wsh.at[at])
+    group_sh.start(shr_share)
+
+    own_pack.wait()
+    for i in range(1, groups * 4):
+        wire.arrived(packs.at[(f + groups * 4 - i) % (groups * 4)], pack_slots[i])
+    per_lane = 128 // own_rows
+    lane = lax.broadcasted_iota(jnp.int32, (1, 128), 1)
+    for j in range(width // 128):
+        piece = packs[j * per_lane].astype(F32)
+        for k in range(1, per_lane):
+            piece = jnp.where(lane >= k * own_rows, packs[j * per_lane + k].astype(F32), piece)
+        vecs[:, j * 128 : (j + 1) * 128] = piece
+    for c in range(groups):
+        both = packs[c * 4 + t // 2].astype(F32)
+        ebias[0:1, c * chunk : (c + 1) * chunk] = jnp.where(y == 0, both[8:9], both[9:10])
+
+    gather_tok.wait()
+    strip = 32
+
+    def first_norm(i, carry):
+        at = pl.ds(pl.multiple_of(i * strip, strip), strip)
+        n, _ = row_stats(tok_all[at, :].astype(F32))
+        first_all[at, :] = (n * vecs[0:1, :] + vecs[1:2, :]).astype(BF16)
+        return carry
+
+    lax.fori_loop(0, total_rows // strip, first_norm, 0)
+
+    own_out.wait()
+    group_wo.wait()
+    gather_wo = SlabGather(wire, lambda at: wo.at[:, at])
+    gather_wo.start(wo.at[:, t])
+
+    group_in.wait()
+    tile = 256
+    at_head = pl.ds(pl.multiple_of(t * head2, head2), head2)
+    bias = jnp.concatenate([vecs[2:3, at_head], jnp.zeros((1, head2), F32), vecs[3:4, at_head]], axis=1)
+
+    def project(i, carry):
+        at = pl.ds(pl.multiple_of(i * tile, tile), tile)
+        qkv[at, :] = (matmul(first_all[at, :], win[...]) + bias).astype(BF16)
+        return carry
+
+    lax.fori_loop(0, total_rows // tile, project, 0)
+
+    gather_wo.forward()
+
+    head_size = head2 // 2
+    low_half = lane < head_size
+    half_masks = [low_half.astype(F32).astype(BF16), (1.0 - low_half.astype(F32)).astype(BF16)]
+    key_at = lax.broadcasted_iota(jnp.int32, (1, slots), 1).astype(F32)
+
+    def attend(i, carry):
+        at = pl.ds(pl.multiple_of(i * slots, slots), slots)
+        q = qkv[at, 0:head2]
+        k = qkv[at, head2 : 2 * head2]
+        v = qkv[at, 2 * head2 : 3 * head2]
+        count = packs[r * 4 + i].astype(F32)[10:11, 0:1]
+        key_valid = key_at < count
+        halves = []
+        for h in range(2):
+            scores = matmul_bt(q * half_masks[h], k) * scale
+            scores = jnp.where(key_valid, scores, -1e30)
+            top = jnp.max(scores, axis=-1, keepdims=True)
+            log_total = top + jnp.log(jnp.sum(jnp.exp(scores - top), axis=-1, keepdims=True))
+            soft = jnp.exp(scores - log_total)
+            soft_all[i * 2 + h] = soft
+            halves.append(matmul(soft.astype(BF16), v))
+        blend_t[at, :] = jnp.where(low_half, halves[0], halves[1]).astype(BF16)
+        return carry
+
+    lax.fori_loop(0, clips, attend, 0)
+
+    swap_blend = SlabSwap(wire, lambda at: rows(blend_t, at, seg), lambda at: cols(blend, at, head2))
+    swap_blend.start()
+    gather_gls = SlabGather(wire, lambda at: rows(gls_all, at, seg))
+    own_gls = wire.local(gls, rows(gls_all, t, seg))
+
+    gather_wo.wait()
+    swap_blend.wait()
+    wide = 256
+    for j in range(width // wide):
+        at = slice(j * wide, (j + 1) * wide)
+        product = matmul(blend[...], wo[:, :, :, at].reshape(width, wide))
+        middle[:, at] = tokens[:, at].astype(F32) + (product + vecs[4:5, at])
+
+    def second_norm(i, carry):
+        at = pl.ds(pl.multiple_of(i * strip, strip), strip)
+        n, inverse = row_stats(middle[at, :])
+        normed[at, :] = n
+        inverses[at, :] = jnp.broadcast_to(inverse, (strip, 128))
+        second[at, :] = (n * vecs[5:6, :] + vecs[6:7, :]).astype(BF16)
+        return carry
+
+    lax.fori_loop(0, seg // strip, second_norm, 0)
+
+    gather_second = SlabGather(wire, lambda at: rows(second_all, at, seg))
+    gather_second.start(second)
+    own_second = wire.local(second, rows(second_all, t, seg))
+    gather_gls.start(gls)
+    gather_second.forward()
+    gather_gls.forward()
+    gather_second.wait()
+    own_second.wait()
+    gather_gls.wait()
+    own_gls.wait()
+    for copy in (own_shr,):
+        copy.wait()
+    group_ex.wait()
+    group_sh.wait()
+
+    hidden_units = groups * chunk
+
+    def feed(i, carry):
+        at = pl.ds(pl.multiple_of(i * tile, tile), tile)
+        hidden = matmul(second_all[at, :], wex[...]) + ebias[0:1, :]
+        grad_active = matmul_bt(gls_all[at, :], wsh[...].reshape(hidden_units, width))
+        cdf = 0.5 * (1.0 + lax.erf(hidden * 0.7071067811865476))
+        active[at, :] = (hidden * cdf).astype(BF16)
+        slope = cdf + hidden * (0.3989422804014327 * jnp.exp(-0.5 * hidden * hidden))
+        grad_hidden = (grad_active * slope).astype(BF16)
+        ghid[at, :] = grad_hidden
+        gvec_exp[...] += jnp.sum(grad_hidden.astype(F32), axis=0, keepdims=True)
+        part_a[at, :] = matmul_bt(grad_hidden, wex[...]).astype(BF16)
+        return carry
+
+    gvec_exp[...] = jnp.zeros_like(gvec_exp)
+    lax.fori_loop(0, total_rows // tile, feed, 0)
+
+    scatter_second = SlabScatter(wire, part_a, core_a, chip_a, seg)
+    scatter_second.cores()
+
+    def feed_out(i, carry):
+        at = pl.ds(pl.multiple_of(i * tile, tile), tile)
+        part_b[at, :] = matmul(active[at, :], wsh[...].reshape(hidden_units, width)).astype(BF16)
+        return carry
+
+    lax.fori_loop(0, total_rows // tile, feed_out, 0)
+    scatter_second.chips()
+
+    group_shr = GroupScatter(wire, sh_out, sh_in, sh_own)
+    group_shr.start(
+        lambda c: matmul_at(active[:, pl.ds(pl.multiple_of(c * chunk, chunk), chunk)], gls_all[...])
+    )
+    scatter_second.wait()
+
+    gvec[...] = jnp.zeros_like(gvec)
+
+    def second_back(i, carry):
+        first = i * strip
+        at = pl.ds(pl.multiple_of(first, strip), strip)
+        grad = scatter_second.total(first, strip)
+        n = normed[at, :]
+        back = row_norm_back(grad, n, inverses[at, 0:1], vecs[5:6, :])
+        grad_result = gls[at, :].astype(F32)
+        grad_middle = grad_result + back
+        gsec[at, :] = grad_middle
+        low = grad_middle.astype(BF16)
+        glow[at, :] = low
+        gvec[4:5, :] += jnp.sum(low.astype(F32), axis=0, keepdims=True)
+        gvec[5:6, :] += jnp.sum(grad * n, axis=0, keepdims=True)
+        gvec[6:7, :] += jnp.sum(grad, axis=0, keepdims=True)
+        gvec[7:8, :] += jnp.sum(grad_result, axis=0, keepdims=True)
+        return carry
+
+    lax.fori_loop(0, seg // strip, second_back, 0)
+
+    for j in range(width // wide):
+        rows_of = slice(j * (groups * wide // width), (j + 1) * (groups * wide // width))
+        gblend[:, j * wide : (j + 1) * wide] = matmul_bt(
+            glow[...], wo[rows_of].reshape(wide, width)
+        ).astype(BF16)
+    swap_gblend = SlabSwap(wire, lambda at: cols(gblend, at, head2), lambda at: rows(gblend_t, at, seg))
+    swap_gblend.start()
+
+    scatter_result = SlabScatter(wire, part_b, core_b, chip_b, seg)
+    scatter_result.cores()
+    group_exp = GroupScatter(wire, ex_out, ex_in, ex_own)
+    group_exp.start(
+        lambda c: matmul_at(second_all[:, pl.ds(pl.multiple_of(c * slab_rows, slab_rows), slab_rows)], ghid[...])
+    )
+    scatter_result.chips()
+
+    swap_gblend.wait()
+
+    def attend_back(i, carry):
+        at = pl.ds(pl.multiple_of(i * slots, slots), slots)
+        q = qkv[at, 0:head2]
+        k = qkv[at, head2 : 2 * head2]
+        v = qkv[at, 2 * head2 : 3 * head2]
+        grad = gblend_t[at, :]
+        parts = []
+        for h in range(2):
+            soft = soft_all[i * 2 + h]
+            grad_soft = matmul_bt(grad * half_masks[h], v)
+            inner = jnp.sum(grad_soft * soft, axis=-1, keepdims=True)
+            grad_scores = (soft * (grad_soft - inner)).astype(BF16)
+            parts.append(
+                (
+                    matmul(grad_scores, k) * scale,
+                    matmul_at(grad_scores, q) * scale,
+                    matmul_at(soft.astype(BF16), grad),
+                )
+            )
+        for c in range(3):
+            gqkv[at, c * head2 : (c + 1) * head2] = jnp.where(low_half, parts[0][c], parts[1][c]).astype(BF16)
+        return carry
+
+    lax.fori_loop(0, clips, attend_back, 0)
+
+    def project_back(i, carry):
+        at = pl.ds(pl.multiple_of(i * tile, tile), tile)
+        part_c[at, :] = matmul_bt(gqkv[at, :], win[...]).astype(BF16)
+        return carry
+
+    lax.fori_loop(0, total_rows // tile, project_back, 0)
+    scatter_first = SlabScatter(wire, part_c, core_c, chip_c, seg)
+    scatter_first.cores()
+
+    group_inw = GroupScatter(wire, in_out, in_in, in_own)
+    group_inw.start(
+        lambda c: matmul_at(first_all[:, pl.ds(pl.multiple_of(c * slab_rows, slab_rows), slab_rows)], gqkv[...])
+    )
+    scatter_first.chips()
+    gvec[2:3, at_head] = jnp.sum(gqkv[:, 0:head2].astype(F32), axis=0, keepdims=True)
+    gvec[3:4, at_head] = jnp.sum(gqkv[:, 2 * head2 :].astype(F32), axis=0, keepdims=True)
+
+    for c in range(groups):
+        product = matmul_at(blend[:, c * slab_rows : (c + 1) * slab_rows], glow[...])
+        for to in range(SLAB):
+            part_d[to * seg + c * share : to * seg + (c + 1) * share, :] = product[
+                to * share : (to + 1) * share
+            ].astype(BF16)
+    scatter_out = SlabScatter(wire, part_d, core_d, chip_d, seg)
+    scatter_out.cores()
+
+    scatter_result.wait()
+
+    def finish_out(i, carry):
+        first = i * strip
+        at = pl.ds(pl.multiple_of(first, strip), strip)
+        result = middle[at, :] + (scatter_result.total(first, strip) + vecs[7:8, :])
+        spot = y * seg + first + lax.broadcasted_iota(jnp.int32, (strip, 1), 0)
+        valid = spot.astype(F32) < pack[10:11, 0:1].astype(F32)
+        layer_out[at, :] = jnp.where(valid, result, 0.0).astype(BF16)
+        return carry
+
+    lax.fori_loop(0, seg // strip, finish_out, 0)
+    shr_grad[...] = group_shr.total()
+    ex_sum[...] = group_exp.total().astype(BF16)
+    swap_exp = SlabSwap(wire, lambda at: rows(ex_sum, at, share), lambda at: ex_all.at[at])
+    swap_exp.start()
+
+    scatter_out.chips()
+    scatter_first.wait()
+
+    def first_back(i, carry):
+        first = i * strip
+        at = pl.ds(pl.multiple_of(first, strip), strip)
+        grad = scatter_first.total(first, strip)
+        n, inverse = row_stats(tokens[at, :].astype(F32))
+        tokens_grad[at, :] = gsec[at, :] + row_norm_back(grad, n, inverse, vecs[0:1, :])
+        gvec[0:1, :] += jnp.sum(grad * n, axis=0, keepdims=True)
+        gvec[1:2, :] += jnp.sum(grad, axis=0, keepdims=True)
+        return carry
+
+    lax.fori_loop(0, seg // strip, first_back, 0)
+
+    per_chunk = 128 // share
+    for j in range(width // 128):
+        gvec_out[j, 0:8, :] = gvec[:, j * 128 : (j + 1) * 128]
+        c = j * per_chunk // SLAB
+        gvec_out[j, 8:16, :] = jnp.broadcast_to(gvec_exp[0:1, c * chunk : (c + 1) * chunk], (8, chunk))
+    vec_slots = wire.recv_slots(devices)
+    for i in range(1, devices):
+        to = (me + i) % devices
+        wire.send(gvec_out.at[to // per_chunk], gvec_in.at[me], vec_slots[i], (to // SLAB, to % SLAB))
+    own_vec = wire.local(gvec_out.at[me // per_chunk], gvec_in.at[me])
+
+    in_sum[...] = group_inw.total().astype(BF16)
+    swap_in = SlabSwap(wire, lambda at: rows(in_sum, at, share), lambda at: in_all.at[at])
+    swap_in.start()
+
+    scatter_out.wait()
+    group_out = GroupScatter(wire, ou_out, ou_in, ou_own)
+    group_out.start(lambda c: scatter_out.total(c * share, share))
+
+    swap_exp.wait()
+    for frm in range(SLAB):
+        for c in range(groups):
+            place_at = (c * SLAB + frm) * chunk
+            exp_grad[:, place_at : place_at + chunk] = ex_all[frm, :, c * chunk : (c + 1) * chunk].astype(F32)
+    swap_in.wait()
+    for frm in range(SLAB):
+        for c in range(3):
+            place_at = c * width + frm * head2
+            in_grad[:, place_at : place_at + head2] = in_all[frm, :, c * head2 : (c + 1) * head2].astype(F32)
+    own_vec.wait()
+    for i in range(1, devices):
+        wire.arrived(gvec_in.at[(me + devices - i) % devices], vec_slots[i])
+    summed = gvec_in[0]
+    for i in range(1, devices):
+        summed = summed + gvec_in[i]
+    for_exp = gvec_in[t]
+    for c in range(1, groups):
+        for_exp = for_exp + gvec_in[c * SLAB + t]
+    vec_grad[0:8, :] = pltpu.roll(summed[0:8], (128 - share * (me % per_chunk)) % 128, 1)
+    vec_grad[8:16, :] = for_exp[8:16]
+    out_grad[...] = group_out.total()
+    wire.finish()
+
+
+def fused_shards(
+    tokens,
+    visible,
+    first_gain,
+    first_shift,
+    inward_weight,
+    query_bias,
+    value_bias,
+    outward_weight,
+    outward_bias,
+    second_gain,
+    second_shift,
+    expand_weight,
+    expand_bias,
+    shrink_weight,
+    shrink_bias,
+    upstream,
+):
+    seg, width = tokens.shape[1:]
+    groups = lax.axis_size("fsdp") // 4
+    devices = groups * SLAB
+    own_rows = inward_weight.shape[0]
+    hidden = expand_weight.shape[1]
+    share = width // devices
+    chunk = hidden // devices
+    units = groups * chunk
+    head2 = width // SLAB
+    scale = (width // HEADS) ** (-0.5)
+    total_rows = SLAB * seg
+    slab_rows = 4 * own_rows
+    vectors = jnp.stack(
+        [first_gain, first_shift, query_bias, value_bias, outward_bias, second_gain, second_shift, shrink_bias]
+    )
+    pack = jnp.concatenate(
+        [
+            jnp.concatenate([vectors] * (128 // own_rows), axis=1),
+            expand_bias.reshape(2, 128),
+            jnp.broadcast_to(visible.astype(BF16)[:, None], (6, 128)),
+        ]
+    )
+    vmem = pl.BlockSpec(memory_space=pltpu.VMEM)
+    anywhere = pl.BlockSpec(memory_space=pl.ANY)
+    outs = pl.pallas_call(
+        functools.partial(layer_kernel, groups, scale),
+        out_shape=(
+            jax.ShapeDtypeStruct((seg, width), BF16),
+            jax.ShapeDtypeStruct((seg, width), F32),
+            jax.ShapeDtypeStruct((share, 3 * width), F32),
+            jax.ShapeDtypeStruct((share, width), F32),
+            jax.ShapeDtypeStruct((share, hidden), F32),
+            jax.ShapeDtypeStruct((chunk, width), F32),
+            jax.ShapeDtypeStruct((16, 128), F32),
+        ),
+        in_specs=[vmem, vmem, vmem, anywhere, anywhere, anywhere, anywhere],
+        out_specs=[vmem] * 7,
+        scratch_shapes=[
+            pltpu.VMEM((groups * 4, 16, 128), BF16),
+            pltpu.VMEM((total_rows, width), BF16),
+            pltpu.VMEM((total_rows, width), BF16),
+            pltpu.VMEM((width, 3 * head2), BF16),
+            pltpu.VMEM((width, units), BF16),
+            pltpu.VMEM((groups, chunk, width), BF16),
+            pltpu.VMEM((groups, SLAB, share, width), BF16),
+            pltpu.VMEM((seg, width), BF16),
+            pltpu.VMEM((total_rows, width), BF16),
+            pltpu.VMEM((16, width), F32),
+            pltpu.VMEM((8, units), F32),
+            pltpu.VMEM((total_rows, 3 * head2), BF16),
+            pltpu.VMEM((total_rows, 3 * head2), BF16),
+            pltpu.VMEM((SLAB, 2 * seg, 2 * seg), F32),
+            pltpu.VMEM((total_rows, head2), BF16),
+            pltpu.VMEM((seg, width), BF16),
+            pltpu.VMEM((seg, width), F32),
+            pltpu.VMEM((seg, width), F32),
+            pltpu.VMEM((seg, 128), F32),
+            pltpu.VMEM((seg, width), BF16),
+            pltpu.VMEM((total_rows, width), BF16),
+            pltpu.VMEM((total_rows, units), BF16),
+            pltpu.VMEM((total_rows, units), BF16),
+        ]
+        + [pltpu.VMEM((total_rows, width), BF16)] * 4
+        + [pltpu.VMEM((4, seg, width), BF16)] * 4
+        + [pltpu.VMEM((3, seg, width), BF16)] * 4
+        + [
+            pltpu.VMEM((seg, width), F32),
+            pltpu.VMEM((seg, width), BF16),
+            pltpu.VMEM((seg, width), BF16),
+            pltpu.VMEM((total_rows, head2), BF16),
+            pltpu.VMEM((groups - 1, chunk, width), BF16),
+            pltpu.VMEM((groups - 1, chunk, width), BF16),
+            pltpu.VMEM((chunk, width), F32),
+            pltpu.VMEM((groups - 1, slab_rows, units), BF16),
+            pltpu.VMEM((groups - 1, slab_rows, units), BF16),
+            pltpu.VMEM((slab_rows, units), F32),
+            pltpu.VMEM((slab_rows, units), BF16),
+            pltpu.VMEM((SLAB, share, units), BF16),
+            pltpu.VMEM((groups - 1, slab_rows, 3 * head2), BF16),
+            pltpu.VMEM((groups - 1, slab_rows, 3 * head2), BF16),
+            pltpu.VMEM((slab_rows, 3 * head2), F32),
+            pltpu.VMEM((slab_rows, 3 * head2), BF16),
+            pltpu.VMEM((SLAB, share, 3 * head2), BF16),
+            pltpu.VMEM((groups - 1, share, width), BF16),
+            pltpu.VMEM((groups - 1, share, width), BF16),
+            pltpu.VMEM((share, width), F32),
+            pltpu.VMEM((8, width), F32),
+            pltpu.VMEM((1, units), F32),
+            pltpu.VMEM((width // 128, 16, 128), F32),
+            pltpu.VMEM((devices, 16, 128), F32),
+            pltpu.SemaphoreType.DMA((320,)),
+            pltpu.SemaphoreType.DMA((320,)),
+            pltpu.SemaphoreType.DMA((40,)),
+        ],
+        compiler_params=pltpu.CompilerParams(
+            collective_id=0, has_side_effects=True, vmem_limit_bytes=67043328
+        ),
+        name="layer",
+    )(
+        tokens.reshape(seg, width),
+        upstream.reshape(seg, width),
+        pack,
+        inward_weight,
+        outward_weight,
+        expand_weight,
+        shrink_weight,
+    )
+    layer_out, tokens_grad, in_grad, out_grad, exp_grad, shr_grad, vec = outs
+
+    def vector(k):
+        return vec[k, :share]
+
+    return (
+        layer_out.reshape(1, seg, width),
+        tokens_grad.reshape(1, seg, width),
+        vector(0),
+        vector(1),
+        in_grad,
+        vector(2),
+        vector(3),
+        out_grad,
+        vector(4),
+        vector(5),
+        vector(6),
+        exp_grad,
+        vec[8],
+        shr_grad,
+        vector(7),
+    )
+
+
+def fits_fused(mesh, tokens, inward_weight, expand_weight):
+    fsdp, seq = mesh.shape["fsdp"], mesh.shape["seq"]
+    clips, slots, width = tokens.shape
+    devices = fsdp * seq
+    return (
+        seq == 2
+        and clips == fsdp
+        and fsdp % 4 == 0
+        and width // HEADS * 2 == 128
+        and width == SLAB * 128
+        and slots % 64 == 0
+        and width % (16 * devices) == 0
+        and 128 % (width // fsdp) == 0
+        and expand_weight.shape[1] == 128 * devices
+    )
+
+
 def solution(mesh):
     in_specs = (
         P("fsdp", "seq", None),
@@ -391,4 +1268,9 @@
         P(("fsdp", "seq"), None),
         P(("fsdp", "seq")),
     )
-    return jax.shard_map(shards, mesh=mesh, in_specs=in_specs, out_specs=out_specs, check_vma=False)
+
+    def step(*args):
+        body = fused_shards if fits_fused(mesh, args[0], args[4], args[11]) else shards
+        return jax.shard_map(body, mesh=mesh, in_specs=in_specs, out_specs=out_specs, check_vma=False)(*args)
+
+    return step

time: 1360 us -> 198 us (0.15)
  waiting for transfers between devices: 1080 us -> 0 us
  Pallas kernels: 0 us -> 185 us
  blocking collectives: 141 us -> 0 us
  matrix products: 78.4 us -> 0 us
  local copies, waits for them, and re-layouts: 33.4 us -> 10.7 us
  between operations: 16.1 us -> 1.37 us
    reduce_scatter x4 -> x0, waiting for transfers between devices: 933 us -> none  [the longest x1 361 us: backward(): lax.psum_scatter(shrink_weight_grad, ('fsdp', 'seq'), scatter_dimension=0...]
    pallas_call x0 -> x1, Pallas kernels: none -> 185 us  [fused_shards(): pl.pallas_call(functools.partial(layer_kernel, groups, scale), out_shape=...]
    all_gather x4 -> x0, waiting for transfers between devices: 129 us -> none  [the longest x1 68.9 us: gather_weights(): lax.all_gather(shrink_weight, 'fsdp', axis=0, tiled=True)]
    unnamed x2 -> x0, blocking collectives: 106 us -> none
    dot_general x18 -> x0, matrix products: 78.4 us -> none  [the longest x1 10.9 us: backward(): jnp.einsum('csf,csd->fd', saved['active'], grad_low_second, preferred_ele...]
    all_gather x3 -> x0, blocking collectives: 35.2 us -> none  [the longest x1 17.1 us: gather_weights(): lax.all_gather(expand_bias, 'fsdp', axis=0, tiled=True)]
    unnamed x66 -> x34, local copies, waits for them, and re-layouts: 30.2 us -> 7.91 us
    unnamed x12 -> x0, waiting for transfers between devices: 20.6 us -> none
  transfers between devices with their start and end apart: 10 -> 0, of which waited for: 8 -> 0; matrix products, arithmetic and copies ran while one was open for 6% -> 0% of each run, Pallas kernels for 0% -> 0%
where the time goes in v1:
time: 198 us
  Pallas kernels  185 us (93%)
  local copies, waits for them, and re-layouts  10.7 us (5%)
    pallas_call x1, Pallas kernels, fused_shards(): pl.pallas_call(functools.partial(layer_kernel, groups, scale), out_shape=...  185 us
    unnamed x34, local copies, waits for them, and re-layouts  7.91 us

profile of v1, /device:TPU:0, one launch (start us, length us, event | category | flops | bytes accessed | tf_op | source)
XLA Modules:
  0.0 197.8 jit_solution(11199010758248710743)
XLA Ops:
  1.3 0.1 pad.3.clone
  1.4 0.0 copy-start.13
  1.4 0.0 copy-start.9
  1.4 0.0 copy-start.10
  1.4 0.0 copy-start.11
  1.4 0.0 copy-start.12
  1.4 0.0 copy-start.6
  1.4 0.0 copy-start.7
  1.4 0.0 copy-start.8
  1.4 0.6 copy-done.13
  2.0 0.0 copy-done.9
  2.1 0.0 copy-done.10
  2.1 0.0 copy-done.11
  2.1 0.0 copy-done.12
  2.1 0.0 copy-done.6
  2.1 0.0 copy-done.7
  2.1 0.0 copy-done.8
  2.2 0.0 copy-start.5
  2.2 0.7 copy-done.5
  2.8 0.7 maximum_maximum_fusion.pack
  3.5 185.0 %layer.1 = (bf16[128,1024]{1,0:T(8,128)(2,1)}, f32[128,1024]{1,0:T(8,128)}, f32[32,3072]{1,0:T(8,128)}, f32[32,1024]{1,0:T(8,128)}, f32[32,4096]{1,0:T(8,128)}, /*index=5*/f32[128,1024]{1,0:T(8,128)}, f32[16,128]{1,0:T(8,128)}) custom-call(bf16[128,1024]{1,0:T(8,128)(2,1)} %bitcast.34, bf16[128,1024]{1,0:T(8,128)(2,1)} %bitcast.35, ...), custom_call_target="tpu_custom_call" | custom-call | tf_op jit(solution)/shard_map/layer/pallas_call | solution.py:1111
  188.5 0.0 copy-start.2
  188.5 1.5 slice_bitcast_fusion
  190.0 1.2 slice_bitcast_fusion.1
  191.2 1.7 copy.38
  192.9 0.0 copy-done.2
  192.9 0.0 copy-start.3
  192.9 0.8 copy.39
  193.7 0.4 copy-done.3
  194.1 0.0 copy-start.4
  194.1 0.0 copy-start.1
  194.1 0.7 copy.40
  194.8 0.2 copy-done.4
  195.1 0.7 copy.41
  195.7 0.0 copy-done.1
  195.7 0.0 copy-start
  195.8 0.8 copy.42
  196.5 0.4 copy-done
  197.0 0.8 copy.43
  (2 shorter events, 0.0 us)
Async XLA Ops:
  1.4 0.7 copy-start.13
  1.4 0.7 copy-start.9
  1.4 0.7 copy-start.10
  1.4 0.7 copy-start.11
  1.4 0.7 copy-start.12
  1.4 0.7 copy-start.6
  1.4 0.7 copy-start.7
  1.4 0.7 copy-start.8
  2.2 0.7 copy-start.5
  188.5 4.4 %copy-start.2 = (f32[128,1024]{1,0:T(8,128)S(1)}, f32[128,1024]{1,0:T(8,128)}, u32[]{:S(2)}) copy-start(f32[128,1024]{1,0:T(8,128)} %get-tuple-element.23) | copy-start | bytes 1572868
  192.9 1.2 copy-start.3
  194.1 1.0 copy-start.4
  194.1 1.7 copy-start.1
  195.7 1.2 copy-start

commit v2 on v1

--- a/solution.py
+++ b/solution.py
@@ -362,6 +362,7 @@
 F32 = jnp.float32
 BF16 = jnp.bfloat16
 MESH = pl.DeviceIdType.MESH
+SENDS, RECVS, LOCALS = 200, 138, 22
 SLAB = 8
 
 
@@ -426,35 +427,61 @@
         self.place = place
         self.send_sems, self.recv_sems, self.local_sems = send_sems, recv_sems, local_sems
         self.sends = self.recvs = self.locals = 0
-        self.open_sends = []
+        self.free, self.open_sends = [], []
 
     def recv_slots(self, count):
         first = self.recvs
         self.recvs += count
         return [self.recv_sems.at[first + i] for i in range(count)]
 
-    def send(self, src, dst, slot, to):
-        copy = pltpu.make_async_remote_copy(
-            src_ref=src,
-            dst_ref=dst,
-            send_sem=self.send_sems.at[self.sends],
-            recv_sem=slot,
-            device_id=self.place.device(*to),
-            device_id_type=MESH,
-        )
-        self.sends += 1
-        copy.start()
-        self.open_sends.append(copy)
-
-    def arrived(self, dst, slot):
-        pltpu.make_async_remote_copy(
-            src_ref=dst,
-            dst_ref=dst,
-            send_sem=self.send_sems.at[0],
-            recv_sem=slot,
-            device_id=self.place.device(self.place.r, self.place.peer(2)),
-            device_id_type=MESH,
-        ).wait_recv()
+    def send(self, src, dst, slot, to, when=None):
+        if not self.free:
+            self.free.append(self.sends)
+            self.sends += 1
+        spot = self.free.pop()
+        send_sem = self.send_sems.at[spot]
+
+        def make():
+            return pltpu.make_async_remote_copy(
+                src_ref=src,
+                dst_ref=dst,
+                send_sem=send_sem,
+                recv_sem=slot,
+                device_id=self.place.device(*to),
+                device_id_type=MESH,
+            )
+
+        if when is None:
+            make().start()
+        else:
+            pl.when(when)(lambda: make().start())
+        self.open_sends.append((make, when, spot))
+
+    def settle(self, count=None):
+        count = len(self.open_sends) if count is None else count
+        for make, when, spot in self.open_sends[:count]:
+            if when is None:
+                make().wait_send()
+            else:
+                pl.when(when)(lambda make=make: make().wait_send())
+            self.free.append(spot)
+        self.open_sends = self.open_sends[count:]
+
+    def arrived(self, dst, slot, when=None):
+        def wait():
+            pltpu.make_async_remote_copy(
+                src_ref=dst,
+                dst_ref=dst,
+                send_sem=self.send_sems.at[0],
+                recv_sem=slot,
+                device_id=self.place.device(self.place.r, self.place.peer(2)),
+                device_id_type=MESH,
+            ).wait_recv()
+
+        if when is None:
+            wait()
+        else:
+            pl.when(when)(wait)
 
     def local(self, src, dst):
         copy = pltpu.make_async_copy(src, dst, self.local_sems.at[self.locals])
@@ -462,39 +489,59 @@
         copy.start()
         return copy
 
-    def finish(self):
-        for copy in self.open_sends:
-            copy.wait_send()
-
 
 class SlabGather:
-    def __init__(self, wire, at):
-        self.wire, self.at = wire, at
-        self.slots = wire.recv_slots(8)
-
-    def start(self, src):
-        place = self.wire.place
-        for mask in (5, 4, 1, 2):
-            self.wire.send(src, self.at(place.t), self.slots[mask], (place.r, place.peer(mask)))
+    def __init__(self, wire, at, half):
+        self.wire, self.at, self.half = wire, at, half
+        self.slots = wire.recv_slots(11)
+
+    def start(self, whole, halves):
+        wire, place, slots = self.wire, self.wire.place, self.slots
+        t, r = place.t, place.r
+        wire.send(halves[0], self.half(t, 0), slots[0], (r, place.peer(4)))
+        wire.send(halves[1], self.half(t, 1), slots[3], (r, place.peer(1)))
+        wire.send(halves[1], self.half(t, 1), slots[1], (r, place.peer(4)))
+        wire.send(halves[0], self.half(t, 0), slots[2], (r, place.peer(1)))
+        wire.send(whole, self.at(t), slots[6], (r, place.peer(2)))
+
+    def relay(self):
+        wire, place, slots = self.wire, self.wire.place, self.slots
+        r, far, near = place.r, place.peer(4), place.peer(1)
+        wire.arrived(self.half(far, 0), slots[0])
+        wire.send(self.half(far, 0), self.half(far, 0), slots[4], (r, near))
+        wire.arrived(self.half(near, 1), slots[3])
+        wire.send(self.half(near, 1), self.half(near, 1), slots[5], (r, far))
+        wire.arrived(self.half(far, 1), slots[1])
+        wire.send(self.at(far), self.at(far), slots[7], (r, place.peer(2)))
+        wire.arrived(self.half(near, 0), slots[2])
+        wire.send(self.at(near), self.at(near), slots[8], (r, place.peer(2)))
 
     def forward(self):
-        place = self.wire.place
-        for mask in (4, 1, 5):
-            block = self.at(place.peer(mask))
-            self.wire.arrived(block, self.slots[mask])
-            self.wire.send(block, block, self.slots[mask ^ 2], (place.r, place.peer(2)))
+        wire, place, slots = self.wire, self.wire.place, self.slots
+        across = place.peer(5)
+        for h in range(2):
+            block = self.half(across, h)
+            wire.arrived(block, slots[4 + h])
+            wire.send(block, block, slots[9 + h], (place.r, place.peer(2)))
+
+    def wait_block(self, mask):
+        wire, place, slots = self.wire, self.wire.place, self.slots
+        if mask == 7:
+            for h in range(2):
+                wire.arrived(self.half(place.peer(7), h), slots[9 + h])
+        else:
+            wire.arrived(self.at(place.peer(mask)), slots[{2: 6, 6: 7, 3: 8}[mask]])
 
     def wait(self):
-        place = self.wire.place
         for mask in (2, 6, 3, 7):
-            self.wire.arrived(self.at(place.peer(mask)), self.slots[mask])
+            self.wait_block(mask)
 
 
 class SlabScatter:
     def __init__(self, wire, part, core_in, chip_in, block):
         self.wire, self.part, self.core_in, self.chip_in, self.block = wire, part, core_in, chip_in, block
         self.core_slots = wire.recv_slots(4)
-        self.chip_slots = wire.recv_slots(3)
+        self.slots = wire.recv_slots(6)
         self.order = (5, 4, 1, 0)
 
     def cores(self):
@@ -507,80 +554,154 @@
                 (place.r, place.peer(2)),
             )
 
+    def half(self, mask, h):
+        return rows(self.part, self.wire.place.peer(mask) * 2 + h, self.block // 2)
+
+    def add_core(self, i):
+        mask = self.order[i]
+        self.wire.arrived(self.core_in.at[i], self.core_slots[i])
+        mine = rows(self.part, self.wire.place.peer(mask), self.block)
+        mine[...] = (mine[...].astype(F32) + self.core_in[i].astype(F32)).astype(BF16)
+
     def chips(self):
-        place = self.wire.place
-        for i, mask in enumerate(self.order[:3]):
-            self.wire.arrived(self.core_in.at[i], self.core_slots[i])
-            mine = rows(self.part, place.peer(mask), self.block)
-            mine[...] = (mine[...].astype(F32) + self.core_in[i].astype(F32)).astype(BF16)
-            self.wire.send(mine, self.chip_in.at[i], self.chip_slots[i], (place.r, place.peer(mask)))
-        self.wire.arrived(self.core_in.at[3], self.core_slots[3])
+        wire, place = self.wire, self.wire.place
+        far, near = (place.r, place.peer(4)), (place.r, place.peer(1))
+        self.add_core(0)
+        wire.send(self.half(5, 0), self.chip_in.at[0], self.slots[0], far)
+        wire.send(self.half(5, 1), self.chip_in.at[1], self.slots[1], near)
+        self.add_core(1)
+        wire.send(self.half(4, 0), self.chip_in.at[2], self.slots[2], far)
+        self.add_core(2)
+        wire.send(self.half(1, 1), self.chip_in.at[3], self.slots[3], near)
+        wire.arrived(self.core_in.at[3], self.core_slots[3])
+
+    def relay(self):
+        wire, place = self.wire, self.wire.place
+        far, near = (place.r, place.peer(4)), (place.r, place.peer(1))
+        for i, (block, to) in enumerate(((self.half(1, 0), near), (self.half(4, 1), far))):
+            wire.arrived(self.chip_in.at[i], self.slots[i])
+            block[...] = (block[...].astype(F32) + self.chip_in[i].astype(F32)).astype(BF16)
+            wire.send(block, self.chip_in.at[4 + i], self.slots[4 + i], to)
 
     def wait(self):
-        for i in range(3):
-            self.wire.arrived(self.chip_in.at[i], self.chip_slots[i])
+        for i in range(2, 6):
+            self.wire.arrived(self.chip_in.at[i], self.slots[i])
 
     def total(self, first, size):
         mine = self.part[pl.ds(pl.multiple_of(self.wire.place.t * self.block + first, size), size), :].astype(F32)
-        mine = mine + self.core_in[3, pl.ds(first, size), :].astype(F32)
-        for i in range(3):
-            mine = mine + self.chip_in[i, pl.ds(first, size), :].astype(F32)
-        return mine
+        mine = mine + self.core_in[3, pl.ds(pl.multiple_of(first, size), size), :].astype(F32)
+        h = first // (self.block // 2)
+        at = pl.ds(pl.multiple_of(first % (self.block // 2), size), size)
+        return mine + self.chip_in[2 + h, at, :].astype(F32) + self.chip_in[4 + h, at, :].astype(F32)
 
 
 class SlabSwap:
-    def __init__(self, wire, source, target):
-        self.wire, self.source, self.target = wire, source, target
-        self.slots = wire.recv_slots(8)
+    def __init__(self, wire, source, target, seven):
+        self.wire, self.source, self.target, self.seven = wire, source, target, seven
+        (self.slot,) = wire.recv_slots(1)
 
     def start(self):
         place = self.wire.place
         self.own = self.wire.local(self.source(place.t), self.target(place.t))
         for i in (4, 5, 3, 6, 2, 7, 1):
             to = (place.t + i) % SLAB
-            self.wire.send(self.source(to), self.target(place.t), self.slots[i], (place.r, to))
+            self.wire.send(self.source(to), self.target(place.t), self.slot, (place.r, to))
 
     def wait(self):
-        place = self.wire.place
-        for i in range(1, SLAB):
-            self.wire.arrived(self.target((place.t + SLAB - i) % SLAB), self.slots[i])
+        self.wire.arrived(self.seven, self.slot)
         self.own.wait()
 
 
 class GroupGather:
     def __init__(self, wire, at):
         self.wire, self.at = wire, at
-        self.slots = wire.recv_slots(wire.place.groups)
+        self.slots = wire.recv_slots(4)
+        self.first = wire.recvs - 4
+        r = wire.place.r
+        self.inner, self.outer = (r + 1) // 2 == 1, (r + 1) // 2 != 1
 
     def start(self, src):
-        place = self.wire.place
-        for i in range(1, place.groups):
-            self.wire.send(src, self.at(place.r), self.slots[i], ((place.r + i) % place.groups, place.t))
+        wire, place = self.wire, self.wire.place
+        r = place.r
+        wire.send(src, self.at(r), self.slots[1], ((r + 1) % 4, place.t), r != 3)
+        wire.send(src, self.at(r), self.slots[3], ((r + 3) % 4, place.t), r != 0)
+
+    def pass_on(self):
+        wire, place = self.wire, self.wire.place
+        r = place.r
+        below, above = (r + 3) % 4, (r + 1) % 4
+        for block, slot, to in ((self.at(below), self.slots[1], above), (self.at(above), self.slots[3], below)):
+            wire.arrived(block, slot, self.inner)
+            wire.send(block, block, self.slots[2], (to, place.t), self.inner)
+
+    def pass_far(self):
+        wire, place = self.wire, self.wire.place
+        r = place.r
+        block = self.at((r + 2) % 4)
+        wire.arrived(block, self.slots[2], self.inner)
+        slot = wire.recv_sems.at[self.first + (2 * r + 3) % 4]
+        wire.send(block, block, slot, ((3 * r + 1) % 4, place.t), self.inner)
 
     def wait(self):
-        place = self.wire.place
-        for i in range(1, place.groups):
-            self.wire.arrived(self.at((place.r + place.groups - i) % place.groups), self.slots[i])
+        wire, r = self.wire, self.wire.place.r
+        for i in (1, 2, 3):
+            wire.arrived(self.at((r + 4 - i) % 4), self.slots[i], self.outer)
 
 
 class GroupScatter:
-    def __init__(self, wire, out, into, own):
-        self.wire, self.out, self.into, self.own = wire, out, into, own
-        self.slots = wire.recv_slots(wire.place.groups)
+    def __init__(self, wire, out, into, own, passing):
+        self.wire, self.out, self.into, self.own, self.passing = wire, out, into, own, passing
+        self.slots = wire.recv_slots(5)
+        self.first = wire.recvs - 5
+        r = wire.place.r
+
+        @pl.when(r == 0)
+        def _():
+            into[0] = jnp.zeros_like(into[0])
+
+        @pl.when(r == 3)
+        def _():
+            into[2] = jnp.zeros_like(into[2])
 
     def start(self, make):
-        place = self.wire.place
-        for i in range(1, place.groups):
-            to = (place.r + i) % place.groups
-            self.out[i - 1] = make(to).astype(BF16)
-            self.wire.send(self.out.at[i - 1], self.into.at[i - 1], self.slots[i], (to, place.t))
-        self.own[...] = make(place.r)
+        wire, place = self.wire, self.wire.place
+        r, t = place.r, place.t
+        inner = (r + 1) // 2 == 1
+        outer = (r + 1) // 2 != 1
+        low = 1 - r // 2
+        pair = r + 1 - 2 * (r % 2)
+        first, last = 1 + 2 * low, 3 - 2 * low
+        self.out[0] = make((r + first) % 4).astype(BF16)
+        wire.send(self.out.at[0], self.passing, self.slots[0], (pair, t), outer)
+        wire.send(self.out.at[0], self.into.at[first - 1], wire.recv_sems.at[self.first + first], (pair, t), inner)
+        self.out[1] = make((r + 2) % 4).astype(BF16)
+        wire.send(self.out.at[1], self.into.at[1], self.slots[2], ((r + 2) % 4, t), outer)
+        self.out[2] = make((r + last) % 4).astype(BF16)
+        wire.send(
+            self.out.at[2], self.into.at[last - 1], wire.recv_sems.at[self.first + last], ((r + last) % 4, t)
+        )
+        self.own[...] = make(r)
+
+    def relay(self):
+        wire, place = self.wire, self.wire.place
+        r = place.r
+        inner = (r + 1) // 2 == 1
+        wire.arrived(self.passing, self.slots[0], inner)
+
+        @pl.when(inner)
+        def _():
+            self.out[1] = (self.out[1].astype(F32) + self.passing[...].astype(F32)).astype(BF16)
+
+        wire.send(self.out.at[1], self.into.at[1], self.slots[2], ((r + 2) % 4, place.t), inner)
 
     def total(self):
+        wire, r = self.wire, self.wire.place.r
+        wire.arrived(self.into.at[1], self.slots[2])
+        wire.arrived(self.into.at[0], self.slots[1], r != 0)
+        wire.arrived(self.into.at[2], self.slots[3], r != 3)
         total = self.own[...]
-        for i in range(1, self.wire.place.groups):
-            self.wire.arrived(self.into.at[i - 1], self.slots[i])
-            total = total + self.into[i - 1].astype(F32)
+        for i in range(3):
+            total = total + self.into[i].astype(F32)
         return total
 
 
@@ -594,11 +715,16 @@
     w_out,
     w_exp,
     w_shr,
+    layer_hbm,
+    tokens_hbm,
+    in_hbm,
+    out_hbm,
+    exp_hbm,
+    shr_hbm,
+    vec_hbm,
     layer_out,
     tokens_grad,
-    in_grad,
     out_grad,
-    exp_grad,
     shr_grad,
     vec_grad,
     packs,
@@ -643,19 +769,23 @@
     sh_out,
     sh_in,
     sh_own,
+    sh_pass,
     ex_out,
     ex_in,
     ex_own,
+    ex_pass,
     ex_sum,
     ex_all,
     in_out,
     in_in,
     in_own,
+    in_pass,
     in_sum,
     in_all,
     ou_out,
     ou_in,
     ou_own,
+    ou_pass,
     gvec,
     gvec_exp,
     gvec_out,
@@ -678,6 +808,8 @@
     slab_rows = own_rows * 4
     share = width // devices
     chunk = wsh.shape[1]
+    strip = 32
+    tile = 256
 
     barrier = pltpu.get_barrier_semaphore()
     for i in range(1, devices):
@@ -685,14 +817,14 @@
         pl.semaphore_signal(barrier, inc=1, device_id=place.device(to // SLAB, to % SLAB), device_id_type=MESH)
     pl.semaphore_wait(barrier, devices - 1)
 
-    pack_slots = wire.recv_slots(groups * 4)
+    (pack_slot,) = wire.recv_slots(1)
     for i in range(1, groups * 4):
         to = (f + i) % (groups * 4)
-        wire.send(pack, packs.at[f], pack_slots[i], (to // 4, (to % 4) * 2 + y))
+        wire.send(pack, packs.at[f], pack_slot, (to // 4, (to % 4) * 2 + y))
     own_pack = wire.local(pack, packs.at[f])
 
-    in_slots = wire.recv_slots(12)
-    ex_slots = wire.recv_slots(4 * groups)
+    in_slots = wire.recv_slots(4)
+    ex_slots = wire.recv_slots(4)
 
     def in_piece(index, c):
         return win.at[pl.ds(pl.multiple_of(index * own_rows, own_rows), own_rows), pl.ds(c * head2, head2)]
@@ -708,15 +840,22 @@
             if i == 0:
                 own_in.append(wire.local(src, in_piece(f, c)))
             else:
-                wire.send(src, in_piece(f, c), in_slots[i * 3 + c], (r, to))
-    gather_tok = SlabGather(wire, lambda at: rows(tok_all, at, seg))
-    gather_tok.start(tokens)
-    own_tok = wire.local(tokens, rows(tok_all, t, seg))
+                wire.send(src, in_piece(f, c), in_slots[i], (r, to))
 
     out_share = w_out.at[pl.ds(pl.multiple_of(y * share, share), share), :]
     own_out = wire.local(out_share, wo.at[r, t])
     group_wo = GroupGather(wire, lambda at: wo.at[at, t])
     group_wo.start(out_share)
+    shr_share = w_shr.at[pl.ds(pl.multiple_of(y * chunk, chunk), chunk), :]
+    own_shr = wire.local(shr_share, wsh.at[r])
+    group_sh = GroupGather(wire, lambda at: wsh.at[at])
+    group_sh.start(shr_share)
+
+    def slab_gather(ref):
+        return SlabGather(wire, lambda at: rows(ref, at, seg), lambda at, h: rows(ref, at * 2 + h, seg // 2))
+
+    gather_tok = slab_gather(tok_all)
+    gather_tok.start(tokens, [rows(tokens, h, seg // 2) for h in range(2)])
 
     own_ex = []
     for i in (2, 3, 1, 0):
@@ -726,40 +865,32 @@
             if i == 0:
                 own_ex.append(wire.local(src, ex_piece(f, c)))
             else:
-                wire.send(src, ex_piece(f, c), ex_slots[i * groups + c], (r, to))
+                wire.send(src, ex_piece(f, c), ex_slots[i], (r, to))
 
     row_at = y * seg + lax.broadcasted_iota(jnp.int32, (seg, 1), 0)
     row_valid = row_at.astype(F32) < pack[10:11, 0:1].astype(F32)
     gls[...] = jnp.where(row_valid, upstream[...].astype(F32), 0.0).astype(BF16)
+    gls_all[pl.ds(pl.multiple_of(t * seg, seg), seg), :] = gls[...]
+    gvec[...] = jnp.zeros_like(gvec)
+    gvec_exp[...] = jnp.zeros_like(gvec_exp)
+    group_shr = GroupScatter(wire, sh_out, sh_in, sh_own, sh_pass)
+    group_exp = GroupScatter(wire, ex_out, ex_in, ex_own, ex_pass)
+    group_inw = GroupScatter(wire, in_out, in_in, in_own, in_pass)
+    group_out = GroupScatter(wire, ou_out, ou_in, ou_own, ou_pass)
 
     for i in range(1, 4):
         frm = r * 4 + (xc + 4 - i) % 4
-        for c in range(3):
-            wire.arrived(in_piece(frm, c), in_slots[i * 3 + c])
+        wire.arrived(rows(win, frm, own_rows), in_slots[i])
     for copy in own_in:
         copy.wait()
+    own_out.wait()
+    group_wo.pass_on()
     group_in = GroupGather(wire, lambda at: rows(win, at, slab_rows))
     group_in.start(rows(win, r, slab_rows))
-
-    gather_tok.forward()
-    own_tok.wait()
-
-    shr_share = w_shr.at[pl.ds(pl.multiple_of(y * chunk, chunk), chunk), :]
-    own_shr = wire.local(shr_share, wsh.at[r])
-    for i in range(1, 4):
-        frm = r * 4 + (xc + 4 - i) % 4
-        for c in range(groups):
-            wire.arrived(ex_piece(frm, c), ex_slots[i * groups + c])
-    for copy in own_ex:
-        copy.wait()
-    group_ex = GroupGather(wire, lambda at: rows(wex, at, slab_rows))
-    group_ex.start(rows(wex, r, slab_rows))
-    group_sh = GroupGather(wire, lambda at: wsh.at[at])
-    group_sh.start(shr_share)
+    group_wo.pass_far()
 
     own_pack.wait()
-    for i in range(1, groups * 4):
-        wire.arrived(packs.at[(f + groups * 4 - i) % (groups * 4)], pack_slots[i])
+    wire.arrived(packs.at[pl.ds(0, groups * 4 - 1)], pack_slot)
     per_lane = 128 // own_rows
     lane = lax.broadcasted_iota(jnp.int32, (1, 128), 1)
     for j in range(width // 128):
@@ -771,24 +902,52 @@
         both = packs[c * 4 + t // 2].astype(F32)
         ebias[0:1, c * chunk : (c + 1) * chunk] = jnp.where(y == 0, both[8:9], both[9:10])
 
-    gather_tok.wait()
-    strip = 32
-
-    def first_norm(i, carry):
-        at = pl.ds(pl.multiple_of(i * strip, strip), strip)
-        n, _ = row_stats(tok_all[at, :].astype(F32))
-        first_all[at, :] = (n * vecs[0:1, :] + vecs[1:2, :]).astype(BF16)
-        return carry
-
-    lax.fori_loop(0, total_rows // strip, first_norm, 0)
-
-    own_out.wait()
+    def first_norm(src, offset, block):
+        def strip_norm(i, carry):
+            at = pl.multiple_of(i * strip, strip)
+            n, _ = row_stats(src[pl.ds(offset + at, strip), :].astype(F32))
+            to = pl.multiple_of(block * seg + at, strip)
+            first_all[pl.ds(to, strip), :] = (n * vecs[0:1, :] + vecs[1:2, :]).astype(BF16)
+            return carry
+
+        lax.fori_loop(0, seg // strip, strip_norm, 0)
+
+    first_norm(tokens, 0, t)
+
+    def norm_block(mask):
+        block = place.peer(mask)
+        first_norm(tok_all, pl.multiple_of(block * seg, seg), block)
+
+    gather_tok.relay()
+    group_in.pass_on()
+    norm_block(4)
+    norm_block(1)
+
+    gather_tok.forward()
+
+    norm_block(5)
+    group_in.pass_far()
+    group_sh.pass_on()
+    for i in range(1, 4):
+        frm = r * 4 + (xc + 4 - i) % 4
+        wire.arrived(rows(wex, frm, own_rows), ex_slots[i])
+    for copy in own_ex:
+        copy.wait()
+    group_ex = GroupGather(wire, lambda at: rows(wex, at, slab_rows))
+    group_ex.start(rows(wex, r, slab_rows))
+
     group_wo.wait()
-    gather_wo = SlabGather(wire, lambda at: wo.at[:, at])
-    gather_wo.start(wo.at[:, t])
-
+    gather_wo = SlabGather(wire, lambda at: wo.at[:, at], lambda at, h: wo.at[pl.ds(h * (groups // 2), groups // 2), at])
+    gather_wo.start(wo.at[:, t], [wo.at[pl.ds(h * (groups // 2), groups // 2), t] for h in range(2)])
+    gather_gls = slab_gather(gls_all)
+    gather_gls.start(gls, [rows(gls, h, seg // 2) for h in range(2)])
+
+    for mask in (2, 6, 3, 7):
+        gather_tok.wait_block(mask)
+        norm_block(mask)
+
+    gather_wo.relay()
     group_in.wait()
-    tile = 256
     at_head = pl.ds(pl.multiple_of(t * head2, head2), head2)
     bias = jnp.concatenate([vecs[2:3, at_head], jnp.zeros((1, head2), F32), vecs[3:4, at_head]], axis=1)
 
@@ -827,43 +986,46 @@
 
     lax.fori_loop(0, clips, attend, 0)
 
-    swap_blend = SlabSwap(wire, lambda at: rows(blend_t, at, seg), lambda at: cols(blend, at, head2))
+    group_sh.pass_far()
+    swap_blend = SlabSwap(wire, lambda at: rows(blend_t, at, seg), lambda at: cols(blend, at, head2), blend.at[:, 0 : 7 * head2])
     swap_blend.start()
-    gather_gls = SlabGather(wire, lambda at: rows(gls_all, at, seg))
-    own_gls = wire.local(gls, rows(gls_all, t, seg))
-
+    gather_gls.relay()
     gather_wo.wait()
     swap_blend.wait()
+    group_ex.pass_on()
     wide = 256
     for j in range(width // wide):
         at = slice(j * wide, (j + 1) * wide)
         product = matmul(blend[...], wo[:, :, :, at].reshape(width, wide))
         middle[:, at] = tokens[:, at].astype(F32) + (product + vecs[4:5, at])
 
+    own_second_rows = pl.multiple_of(t * seg, seg)
+
     def second_norm(i, carry):
         at = pl.ds(pl.multiple_of(i * strip, strip), strip)
         n, inverse = row_stats(middle[at, :])
         normed[at, :] = n
         inverses[at, :] = jnp.broadcast_to(inverse, (strip, 128))
-        second[at, :] = (n * vecs[5:6, :] + vecs[6:7, :]).astype(BF16)
+        low = (n * vecs[5:6, :] + vecs[6:7, :]).astype(BF16)
+        second[at, :] = low
+        second_all[pl.ds(pl.multiple_of(own_second_rows + i * strip, strip), strip), :] = low
         return carry
 
     lax.fori_loop(0, seg // strip, second_norm, 0)
 
-    gather_second = SlabGather(wire, lambda at: rows(second_all, at, seg))
-    gather_second.start(second)
-    own_second = wire.local(second, rows(second_all, t, seg))
-    gather_gls.start(gls)
+    gather_second = slab_gather(second_all)
+    gather_second.start(second, [rows(second, h, seg // 2) for h in range(2)])
+    gather_gls.forward()
+    gather_second.relay()
+    group_ex.pass_far()
     gather_second.forward()
-    gather_gls.forward()
+    gather_gls.wait()
     gather_second.wait()
-    own_second.wait()
-    gather_gls.wait()
-    own_gls.wait()
-    for copy in (own_shr,):
-        copy.wait()
     group_ex.wait()
     group_sh.wait()
+    own_shr.wait()
+
+    front_sends = len(wire.open_sends)
 
     hidden_units = groups * chunk
 
@@ -880,11 +1042,18 @@
         part_a[at, :] = matmul_bt(grad_hidden, wex[...]).astype(BF16)
         return carry
 
-    gvec_exp[...] = jnp.zeros_like(gvec_exp)
     lax.fori_loop(0, total_rows // tile, feed, 0)
 
     scatter_second = SlabScatter(wire, part_a, core_a, chip_a, seg)
     scatter_second.cores()
+    group_shr.start(
+        lambda c: matmul_at(active[:, pl.ds(pl.multiple_of(c * chunk, chunk), chunk)], gls_all[...])
+    )
+    scatter_second.chips()
+    group_exp.start(
+        lambda c: matmul_at(second_all[:, pl.ds(pl.multiple_of(c * slab_rows, slab_rows), slab_rows)], ghid[...])
+    )
+    scatter_second.relay()
 
     def feed_out(i, carry):
         at = pl.ds(pl.multiple_of(i * tile, tile), tile)
@@ -892,15 +1061,13 @@
         return carry
 
     lax.fori_loop(0, total_rows // tile, feed_out, 0)
-    scatter_second.chips()
-
-    group_shr = GroupScatter(wire, sh_out, sh_in, sh_own)
-    group_shr.start(
-        lambda c: matmul_at(active[:, pl.ds(pl.multiple_of(c * chunk, chunk), chunk)], gls_all[...])
-    )
+    scatter_result = SlabScatter(wire, part_b, core_b, chip_b, seg)
+    scatter_result.cores()
+
     scatter_second.wait()
-
-    gvec[...] = jnp.zeros_like(gvec)
+    wire.settle(front_sends)
+
+    feed_sends = len(wire.open_sends)
 
     def second_back(i, carry):
         first = i * strip
@@ -926,16 +1093,19 @@
         gblend[:, j * wide : (j + 1) * wide] = matmul_bt(
             glow[...], wo[rows_of].reshape(wide, width)
         ).astype(BF16)
-    swap_gblend = SlabSwap(wire, lambda at: cols(gblend, at, head2), lambda at: rows(gblend_t, at, seg))
+    swap_gblend = SlabSwap(wire, lambda at: cols(gblend, at, head2), lambda at: rows(gblend_t, at, seg), gblend_t.at[pl.ds(0, 7 * seg), :])
     swap_gblend.start()
-
-    scatter_result = SlabScatter(wire, part_b, core_b, chip_b, seg)
-    scatter_result.cores()
-    group_exp = GroupScatter(wire, ex_out, ex_in, ex_own)
-    group_exp.start(
-        lambda c: matmul_at(second_all[:, pl.ds(pl.multiple_of(c * slab_rows, slab_rows), slab_rows)], ghid[...])
-    )
     scatter_result.chips()
+    group_shr.relay()
+
+    for c in range(groups):
+        product = matmul_at(blend[:, c * slab_rows : (c + 1) * slab_rows], glow[...])
+        for to in range(SLAB):
+            part_d[to * seg + c * share : to * seg + (c + 1) * share, :] = product[
+                to * share : (to + 1) * share
+            ].astype(BF16)
+    scatter_out = SlabScatter(wire, part_d, core_d, chip_d, seg)
+    scatter_out.cores()
 
     swap_gblend.wait()
 
@@ -973,7 +1143,6 @@
     scatter_first = SlabScatter(wire, part_c, core_c, chip_c, seg)
     scatter_first.cores()
 
-    group_inw = GroupScatter(wire, in_out, in_in, in_own)
     group_inw.start(
         lambda c: matmul_at(first_all[:, pl.ds(pl.multiple_of(c * slab_rows, slab_rows), slab_rows)], gqkv[...])
     )
@@ -981,15 +1150,10 @@
     gvec[2:3, at_head] = jnp.sum(gqkv[:, 0:head2].astype(F32), axis=0, keepdims=True)
     gvec[3:4, at_head] = jnp.sum(gqkv[:, 2 * head2 :].astype(F32), axis=0, keepdims=True)
 
-    for c in range(groups):
-        product = matmul_at(blend[:, c * slab_rows : (c + 1) * slab_rows], glow[...])
-        for to in range(SLAB):
-            part_d[to * seg + c * share : to * seg + (c + 1) * share, :] = product[
-                to * share : (to + 1) * share
-            ].astype(BF16)
-    scatter_out = SlabScatter(wire, part_d, core_d, chip_d, seg)
-    scatter_out.cores()
-
+    scatter_result.relay()
+    group_exp.relay()
+    scatter_first.relay()
+    scatter_out.chips()
     scatter_result.wait()
 
     def finish_out(i, carry):
@@ -1002,13 +1166,10 @@
         return carry
 
     lax.fori_loop(0, seg // strip, finish_out, 0)
-    shr_grad[...] = group_shr.total()
-    ex_sum[...] = group_exp.total().astype(BF16)
-    swap_exp = SlabSwap(wire, lambda at: rows(ex_sum, at, share), lambda at: ex_all.at[at])
-    swap_exp.start()
-
-    scatter_out.chips()
+    stores = [wire.local(layer_out, layer_hbm)]
+
     scatter_first.wait()
+    wire.settle(feed_sends)
 
     def first_back(i, carry):
         first = i * strip
@@ -1021,39 +1182,31 @@
         return carry
 
     lax.fori_loop(0, seg // strip, first_back, 0)
+    stores.append(wire.local(tokens_grad, tokens_hbm))
 
     per_chunk = 128 // share
     for j in range(width // 128):
         gvec_out[j, 0:8, :] = gvec[:, j * 128 : (j + 1) * 128]
         c = j * per_chunk // SLAB
         gvec_out[j, 8:16, :] = jnp.broadcast_to(gvec_exp[0:1, c * chunk : (c + 1) * chunk], (8, chunk))
-    vec_slots = wire.recv_slots(devices)
+    (vec_slot,) = wire.recv_slots(1)
     for i in range(1, devices):
         to = (me + i) % devices
-        wire.send(gvec_out.at[to // per_chunk], gvec_in.at[me], vec_slots[i], (to // SLAB, to % SLAB))
+        wire.send(gvec_out.at[to // per_chunk], gvec_in.at[me], vec_slot, (to // SLAB, to % SLAB))
     own_vec = wire.local(gvec_out.at[me // per_chunk], gvec_in.at[me])
 
-    in_sum[...] = group_inw.total().astype(BF16)
-    swap_in = SlabSwap(wire, lambda at: rows(in_sum, at, share), lambda at: in_all.at[at])
-    swap_in.start()
-
+    scatter_out.relay()
     scatter_out.wait()
-    group_out = GroupScatter(wire, ou_out, ou_in, ou_own)
     group_out.start(lambda c: scatter_out.total(c * share, share))
-
-    swap_exp.wait()
-    for frm in range(SLAB):
-        for c in range(groups):
-            place_at = (c * SLAB + frm) * chunk
-            exp_grad[:, place_at : place_at + chunk] = ex_all[frm, :, c * chunk : (c + 1) * chunk].astype(F32)
-    swap_in.wait()
-    for frm in range(SLAB):
-        for c in range(3):
-            place_at = c * width + frm * head2
-            in_grad[:, place_at : place_at + head2] = in_all[frm, :, c * head2 : (c + 1) * head2].astype(F32)
+    shr_grad[...] = group_shr.total()
+    stores.append(wire.local(shr_grad, shr_hbm))
+    group_inw.relay()
+    group_out.relay()
+    ex_sum[...] = group_exp.total().astype(BF16)
+    swap_exp = SlabSwap(wire, lambda at: rows(ex_sum, at, share), lambda at: ex_all.at[at], ex_all.at[pl.ds(0, 7)])
+    swap_exp.start()
     own_vec.wait()
-    for i in range(1, devices):
-        wire.arrived(gvec_in.at[(me + devices - i) % devices], vec_slots[i])
+    wire.arrived(gvec_in.at[pl.ds(0, devices - 1)], vec_slot)
     summed = gvec_in[0]
     for i in range(1, devices):
         summed = summed + gvec_in[i]
@@ -1062,8 +1215,119 @@
         for_exp = for_exp + gvec_in[c * SLAB + t]
     vec_grad[0:8, :] = pltpu.roll(summed[0:8], (128 - share * (me % per_chunk)) % 128, 1)
     vec_grad[8:16, :] = for_exp[8:16]
+    stores.append(wire.local(vec_grad, vec_hbm))
+
+    in_sum[...] = group_inw.total().astype(BF16)
+    swap_in = SlabSwap(wire, lambda at: rows(in_sum, at, share), lambda at: in_all.at[at], in_all.at[pl.ds(0, 7)])
+    swap_in.start()
     out_grad[...] = group_out.total()
-    wire.finish()
+    stores.append(wire.local(out_grad, out_hbm))
+    swap_exp.wait()
+    stores.append(wire.local(ex_all, exp_hbm))
+    swap_in.wait()
+    stores.append(wire.local(in_all, in_hbm))
+    for copy in stores:
+        copy.wait()
+    wire.settle()
+    assert wire.sends <= SENDS and wire.recvs <= RECVS and wire.locals <= LOCALS
+
+
+def output_kernel(
+    groups,
+    layer_in,
+    tokens_in,
+    in_pieces,
+    out_in,
+    exp_pieces,
+    shr_in,
+    vec_in,
+    layer_out,
+    tokens_grad,
+    first_gain_grad,
+    first_shift_grad,
+    in_grad,
+    query_bias_grad,
+    value_bias_grad,
+    out_grad,
+    outward_bias_grad,
+    second_gain_grad,
+    second_shift_grad,
+    exp_grad,
+    expand_bias_grad,
+    shr_grad,
+    shrink_bias_grad,
+    layer_buf,
+    tokens_buf,
+    in_buf,
+    out_buf,
+    exp_buf,
+    shr_buf,
+    vec_buf,
+    in_wide,
+    exp_wide,
+    load_sems,
+    store_sems,
+):
+    share, width = out_buf.shape
+    head2, chunk = in_buf.shape[2] // 3, exp_buf.shape[2] // groups
+    loads = [
+        pltpu.make_async_copy(src, dst, load_sems.at[i])
+        for i, (src, dst) in enumerate(
+            (
+                (vec_in, vec_buf),
+                (exp_pieces, exp_buf),
+                (in_pieces, in_buf),
+                (shr_in, shr_buf),
+                (tokens_in, tokens_buf),
+                (layer_in, layer_buf),
+                (out_in, out_buf),
+            )
+        )
+    ]
+    for copy in loads:
+        copy.start()
+    stores = []
+
+    def store(src, dst):
+        stores.append(pltpu.make_async_copy(src, dst, store_sems.at[len(stores)]))
+        stores[-1].start()
+
+    loads[0].wait()
+    vectors = (
+        first_gain_grad,
+        first_shift_grad,
+        query_bias_grad,
+        value_bias_grad,
+        outward_bias_grad,
+        second_gain_grad,
+        second_shift_grad,
+        shrink_bias_grad,
+    )
+    for k, ref in enumerate(vectors):
+        ref[...] = vec_buf[k, 0:share]
+    expand_bias_grad[...] = vec_buf[8, :]
+    loads[1].wait()
+    for frm in range(SLAB):
+        for c in range(groups):
+            at = (c * SLAB + frm) * chunk
+            exp_wide[:, at : at + chunk] = exp_buf[frm, :, c * chunk : (c + 1) * chunk].astype(F32)
+    store(exp_wide, exp_grad)
+    loads[2].wait()
+    for frm in range(SLAB):
+        for c in range(3):
+            at = c * width + frm * head2
+            in_wide[:, at : at + head2] = in_buf[frm, :, c * head2 : (c + 1) * head2].astype(F32)
+    store(in_wide, in_grad)
+    for copy, src, dst in (
+        (loads[3], shr_buf, shr_grad),
+        (loads[4], tokens_buf, tokens_grad.at[0]),
+        (loads[5], layer_buf, layer_out.at[0]),
+        (loads[6], out_buf, out_grad),
+    ):
+        copy.wait()
+        store(src, dst)
+    for copy in stores:
+        copy.wait()
 
 
 def fused_shards(
@@ -1113,15 +1377,20 @@
         out_shape=(
             jax.ShapeDtypeStruct((seg, width), BF16),
             jax.ShapeDtypeStruct((seg, width), F32),
-            jax.ShapeDtypeStruct((share, 3 * width), F32),
+            jax.ShapeDtypeStruct((SLAB, share, 3 * head2), BF16),
             jax.ShapeDtypeStruct((share, width), F32),
-            jax.ShapeDtypeStruct((share, hidden), F32),
+            jax.ShapeDtypeStruct((SLAB, share, units), BF16),
             jax.ShapeDtypeStruct((chunk, width), F32),
             jax.ShapeDtypeStruct((16, 128), F32),
         ),
         in_specs=[vmem, vmem, vmem, anywhere, anywhere, anywhere, anywhere],
-        out_specs=[vmem] * 7,
+        out_specs=[anywhere] * 7,
         scratch_shapes=[
+            pltpu.VMEM((seg, width), BF16),
+            pltpu.VMEM((seg, width), F32),
+            pltpu.VMEM((share, width), F32),
+            pltpu.VMEM((chunk, width), F32),
+            pltpu.VMEM((16, 128), F32),
             pltpu.VMEM((groups * 4, 16, 128), BF16),
             pltpu.VMEM((total_rows, width), BF16),
             pltpu.VMEM((total_rows, width), BF16),
@@ -1148,7 +1417,7 @@
         ]
         + [pltpu.VMEM((total_rows, width), BF16)] * 4
         + [pltpu.VMEM((4, seg, width), BF16)] * 4
-        + [pltpu.VMEM((3, seg, width), BF16)] * 4
+        + [pltpu.VMEM((6, seg // 2, width), BF16)] * 4
         + [
             pltpu.VMEM((seg, width), F32),
             pltpu.VMEM((seg, width), BF16),
@@ -1157,26 +1426,30 @@
             pltpu.VMEM((groups - 1, chunk, width), BF16),
             pltpu.VMEM((groups - 1, chunk, width), BF16),
             pltpu.VMEM((chunk, width), F32),
+            pltpu.VMEM((chunk, width), BF16),
             pltpu.VMEM((groups - 1, slab_rows, units), BF16),
             pltpu.VMEM((groups - 1, slab_rows, units), BF16),
             pltpu.VMEM((slab_rows, units), F32),
+            pltpu.VMEM((slab_rows, units), BF16),
             pltpu.VMEM((slab_rows, units), BF16),
             pltpu.VMEM((SLAB, share, units), BF16),
             pltpu.VMEM((groups - 1, slab_rows, 3 * head2), BF16),
             pltpu.VMEM((groups - 1, slab_rows, 3 * head2), BF16),
             pltpu.VMEM((slab_rows, 3 * head2), F32),
             pltpu.VMEM((slab_rows, 3 * head2), BF16),
+            pltpu.VMEM((slab_rows, 3 * head2), BF16),
             pltpu.VMEM((SLAB, share, 3 * head2), BF16),
             pltpu.VMEM((groups - 1, share, width), BF16),
             pltpu.VMEM((groups - 1, share, width), BF16),
             pltpu.VMEM((share, width), F32),
+            pltpu.VMEM((share, width), BF16),
             pltpu.VMEM((8, width), F32),
             pltpu.VMEM((1, units), F32),
             pltpu.VMEM((width // 128, 16, 128), F32),
             pltpu.VMEM((devices, 16, 128), F32),
-            pltpu.SemaphoreType.DMA((320,)),
-            pltpu.SemaphoreType.DMA((320,)),
-            pltpu.SemaphoreType.DMA((40,)),
+            pltpu.SemaphoreType.DMA((SENDS,)),
+            pltpu.SemaphoreType.DMA((RECVS,)),
+            pltpu.SemaphoreType.DMA((LOCALS,)),
         ],
         compiler_params=pltpu.CompilerParams(
             collective_id=0, has_side_effects=True, vmem_limit_bytes=67043328
@@ -1191,28 +1464,43 @@
         expand_weight,
         shrink_weight,
     )
-    layer_out, tokens_grad, in_grad, out_grad, exp_grad, shr_grad, vec = outs
-
-    def vector(k):
-        return vec[k, :share]
-
-    return (
-        layer_out.reshape(1, seg, width),
-        tokens_grad.reshape(1, seg, width),
-        vector(0),
-        vector(1),
-        in_grad,
-        vector(2),
-        vector(3),
-        out_grad,
-        vector(4),
-        vector(5),
-        vector(6),
-        exp_grad,
-        vec[8],
-        shr_grad,
-        vector(7),
-    )
+    vector = jax.ShapeDtypeStruct((share,), F32)
+    return pl.pallas_call(
+        functools.partial(output_kernel, groups),
+        out_shape=(
+            jax.ShapeDtypeStruct((1, seg, width), BF16),
+            jax.ShapeDtypeStruct((1, seg, width), F32),
+            vector,
+            vector,
+            jax.ShapeDtypeStruct((share, 3 * width), F32),
+            vector,
+            vector,
+            jax.ShapeDtypeStruct((share, width), F32),
+            vector,
+            vector,
+            vector,
+            jax.ShapeDtypeStruct((share, hidden), F32),
+            jax.ShapeDtypeStruct((chunk,), F32),
+            jax.ShapeDtypeStruct((chunk, width), F32),
+            vector,
+        ),
+        in_specs=[anywhere] * 7,
+        out_specs=[vmem if k in (2, 3, 5, 6, 8, 9, 10, 12, 14) else anywhere for k in range(15)],
+        scratch_shapes=[
+            pltpu.VMEM((seg, width), BF16),
+            pltpu.VMEM((seg, width), F32),
+            pltpu.VMEM((SLAB, share, 3 * head2), BF16),
+            pltpu.VMEM((share, width), F32),
+            pltpu.VMEM((SLAB, share, units), BF16),
+            pltpu.VMEM((chunk, width), F32),
+            pltpu.VMEM((16, 128), F32),
+            pltpu.VMEM((share, 3 * width), F32),
+            pltpu.VMEM((share, hidden), F32),
+            pltpu.SemaphoreType.DMA((7,)),
+            pltpu.SemaphoreType.DMA((15,)),
+        ],
+        name="outputs",
+    )(*outs)
 
 
 def fits_fused(mesh, tokens, inward_weight, expand_weight):
@@ -1222,7 +1510,7 @@
     return (
         seq == 2
         and clips == fsdp
-        and fsdp % 4 == 0
+        and fsdp == 16
         and width // HEADS * 2 == 128
         and width == SLAB * 128
         and slots % 64 == 0

time: 198 us -> 145 us (0.73)
  Pallas kernels: 185 us -> 141 us
  local copies, waits for them, and re-layouts: 10.7 us -> 1.46 us
    pallas_call x1, Pallas kernels: 185 us -> 138 us  [fused_shards(): pl.pallas_call(functools.partial(layer_kernel, groups, scale), out_shape=...]
    unnamed x34 -> x18, local copies, waits for them, and re-layouts: 7.91 us -> 1.35 us
    pallas_call x0 -> x1, Pallas kernels: none -> 3.15 us  [fused_shards(): pl.pallas_call(functools.partial(output_kernel, groups), out_shape=(jax.S...]
    squeeze x2 -> x0, local copies, waits for them, and re-layouts: 2.7 us -> none  [the longest x1 1.51 us: vector(): return vec[k, :share]]
where the time goes in v2:
time: 145 us
  Pallas kernels  141 us (97%)
  between operations  1.52 us (1%)
  local copies, waits for them, and re-layouts  1.46 us (1%)
    pallas_call x1, Pallas kernels, fused_shards(): pl.pallas_call(functools.partial(layer_kernel, groups, scale), out_shape=...  138 us
    pallas_call x1, Pallas kernels, fused_shards(): pl.pallas_call(functools.partial(output_kernel, groups), out_shape=(jax.S...  3.15 us

profile of v2, /device:TPU:0, one launch (start us, length us, event | category | flops | bytes accessed | tf_op | source)
XLA Modules:
  0.0 145.1 jit_solution(9224229373274273250)
XLA Ops:
  1.3 0.1 pad.3.clone
  1.4 0.0 copy-start.8
  1.4 0.0 copy-start.4
  1.4 0.0 copy-start.5
  1.4 0.0 copy-start.6
  1.4 0.0 copy-start.7
  1.4 0.0 copy-start.1
  1.4 0.0 copy-start.2
  1.4 0.0 copy-start.3
  1.4 0.6 copy-done.8
  2.0 0.0 copy-done.4
  2.1 0.0 copy-done.5
  2.1 0.0 copy-done.6
  2.1 0.0 copy-done.7
  2.1 0.0 copy-done.1
  2.1 0.0 copy-done.2
  2.1 0.0 copy-done.3
  2.1 0.0 copy-start
  2.2 0.6 copy-done
  2.8 0.7 maximum_maximum_fusion.pack
  3.5 138.3 %layer.1 = (bf16[128,1024]{1,0:T(8,128)(2,1)}, f32[128,1024]{1,0:T(8,128)}, bf16[8,32,384]{2,1,0:T(8,128)(2,1)}, f32[32,1024]{1,0:T(8,128)}, bf16[8,32,512]{2,1,...) custom-call(bf16[128,1024]{1,0:T(8,128)(2,1)} %bitcast.12, bf16[128,1024]{1,0:T(8,128)(2,1)} %bitcast.13, ...), custom_call_target="tpu_custom_call" | custom-call | tf_op jit(solution)/shard_map/layer/pallas_call | solution.py:1375
  141.8 3.2 %outputs.1 = (bf16[1,128,1024]{2,1,0:T(8,128)(2,1)}, f32[1,128,1024]{2,1,0:T(8,128)}, f32[32]{0:T(128)}, f32[32]{0:T(128)}, f32[32,3072]{1,0:T(8,128)}, /*index=...) custom-call(bf16[128,1024]{1,0:T(8,128)(2,1)} %get-tuple-element.22., ...), custom_call_target="tpu_custom_call" | custom-call | tf_op jit(solution)/shard_map/outputs/pallas_call | solution.py:1468
  (2 shorter events, 0.0 us)
Async XLA Ops:
  1.4 0.7 copy-start.8
  1.4 0.7 copy-start.4
  1.4 0.7 copy-start.5
  1.4 0.7 copy-start.6
  1.4 0.7 copy-start.7
  1.4 0.7 copy-start.1
  1.4 0.7 copy-start.2
  1.4 0.7 copy-start.3
  2.1 0.7 copy-start

commit v3 on v2

--- a/solution.py
+++ b/solution.py
@@ -362,7 +362,7 @@
 F32 = jnp.float32
 BF16 = jnp.bfloat16
 MESH = pl.DeviceIdType.MESH
-SENDS, RECVS, LOCALS = 200, 138, 22
+SENDS, RECVS, LOCALS = 90, 134, 31
 SLAB = 8
 
 
@@ -434,49 +434,61 @@
         self.recvs += count
         return [self.recv_sems.at[first + i] for i in range(count)]
 
-    def send(self, src, dst, slot, to, when=None):
+    def batch(self, whole):
+        spot = self.take()
+        self.open_sends.append((lambda: self.describe(whole, whole, spot, self.recv_sems.at[0], self.near()), None, spot, False))
+        return spot
+
+    def near(self):
+        return (self.place.r, self.place.peer(2))
+
+    def take(self):
         if not self.free:
             self.free.append(self.sends)
             self.sends += 1
-        spot = self.free.pop()
-        send_sem = self.send_sems.at[spot]
+        return self.free.pop()
+
+    def describe(self, src, dst, spot, slot, to):
+        return pltpu.make_async_remote_copy(
+            src_ref=src,
+            dst_ref=dst,
+            send_sem=self.send_sems.at[spot],
+            recv_sem=slot,
+            device_id=self.place.device(*to),
+            device_id_type=MESH,
+        )
+
+    def send(self, src, dst, slot, to, when=None, batch=None):
+        spot = self.take() if batch is None else batch
 
         def make():
-            return pltpu.make_async_remote_copy(
-                src_ref=src,
-                dst_ref=dst,
-                send_sem=send_sem,
-                recv_sem=slot,
-                device_id=self.place.device(*to),
-                device_id_type=MESH,
-            )
+            return self.describe(src, dst, spot, slot, to)
 
         if when is None:
             make().start()
         else:
             pl.when(when)(lambda: make().start())
-        self.open_sends.append((make, when, spot))
-
-    def settle(self, count=None):
+        if batch is None:
+            self.open_sends.append((make, when, spot, to[0] is not self.place.r))
+
+    def settle(self, count=None, slab_only=False):
         count = len(self.open_sends) if count is None else count
-        for make, when, spot in self.open_sends[:count]:
+        kept = []
+        for item in self.open_sends[:count]:
+            make, when, spot, far = item
+            if slab_only and far:
+                kept.append(item)
+                continue
             if when is None:
                 make().wait_send()
             else:
                 pl.when(when)(lambda make=make: make().wait_send())
             self.free.append(spot)
-        self.open_sends = self.open_sends[count:]
+        self.open_sends = kept + self.open_sends[count:]
 
     def arrived(self, dst, slot, when=None):
         def wait():
-            pltpu.make_async_remote_copy(
-                src_ref=dst,
-                dst_ref=dst,
-                send_sem=self.send_sems.at[0],
-                recv_sem=slot,
-                device_id=self.place.device(self.place.r, self.place.peer(2)),
-                device_id_type=MESH,
-            ).wait_recv()
+            self.describe(dst, dst, 0, slot, self.near()).wait_recv()
 
         if when is None:
             wait()
@@ -603,9 +615,10 @@
     def start(self):
         place = self.wire.place
         self.own = self.wire.local(self.source(place.t), self.target(place.t))
+        batch = self.wire.batch(self.seven)
         for i in (4, 5, 3, 6, 2, 7, 1):
             to = (place.t + i) % SLAB
-            self.wire.send(self.source(to), self.target(place.t), self.slot, (place.r, to))
+            self.wire.send(self.source(to), self.target(place.t), self.slot, (place.r, to), batch=batch)
 
     def wait(self):
         self.wire.arrived(self.seven, self.slot)
@@ -710,7 +723,16 @@
     scale,
     tokens,
     upstream,
-    pack,
+    visible,
+    first_gain,
+    first_shift,
+    query_bias,
+    value_bias,
+    outward_bias,
+    second_gain,
+    second_shift,
+    shrink_bias,
+    expand_bias,
     w_in,
     w_out,
     w_exp,
@@ -727,6 +749,9 @@
     out_grad,
     shr_grad,
     vec_grad,
+    pack,
+    small,
+    wide_small,
     packs,
     tok_all,
     first_all,
@@ -750,6 +775,7 @@
     second_all,
     active,
     ghid,
+    slopes,
     part_a,
     part_b,
     part_c,
@@ -811,16 +837,36 @@
     strip = 32
     tile = 256
 
+    vectors = (
+        first_gain,
+        first_shift,
+        query_bias,
+        value_bias,
+        outward_bias,
+        second_gain,
+        second_shift,
+        shrink_bias,
+    )
+    loads = [wire.local(ref, small.at[k]) for k, ref in enumerate(vectors)]
+    loads.append(wire.local(expand_bias, wide_small))
     barrier = pltpu.get_barrier_semaphore()
     for i in range(1, devices):
         to = (me + i) % devices
         pl.semaphore_signal(barrier, inc=1, device_id=place.device(to // SLAB, to % SLAB), device_id_type=MESH)
+    for copy in loads:
+        copy.wait()
+    per_lane = 128 // own_rows
+    lines = [jnp.concatenate([small[k].astype(F32)] * per_lane, axis=1) for k in range(8)]
+    lines.append(wide_small[...].astype(F32))
+    count_here = jnp.full((6, 128), visible[0], jnp.int32).astype(F32)
+    pack[...] = jnp.concatenate(lines + [count_here], axis=0).astype(BF16)
     pl.semaphore_wait(barrier, devices - 1)
 
     (pack_slot,) = wire.recv_slots(1)
+    pack_batch = wire.batch(packs.at[pl.ds(0, groups * 4 - 1)])
     for i in range(1, groups * 4):
         to = (f + i) % (groups * 4)
-        wire.send(pack, packs.at[f], pack_slot, (to // 4, (to % 4) * 2 + y))
+        wire.send(pack, packs.at[f], pack_slot, (to // 4, (to % 4) * 2 + y), batch=pack_batch)
     own_pack = wire.local(pack, packs.at[f])
 
     in_slots = wire.recv_slots(4)
@@ -833,6 +879,7 @@
         return wex.at[pl.ds(pl.multiple_of(index * own_rows, own_rows), own_rows), pl.ds(c * chunk, chunk)]
 
     own_in = []
+    in_batch = wire.batch(win.at[pl.ds(0, 3 * own_rows), :])
     for i in (2, 3, 1, 0):
         to = ((xc + i) % 4) * 2 + y
         for c in range(3):
@@ -840,7 +887,7 @@
             if i == 0:
                 own_in.append(wire.local(src, in_piece(f, c)))
             else:
-                wire.send(src, in_piece(f, c), in_slots[i], (r, to))
+                wire.send(src, in_piece(f, c), in_slots[i], (r, to), batch=in_batch)
 
     out_share = w_out.at[pl.ds(pl.multiple_of(y * share, share), share), :]
     own_out = wire.local(out_share, wo.at[r, t])
@@ -849,7 +896,6 @@
     shr_share = w_shr.at[pl.ds(pl.multiple_of(y * chunk, chunk), chunk), :]
     own_shr = wire.local(shr_share, wsh.at[r])
     group_sh = GroupGather(wire, lambda at: wsh.at[at])
-    group_sh.start(shr_share)
 
     def slab_gather(ref):
         return SlabGather(wire, lambda at: rows(ref, at, seg), lambda at, h: rows(ref, at * 2 + h, seg // 2))
@@ -858,6 +904,7 @@
     gather_tok.start(tokens, [rows(tokens, h, seg // 2) for h in range(2)])
 
     own_ex = []
+    ex_batch = wire.batch(wex.at[pl.ds(0, 3 * own_rows), :])
     for i in (2, 3, 1, 0):
         to = ((xc + i) % 4) * 2 + y
         for c in range(groups):
@@ -865,7 +912,7 @@
             if i == 0:
                 own_ex.append(wire.local(src, ex_piece(f, c)))
             else:
-                wire.send(src, ex_piece(f, c), ex_slots[i], (r, to))
+                wire.send(src, ex_piece(f, c), ex_slots[i], (r, to), batch=ex_batch)
 
     row_at = y * seg + lax.broadcasted_iota(jnp.int32, (seg, 1), 0)
     row_valid = row_at.astype(F32) < pack[10:11, 0:1].astype(F32)
@@ -891,7 +938,6 @@
 
     own_pack.wait()
     wire.arrived(packs.at[pl.ds(0, groups * 4 - 1)], pack_slot)
-    per_lane = 128 // own_rows
     lane = lax.broadcasted_iota(jnp.int32, (1, 128), 1)
     for j in range(width // 128):
         piece = packs[j * per_lane].astype(F32)
@@ -927,7 +973,6 @@
 
     norm_block(5)
     group_in.pass_far()
-    group_sh.pass_on()
     for i in range(1, 4):
         frm = r * 4 + (xc + 4 - i) % 4
         wire.arrived(rows(wex, frm, own_rows), ex_slots[i])
@@ -935,18 +980,19 @@
         copy.wait()
     group_ex = GroupGather(wire, lambda at: rows(wex, at, slab_rows))
     group_ex.start(rows(wex, r, slab_rows))
+    group_sh.start(shr_share)
 
     group_wo.wait()
     gather_wo = SlabGather(wire, lambda at: wo.at[:, at], lambda at, h: wo.at[pl.ds(h * (groups // 2), groups // 2), at])
     gather_wo.start(wo.at[:, t], [wo.at[pl.ds(h * (groups // 2), groups // 2), t] for h in range(2)])
-    gather_gls = slab_gather(gls_all)
-    gather_gls.start(gls, [rows(gls, h, seg // 2) for h in range(2)])
 
     for mask in (2, 6, 3, 7):
         gather_tok.wait_block(mask)
         norm_block(mask)
 
     gather_wo.relay()
+    gather_gls = slab_gather(gls_all)
+    gather_gls.start(gls, [rows(gls, h, seg // 2) for h in range(2)])
     group_in.wait()
     at_head = pl.ds(pl.multiple_of(t * head2, head2), head2)
     bias = jnp.concatenate([vecs[2:3, at_head], jnp.zeros((1, head2), F32), vecs[3:4, at_head]], axis=1)
@@ -957,8 +1003,6 @@
         return carry
 
     lax.fori_loop(0, total_rows // tile, project, 0)
-
-    gather_wo.forward()
 
     head_size = head2 // 2
     low_half = lane < head_size
@@ -986,13 +1030,15 @@
 
     lax.fori_loop(0, clips, attend, 0)
 
-    group_sh.pass_far()
+    group_ex.pass_on()
     swap_blend = SlabSwap(wire, lambda at: rows(blend_t, at, seg), lambda at: cols(blend, at, head2), blend.at[:, 0 : 7 * head2])
     swap_blend.start()
+    gather_wo.forward()
+
     gather_gls.relay()
     gather_wo.wait()
     swap_blend.wait()
-    group_ex.pass_on()
+    group_ex.pass_far()
     wide = 256
     for j in range(width // wide):
         at = slice(j * wide, (j + 1) * wide)
@@ -1015,16 +1061,14 @@
 
     gather_second = slab_gather(second_all)
     gather_second.start(second, [rows(second, h, seg // 2) for h in range(2)])
+    group_sh.pass_on()
     gather_gls.forward()
     gather_second.relay()
-    group_ex.pass_far()
+    group_sh.pass_far()
     gather_second.forward()
     gather_gls.wait()
     gather_second.wait()
     group_ex.wait()
-    group_sh.wait()
-    own_shr.wait()
-
     front_sends = len(wire.open_sends)
 
     hidden_units = groups * chunk
@@ -1032,23 +1076,31 @@
     def feed(i, carry):
         at = pl.ds(pl.multiple_of(i * tile, tile), tile)
         hidden = matmul(second_all[at, :], wex[...]) + ebias[0:1, :]
-        grad_active = matmul_bt(gls_all[at, :], wsh[...].reshape(hidden_units, width))
         cdf = 0.5 * (1.0 + lax.erf(hidden * 0.7071067811865476))
         active[at, :] = (hidden * cdf).astype(BF16)
-        slope = cdf + hidden * (0.3989422804014327 * jnp.exp(-0.5 * hidden * hidden))
-        grad_hidden = (grad_active * slope).astype(BF16)
+        slopes[at, :] = cdf + hidden * (0.3989422804014327 * jnp.exp(-0.5 * hidden * hidden))
+        return carry
+
+    lax.fori_loop(0, total_rows // tile, feed, 0)
+    group_shr.start(
+        lambda c: matmul_at(active[:, pl.ds(pl.multiple_of(c * chunk, chunk), chunk)], gls_all[...])
+    )
+    group_sh.wait()
+    own_shr.wait()
+
+    def feed_back(i, carry):
+        at = pl.ds(pl.multiple_of(i * tile, tile), tile)
+        grad_active = matmul_bt(gls_all[at, :], wsh[...].reshape(hidden_units, width))
+        grad_hidden = (grad_active * slopes[at, :]).astype(BF16)
         ghid[at, :] = grad_hidden
         gvec_exp[...] += jnp.sum(grad_hidden.astype(F32), axis=0, keepdims=True)
         part_a[at, :] = matmul_bt(grad_hidden, wex[...]).astype(BF16)
         return carry
 
-    lax.fori_loop(0, total_rows // tile, feed, 0)
+    lax.fori_loop(0, total_rows // tile, feed_back, 0)
 
     scatter_second = SlabScatter(wire, part_a, core_a, chip_a, seg)
     scatter_second.cores()
-    group_shr.start(
-        lambda c: matmul_at(active[:, pl.ds(pl.multiple_of(c * chunk, chunk), chunk)], gls_all[...])
-    )
     scatter_second.chips()
     group_exp.start(
         lambda c: matmul_at(second_all[:, pl.ds(pl.multiple_of(c * slab_rows, slab_rows), slab_rows)], ghid[...])
@@ -1095,7 +1147,6 @@
         ).astype(BF16)
     swap_gblend = SlabSwap(wire, lambda at: cols(gblend, at, head2), lambda at: rows(gblend_t, at, seg), gblend_t.at[pl.ds(0, 7 * seg), :])
     swap_gblend.start()
-    scatter_result.chips()
     group_shr.relay()
 
     for c in range(groups):
@@ -1109,6 +1160,7 @@
 
     swap_gblend.wait()
 
+    scatter_out.chips()
     def attend_back(i, carry):
         at = pl.ds(pl.multiple_of(i * slots, slots), slots)
         q = qkv[at, 0:head2]
@@ -1134,6 +1186,7 @@
 
     lax.fori_loop(0, clips, attend_back, 0)
 
+    scatter_out.relay()
     def project_back(i, carry):
         at = pl.ds(pl.multiple_of(i * tile, tile), tile)
         part_c[at, :] = matmul_bt(gqkv[at, :], win[...]).astype(BF16)
@@ -1150,26 +1203,13 @@
     gvec[2:3, at_head] = jnp.sum(gqkv[:, 0:head2].astype(F32), axis=0, keepdims=True)
     gvec[3:4, at_head] = jnp.sum(gqkv[:, 2 * head2 :].astype(F32), axis=0, keepdims=True)
 
-    scatter_result.relay()
+    scatter_out.wait()
+    group_out.start(lambda c: scatter_out.total(c * share, share))
     group_exp.relay()
     scatter_first.relay()
-    scatter_out.chips()
-    scatter_result.wait()
-
-    def finish_out(i, carry):
-        first = i * strip
-        at = pl.ds(pl.multiple_of(first, strip), strip)
-        result = middle[at, :] + (scatter_result.total(first, strip) + vecs[7:8, :])
-        spot = y * seg + first + lax.broadcasted_iota(jnp.int32, (strip, 1), 0)
-        valid = spot.astype(F32) < pack[10:11, 0:1].astype(F32)
-        layer_out[at, :] = jnp.where(valid, result, 0.0).astype(BF16)
-        return carry
-
-    lax.fori_loop(0, seg // strip, finish_out, 0)
-    stores = [wire.local(layer_out, layer_hbm)]
-
+    scatter_result.chips()
     scatter_first.wait()
-    wire.settle(feed_sends)
+    wire.settle(feed_sends, slab_only=True)
 
     def first_back(i, carry):
         first = i * strip
@@ -1182,7 +1222,7 @@
         return carry
 
     lax.fori_loop(0, seg // strip, first_back, 0)
-    stores.append(wire.local(tokens_grad, tokens_hbm))
+    stores = [wire.local(tokens_grad, tokens_hbm)]
 
     per_chunk = 128 // share
     for j in range(width // 128):
@@ -1190,18 +1230,31 @@
         c = j * per_chunk // SLAB
         gvec_out[j, 8:16, :] = jnp.broadcast_to(gvec_exp[0:1, c * chunk : (c + 1) * chunk], (8, chunk))
     (vec_slot,) = wire.recv_slots(1)
+    vec_batch = wire.batch(gvec_in.at[pl.ds(0, devices - 1)])
     for i in range(1, devices):
         to = (me + i) % devices
-        wire.send(gvec_out.at[to // per_chunk], gvec_in.at[me], vec_slot, (to // SLAB, to % SLAB))
+        wire.send(gvec_out.at[to // per_chunk], gvec_in.at[me], vec_slot, (to // SLAB, to % SLAB), batch=vec_batch)
     own_vec = wire.local(gvec_out.at[me // per_chunk], gvec_in.at[me])
 
-    scatter_out.relay()
-    scatter_out.wait()
-    group_out.start(lambda c: scatter_out.total(c * share, share))
+    group_inw.relay()
+    scatter_result.relay()
+    group_out.relay()
+    scatter_result.wait()
+
+    def finish_out(i, carry):
+        first = i * strip
+        at = pl.ds(pl.multiple_of(first, strip), strip)
+        result = middle[at, :] + (scatter_result.total(first, strip) + vecs[7:8, :])
+        spot = y * seg + first + lax.broadcasted_iota(jnp.int32, (strip, 1), 0)
+        valid = spot.astype(F32) < pack[10:11, 0:1].astype(F32)
+        layer_out[at, :] = jnp.where(valid, result, 0.0).astype(BF16)
+        return carry
+
+    lax.fori_loop(0, seg // strip, finish_out, 0)
+    stores.append(wire.local(layer_out, layer_hbm))
+
     shr_grad[...] = group_shr.total()
     stores.append(wire.local(shr_grad, shr_hbm))
-    group_inw.relay()
-    group_out.relay()
     ex_sum[...] = group_exp.total().astype(BF16)
     swap_exp = SlabSwap(wire, lambda at: rows(ex_sum, at, share), lambda at: ex_all.at[at], ex_all.at[pl.ds(0, 7)])
     swap_exp.start()
@@ -1265,6 +1318,8 @@
     vec_buf,
     in_wide,
     exp_wide,
+    lines,
+    wide_line,
     load_sems,
     store_sems,
 ):
@@ -1304,8 +1359,10 @@
         shrink_bias_grad,
     )
     for k, ref in enumerate(vectors):
-        ref[...] = vec_buf[k, 0:share]
-    expand_bias_grad[...] = vec_buf[8, :]
+        lines[k] = vec_buf[k, 0:share]
+        store(lines.at[k], ref)
+    wide_line[...] = vec_buf[8, :]
+    store(wide_line, expand_bias_grad)
     loads[1].wait()
     for frm in range(SLAB):
         for c in range(groups):
@@ -1360,16 +1417,6 @@
     scale = (width // HEADS) ** (-0.5)
     total_rows = SLAB * seg
     slab_rows = 4 * own_rows
-    vectors = jnp.stack(
-        [first_gain, first_shift, query_bias, value_bias, outward_bias, second_gain, second_shift, shrink_bias]
-    )
-    pack = jnp.concatenate(
-        [
-            jnp.concatenate([vectors] * (128 // own_rows), axis=1),
-            expand_bias.reshape(2, 128),
-            jnp.broadcast_to(visible.astype(BF16)[:, None], (6, 128)),
-        ]
-    )
     vmem = pl.BlockSpec(memory_space=pltpu.VMEM)
     anywhere = pl.BlockSpec(memory_space=pl.ANY)
     outs = pl.pallas_call(
@@ -1383,7 +1430,7 @@
             jax.ShapeDtypeStruct((chunk, width), F32),
             jax.ShapeDtypeStruct((16, 128), F32),
         ),
-        in_specs=[vmem, vmem, vmem, anywhere, anywhere, anywhere, anywhere],
+        in_specs=[vmem, vmem, pl.BlockSpec(memory_space=pltpu.SMEM)] + [anywhere] * 13,
         out_specs=[anywhere] * 7,
         scratch_shapes=[
             pltpu.VMEM((seg, width), BF16),
@@ -1391,6 +1438,9 @@
             pltpu.VMEM((share, width), F32),
             pltpu.VMEM((chunk, width), F32),
             pltpu.VMEM((16, 128), F32),
+            pltpu.VMEM((16, 128), BF16),
+            pltpu.VMEM((8, 1, own_rows), BF16),
+            pltpu.VMEM((2, 128), BF16),
             pltpu.VMEM((groups * 4, 16, 128), BF16),
             pltpu.VMEM((total_rows, width), BF16),
             pltpu.VMEM((total_rows, width), BF16),
@@ -1414,6 +1464,7 @@
             pltpu.VMEM((total_rows, width), BF16),
             pltpu.VMEM((total_rows, units), BF16),
             pltpu.VMEM((total_rows, units), BF16),
+            pltpu.VMEM((total_rows, units), F32),
         ]
         + [pltpu.VMEM((total_rows, width), BF16)] * 4
         + [pltpu.VMEM((4, seg, width), BF16)] * 4
@@ -1458,7 +1509,21 @@
     )(
         tokens.reshape(seg, width),
         upstream.reshape(seg, width),
-        pack,
+        visible,
+        *(
+            vector.reshape(1, own_rows)
+            for vector in (
+                first_gain,
+                first_shift,
+                query_bias,
+                value_bias,
+                outward_bias,
+                second_gain,
+                second_shift,
+                shrink_bias,
+            )
+        ),
+        expand_bias.reshape(2, 128),
         inward_weight,
         outward_weight,
         expand_weight,
@@ -1485,7 +1550,7 @@
             vector,
         ),
         in_specs=[anywhere] * 7,
-        out_specs=[vmem if k in (2, 3, 5, 6, 8, 9, 10, 12, 14) else anywhere for k in range(15)],
+        out_specs=[anywhere] * 15,
         scratch_shapes=[
             pltpu.VMEM((seg, width), BF16),
             pltpu.VMEM((seg, width), F32),
@@ -1496,6 +1561,8 @@
             pltpu.VMEM((16, 128), F32),
             pltpu.VMEM((share, 3 * width), F32),
             pltpu.VMEM((share, hidden), F32),
+            pltpu.VMEM((8, share), F32),
+            pltpu.VMEM((chunk,), F32),
             pltpu.SemaphoreType.DMA((7,)),
             pltpu.SemaphoreType.DMA((15,)),
         ],

time: 145 us -> 132 us (0.910)
  Pallas kernels: 141 us -> 130 us
  local copies, waits for them, and re-layouts: 1.46 us -> 0 us
    pallas_call x1, Pallas kernels: 138 us -> 128 us  [fused_shards(): pl.pallas_call(functools.partial(layer_kernel, groups, scale), out_shape=...]
where the time goes in v3:
time: 132 us
  Pallas kernels  130 us (98%)
  between operations  1.47 us (1%)
    pallas_call x1, Pallas kernels, fused_shards(): pl.pallas_call(functools.partial(layer_kernel, groups, scale), out_shape=...  128 us

profile of v3, /device:TPU:0, one launch (start us, length us, event | category | flops | bytes accessed | tf_op | source)
XLA Modules:
  0.0 131.9 jit_solution(7276312704530866014)
XLA Ops:
  1.3 127.9 %layer.1 = (bf16[128,1024]{1,0:T(8,128)(2,1)}, f32[128,1024]{1,0:T(8,128)}, bf16[8,32,384]{2,1,0:T(8,128)(2,1)}, f32[32,1024]{1,0:T(8,128)}, bf16[8,32,512]{2,1,...) custom-call(bf16[128,1024]{1,0:T(8,128)(2,1)} %bitcast.11, bf16[128,1024]{1,0:T(8,128)(2,1)} %bitcast.12, ...), custom_call_target="tpu_custom_call" | custom-call | tf_op jit(solution)/shard_map/layer/pallas_call | solution.py:1422
  129.2 2.6 %outputs.1 = (bf16[1,128,1024]{2,1,0:T(8,128)(2,1)}, f32[1,128,1024]{2,1,0:T(8,128)}, f32[32]{0:T(128)}, f32[32]{0:T(128)}, f32[32,3072]{1,0:T(8,128)}, /*index=...) custom-call(bf16[128,1024]{1,0:T(8,128)(2,1)} %get-tuple-element.22., ...), custom_call_target="tpu_custom_call" | custom-call | tf_op jit(solution)/shard_map/outputs/pallas_call | solution.py:1533

commit v4 on v3

--- a/solution.py
+++ b/solution.py
@@ -362,7 +362,7 @@
 F32 = jnp.float32
 BF16 = jnp.bfloat16
 MESH = pl.DeviceIdType.MESH
-SENDS, RECVS, LOCALS = 90, 134, 31
+SENDS, RECVS, LOCALS = 93, 137, 31
 SLAB = 8
 
 
@@ -633,11 +633,12 @@
         r = wire.place.r
         self.inner, self.outer = (r + 1) // 2 == 1, (r + 1) // 2 != 1
 
-    def start(self, src):
+    def start(self, src, dst=None):
         wire, place = self.wire, self.wire.place
         r = place.r
-        wire.send(src, self.at(r), self.slots[1], ((r + 1) % 4, place.t), r != 3)
-        wire.send(src, self.at(r), self.slots[3], ((r + 3) % 4, place.t), r != 0)
+        dst = self.at(r) if dst is None else dst
+        wire.send(src, dst, self.slots[1], ((r + 1) % 4, place.t), r != 3)
+        wire.send(src, dst, self.slots[3], ((r + 3) % 4, place.t), r != 0)
 
     def pass_on(self):
         wire, place = self.wire, self.wire.place
@@ -816,6 +817,8 @@
     gvec_exp,
     gvec_out,
     gvec_in,
+    gvec_sum,
+    gvec_far,
     send_sems,
     recv_sems,
     local_sems,
@@ -897,6 +900,13 @@
     own_shr = wire.local(shr_share, wsh.at[r])
     group_sh = GroupGather(wire, lambda at: wsh.at[at])
 
+    def shr_half(h):
+        at = pl.ds(h * (chunk // 2), chunk // 2)
+        src = w_shr.at[pl.ds(pl.multiple_of(y * chunk + h * (chunk // 2), chunk // 2), chunk // 2), :]
+        group_sh.start(src, wsh.at[r, at])
+
+    shr_half(0)
+
     def slab_gather(ref):
         return SlabGather(wire, lambda at: rows(ref, at, seg), lambda at, h: rows(ref, at * 2 + h, seg // 2))
 
@@ -934,6 +944,7 @@
     group_wo.pass_on()
     group_in = GroupGather(wire, lambda at: rows(win, at, slab_rows))
     group_in.start(rows(win, r, slab_rows))
+    shr_half(1)
     group_wo.pass_far()
 
     own_pack.wait()
@@ -965,6 +976,9 @@
         first_norm(tok_all, pl.multiple_of(block * seg, seg), block)
 
     gather_tok.relay()
+    group_wo.wait()
+    gather_wo = SlabGather(wire, lambda at: wo.at[:, at], lambda at, h: wo.at[pl.ds(h * (groups // 2), groups // 2), at])
+    gather_wo.start(wo.at[:, t], [wo.at[pl.ds(h * (groups // 2), groups // 2), t] for h in range(2)])
     group_in.pass_on()
     norm_block(4)
     norm_block(1)
@@ -980,11 +994,7 @@
         copy.wait()
     group_ex = GroupGather(wire, lambda at: rows(wex, at, slab_rows))
     group_ex.start(rows(wex, r, slab_rows))
-    group_sh.start(shr_share)
-
-    group_wo.wait()
-    gather_wo = SlabGather(wire, lambda at: wo.at[:, at], lambda at, h: wo.at[pl.ds(h * (groups // 2), groups // 2), at])
-    gather_wo.start(wo.at[:, t], [wo.at[pl.ds(h * (groups // 2), groups // 2), t] for h in range(2)])
+
 
     for mask in (2, 6, 3, 7):
         gather_tok.wait_block(mask)
@@ -1097,15 +1107,18 @@
         part_a[at, :] = matmul_bt(grad_hidden, wex[...]).astype(BF16)
         return carry
 
-    lax.fori_loop(0, total_rows // tile, feed_back, 0)
-
+    core = xc % 2
     scatter_second = SlabScatter(wire, part_a, core_a, chip_a, seg)
+    lax.fori_loop(0, 2, lambda k, carry: feed_back(1 - core + 2 * k, carry), 0)
     scatter_second.cores()
+    lax.fori_loop(0, 2, lambda k, carry: feed_back(core + 2 * k, carry), 0)
+
     scatter_second.chips()
     group_exp.start(
         lambda c: matmul_at(second_all[:, pl.ds(pl.multiple_of(c * slab_rows, slab_rows), slab_rows)], ghid[...])
     )
     scatter_second.relay()
+    group_shr.relay()
 
     def feed_out(i, carry):
         at = pl.ds(pl.multiple_of(i * tile, tile), tile)
@@ -1147,7 +1160,6 @@
         ).astype(BF16)
     swap_gblend = SlabSwap(wire, lambda at: cols(gblend, at, head2), lambda at: rows(gblend_t, at, seg), gblend_t.at[pl.ds(0, 7 * seg), :])
     swap_gblend.start()
-    group_shr.relay()
 
     for c in range(groups):
         product = matmul_at(blend[:, c * slab_rows : (c + 1) * slab_rows], glow[...])
@@ -1158,9 +1170,9 @@
     scatter_out = SlabScatter(wire, part_d, core_d, chip_d, seg)
     scatter_out.cores()
 
+    scatter_out.chips()
     swap_gblend.wait()
 
-    scatter_out.chips()
     def attend_back(i, carry):
         at = pl.ds(pl.multiple_of(i * slots, slots), slots)
         q = qkv[at, 0:head2]
@@ -1187,14 +1199,16 @@
     lax.fori_loop(0, clips, attend_back, 0)
 
     scatter_out.relay()
+    group_exp.relay()
     def project_back(i, carry):
         at = pl.ds(pl.multiple_of(i * tile, tile), tile)
         part_c[at, :] = matmul_bt(gqkv[at, :], win[...]).astype(BF16)
         return carry
 
-    lax.fori_loop(0, total_rows // tile, project_back, 0)
     scatter_first = SlabScatter(wire, part_c, core_c, chip_c, seg)
+    lax.fori_loop(0, 2, lambda k, carry: project_back(1 - core + 2 * k, carry), 0)
     scatter_first.cores()
+    lax.fori_loop(0, 2, lambda k, carry: project_back(core + 2 * k, carry), 0)
 
     group_inw.start(
         lambda c: matmul_at(first_all[:, pl.ds(pl.multiple_of(c * slab_rows, slab_rows), slab_rows)], gqkv[...])
@@ -1205,12 +1219,12 @@
 
     scatter_out.wait()
     group_out.start(lambda c: scatter_out.total(c * share, share))
-    group_exp.relay()
     scatter_first.relay()
     scatter_result.chips()
     scatter_first.wait()
     wire.settle(feed_sends, slab_only=True)
 
+    group_inw.relay()
     def first_back(i, carry):
         first = i * strip
         at = pl.ds(pl.multiple_of(first, strip), strip)
@@ -1224,21 +1238,25 @@
     lax.fori_loop(0, seg // strip, first_back, 0)
     stores = [wire.local(tokens_grad, tokens_hbm)]
 
-    per_chunk = 128 // share
-    for j in range(width // 128):
-        gvec_out[j, 0:8, :] = gvec[:, j * 128 : (j + 1) * 128]
-        c = j * per_chunk // SLAB
-        gvec_out[j, 8:16, :] = jnp.broadcast_to(gvec_exp[0:1, c * chunk : (c + 1) * chunk], (8, chunk))
-    (vec_slot,) = wire.recv_slots(1)
-    vec_batch = wire.batch(gvec_in.at[pl.ds(0, devices - 1)])
-    for i in range(1, devices):
-        to = (me + i) % devices
-        wire.send(gvec_out.at[to // per_chunk], gvec_in.at[me], vec_slot, (to // SLAB, to % SLAB), batch=vec_batch)
-    own_vec = wire.local(gvec_out.at[me // per_chunk], gvec_in.at[me])
-
-    group_inw.relay()
+    for to in range(SLAB):
+        gvec_out[to] = jnp.concatenate(
+            [gvec[:, (c * SLAB + to) * share : (c * SLAB + to + 1) * share] for c in range(groups)], axis=1
+        )
+    swap_vec = SlabSwap(wire, lambda at: gvec_out.at[at], lambda at: gvec_in.at[at], gvec_in.at[pl.ds(0, 7)])
+    swap_vec.start()
+
     scatter_result.relay()
-    group_out.relay()
+    swap_vec.wait()
+    summed = gvec_in[0]
+    for i in range(1, SLAB):
+        summed = summed + gvec_in[i]
+    gvec_sum[0:8] = summed
+    for c in range(groups):
+        gvec_sum[8 + c : 9 + c] = gvec_exp[0:1, c * chunk : (c + 1) * chunk]
+    gvec_sum[8 + groups : 16] = jnp.zeros((8 - groups, 128), F32)
+    vec_slots = wire.recv_slots(groups - 1)
+    for i in range(1, groups):
+        wire.send(gvec_sum, gvec_far.at[i - 1], vec_slots[i - 1], ((r + i) % groups, t))
     scatter_result.wait()
 
     def finish_out(i, carry):
@@ -1253,28 +1271,28 @@
     lax.fori_loop(0, seg // strip, finish_out, 0)
     stores.append(wire.local(layer_out, layer_hbm))
 
-    shr_grad[...] = group_shr.total()
-    stores.append(wire.local(shr_grad, shr_hbm))
+    group_out.relay()
     ex_sum[...] = group_exp.total().astype(BF16)
     swap_exp = SlabSwap(wire, lambda at: rows(ex_sum, at, share), lambda at: ex_all.at[at], ex_all.at[pl.ds(0, 7)])
     swap_exp.start()
-    own_vec.wait()
-    wire.arrived(gvec_in.at[pl.ds(0, devices - 1)], vec_slot)
-    summed = gvec_in[0]
-    for i in range(1, devices):
-        summed = summed + gvec_in[i]
-    for_exp = gvec_in[t]
-    for c in range(1, groups):
-        for_exp = for_exp + gvec_in[c * SLAB + t]
-    vec_grad[0:8, :] = pltpu.roll(summed[0:8], (128 - share * (me % per_chunk)) % 128, 1)
-    vec_grad[8:16, :] = for_exp[8:16]
-    stores.append(wire.local(vec_grad, vec_hbm))
-
+    shr_grad[...] = group_shr.total()
+    stores.append(wire.local(shr_grad, shr_hbm))
     in_sum[...] = group_inw.total().astype(BF16)
     swap_in = SlabSwap(wire, lambda at: rows(in_sum, at, share), lambda at: in_all.at[at], in_all.at[pl.ds(0, 7)])
     swap_in.start()
     out_grad[...] = group_out.total()
     stores.append(wire.local(out_grad, out_hbm))
+    for i in range(1, groups):
+        wire.arrived(gvec_far.at[i - 1], vec_slots[i - 1])
+    total = gvec_sum[...]
+    for i in range(1, groups):
+        total = total + gvec_far[i - 1]
+    vec_grad[0:8, :] = pltpu.roll(total[0:8], (128 - share * r) % 128, 1)
+    line = total[8:9]
+    for c in range(1, groups):
+        line = jnp.where(r == c, total[8 + c : 9 + c], line)
+    vec_grad[8:16, :] = jnp.broadcast_to(line, (8, 128))
+    stores.append(wire.local(vec_grad, vec_hbm))
     swap_exp.wait()
     stores.append(wire.local(ex_all, exp_hbm))
     swap_in.wait()
@@ -1282,7 +1300,7 @@
     for copy in stores:
         copy.wait()
     wire.settle()
-    assert wire.sends <= SENDS and wire.recvs <= RECVS and wire.locals <= LOCALS
+    assert (wire.sends, wire.recvs, wire.locals) == (SENDS, RECVS, LOCALS), (wire.sends, wire.recvs, wire.locals)
 
 
 def output_kernel(
@@ -1496,8 +1514,10 @@
             pltpu.VMEM((share, width), BF16),
             pltpu.VMEM((8, width), F32),
             pltpu.VMEM((1, units), F32),
-            pltpu.VMEM((width // 128, 16, 128), F32),
-            pltpu.VMEM((devices, 16, 128), F32),
+            pltpu.VMEM((SLAB, 8, 128), F32),
+            pltpu.VMEM((SLAB, 8, 128), F32),
+            pltpu.VMEM((16, 128), F32),
+            pltpu.VMEM((groups - 1, 16, 128), F32),
             pltpu.SemaphoreType.DMA((SENDS,)),
             pltpu.SemaphoreType.DMA((RECVS,)),
             pltpu.SemaphoreType.DMA((LOCALS,)),
@@ -1583,6 +1603,7 @@
         and slots % 64 == 0
         and width % (16 * devices) == 0
         and 128 % (width // fsdp) == 0
+        and width // devices * 4 == 128
         and expand_weight.shape[1] == 128 * devices
     )
 

time: 132 us -> 126 us (0.955)
  Pallas kernels: 130 us -> 124 us
    pallas_call x1, Pallas kernels: 128 us -> 121 us  [fused_shards(): pl.pallas_call(functools.partial(layer_kernel, groups, scale), out_shape=...]
where the time goes in v4:
time: 126 us; the launch traced here: 125 us
  Pallas kernels  124 us (98%)
  between operations  1.47 us (1%)
    pallas_call x1, Pallas kernels, fused_shards(): pl.pallas_call(functools.partial(layer_kernel, groups, scale), out_shape=...  121 us
    pallas_call x1, Pallas kernels, fused_shards(): pl.pallas_call(functools.partial(output_kernel, groups), out_shape=(jax.S...  2.61 us

profile of v4, /device:TPU:0, one launch (start us, length us, event | category | flops | bytes accessed | tf_op | source)
XLA Modules:
  0.0 125.4 jit_solution(12131682660452946183)
XLA Ops:
  1.3 121.3 %layer.1 = (bf16[128,1024]{1,0:T(8,128)(2,1)}, f32[128,1024]{1,0:T(8,128)}, bf16[8,32,384]{2,1,0:T(8,128)(2,1)}, f32[32,1024]{1,0:T(8,128)}, bf16[8,32,512]{2,1,...) custom-call(bf16[128,1024]{1,0:T(8,128)(2,1)} %bitcast.11, bf16[128,1024]{1,0:T(8,128)(2,1)} %bitcast.12, ...), custom_call_target="tpu_custom_call" | custom-call | tf_op jit(solution)/shard_map/layer/pallas_call | solution.py:1440
  122.6 2.6 %outputs.1 = (bf16[1,128,1024]{2,1,0:T(8,128)(2,1)}, f32[1,128,1024]{2,1,0:T(8,128)}, f32[32]{0:T(128)}, f32[32]{0:T(128)}, f32[32,3072]{1,0:T(8,128)}, /*index=...) custom-call(bf16[128,1024]{1,0:T(8,128)(2,1)} %get-tuple-element.22., ...), custom_call_target="tpu_custom_call" | custom-call | tf_op jit(solution)/shard_map/outputs/pallas_call | solution.py:1553

commit v5 on v4

--- a/solution.py
+++ b/solution.py
@@ -677,7 +677,7 @@
         def _():
             into[2] = jnp.zeros_like(into[2])
 
-    def start(self, make):
+    def start(self, make, hold=None):
         wire, place = self.wire, self.wire.place
         r, t = place.r, place.t
         inner = (r + 1) // 2 == 1
@@ -691,10 +691,18 @@
         self.out[1] = make((r + 2) % 4).astype(BF16)
         wire.send(self.out.at[1], self.into.at[1], self.slots[2], ((r + 2) % 4, t), outer)
         self.out[2] = make((r + last) % 4).astype(BF16)
-        wire.send(
-            self.out.at[2], self.into.at[last - 1], wire.recv_sems.at[self.first + last], ((r + last) % 4, t)
-        )
+        self.last = last
+        if not hold:
+            self.start_last()
+        elif hold == "outer":
+            self.start_last(inner)
         self.own[...] = make(r)
+
+    def start_last(self, when=None):
+        wire, place = self.wire, self.wire.place
+        to = (place.r + self.last) % 4
+        slot = wire.recv_sems.at[self.first + self.last]
+        wire.send(self.out.at[2], self.into.at[self.last - 1], slot, (to, place.t), when)
 
     def relay(self):
         wire, place = self.wire, self.wire.place
@@ -1014,6 +1022,7 @@
 
     lax.fori_loop(0, total_rows // tile, project, 0)
 
+    group_sh.pass_on()
     head_size = head2 // 2
     low_half = lane < head_size
     half_masks = [low_half.astype(F32).astype(BF16), (1.0 - low_half.astype(F32)).astype(BF16)]
@@ -1031,8 +1040,8 @@
             scores = matmul_bt(q * half_masks[h], k) * scale
             scores = jnp.where(key_valid, scores, -1e30)
             top = jnp.max(scores, axis=-1, keepdims=True)
-            log_total = top + jnp.log(jnp.sum(jnp.exp(scores - top), axis=-1, keepdims=True))
-            soft = jnp.exp(scores - log_total)
+            soft = jnp.exp(scores - top)
+            soft = soft * (1.0 / jnp.sum(soft, axis=-1, keepdims=True))
             soft_all[i * 2 + h] = soft
             halves.append(matmul(soft.astype(BF16), v))
         blend_t[at, :] = jnp.where(low_half, halves[0], halves[1]).astype(BF16)
@@ -1071,16 +1080,7 @@
 
     gather_second = slab_gather(second_all)
     gather_second.start(second, [rows(second, h, seg // 2) for h in range(2)])
-    group_sh.pass_on()
     gather_gls.forward()
-    gather_second.relay()
-    group_sh.pass_far()
-    gather_second.forward()
-    gather_gls.wait()
-    gather_second.wait()
-    group_ex.wait()
-    front_sends = len(wire.open_sends)
-
     hidden_units = groups * chunk
 
     def feed(i, carry):
@@ -1091,9 +1091,27 @@
         slopes[at, :] = cdf + hidden * (0.3989422804014327 * jnp.exp(-0.5 * hidden * hidden))
         return carry
 
-    lax.fori_loop(0, total_rows // tile, feed, 0)
+    gather_second.relay()
+    group_sh.pass_far()
+    group_ex.wait()
+    core = xc % 2
+    beside = xc + 1 - 2 * core
+    across = (xc + 2) % 4
+    feed(xc, 0)
+    gather_second.forward()
+    feed(across, 0)
+    gather_second.wait_block(2)
+    gather_second.wait_block(3)
+    feed(beside, 0)
+    gather_second.wait_block(6)
+    gather_second.wait_block(7)
+    feed((beside + 2) % 4, 0)
+    gather_gls.wait()
+    front_sends = len(wire.open_sends)
+
     group_shr.start(
-        lambda c: matmul_at(active[:, pl.ds(pl.multiple_of(c * chunk, chunk), chunk)], gls_all[...])
+        lambda c: matmul_at(active[:, pl.ds(pl.multiple_of(c * chunk, chunk), chunk)], gls_all[...]),
+        hold="outer",
     )
     group_sh.wait()
     own_shr.wait()
@@ -1107,7 +1125,6 @@
         part_a[at, :] = matmul_bt(grad_hidden, wex[...]).astype(BF16)
         return carry
 
-    core = xc % 2
     scatter_second = SlabScatter(wire, part_a, core_a, chip_a, seg)
     lax.fori_loop(0, 2, lambda k, carry: feed_back(1 - core + 2 * k, carry), 0)
     scatter_second.cores()
@@ -1211,20 +1228,26 @@
     lax.fori_loop(0, 2, lambda k, carry: project_back(core + 2 * k, carry), 0)
 
     group_inw.start(
-        lambda c: matmul_at(first_all[:, pl.ds(pl.multiple_of(c * slab_rows, slab_rows), slab_rows)], gqkv[...])
+        lambda c: matmul_at(first_all[:, pl.ds(pl.multiple_of(c * slab_rows, slab_rows), slab_rows)], gqkv[...]),
+        hold="all",
     )
     scatter_first.chips()
     gvec[2:3, at_head] = jnp.sum(gqkv[:, 0:head2].astype(F32), axis=0, keepdims=True)
     gvec[3:4, at_head] = jnp.sum(gqkv[:, 2 * head2 :].astype(F32), axis=0, keepdims=True)
 
     scatter_out.wait()
-    group_out.start(lambda c: scatter_out.total(c * share, share))
+    group_out.start(lambda c: scatter_out.total(c * share, share), hold="outer")
+    outer = (r + 1) // 2 != 1
+    group_inw.start_last(outer)
+    group_out.start_last(outer)
+    group_shr.start_last(outer)
     scatter_first.relay()
     scatter_result.chips()
+    group_inw.relay()
+    group_inw.start_last((r + 1) // 2 == 1)
     scatter_first.wait()
     wire.settle(feed_sends, slab_only=True)
 
-    group_inw.relay()
     def first_back(i, carry):
         first = i * strip
         at = pl.ds(pl.multiple_of(first, strip), strip)
@@ -1238,6 +1261,7 @@
     lax.fori_loop(0, seg // strip, first_back, 0)
     stores = [wire.local(tokens_grad, tokens_hbm)]
 
+    group_out.relay()
     for to in range(SLAB):
         gvec_out[to] = jnp.concatenate(
             [gvec[:, (c * SLAB + to) * share : (c * SLAB + to + 1) * share] for c in range(groups)], axis=1
@@ -1246,6 +1270,9 @@
     swap_vec.start()
 
     scatter_result.relay()
+    ex_sum[...] = group_exp.total().astype(BF16)
+    swap_exp = SlabSwap(wire, lambda at: rows(ex_sum, at, share), lambda at: ex_all.at[at], ex_all.at[pl.ds(0, 7)])
+    swap_exp.start()
     swap_vec.wait()
     summed = gvec_in[0]
     for i in range(1, SLAB):
@@ -1257,6 +1284,9 @@
     vec_slots = wire.recv_slots(groups - 1)
     for i in range(1, groups):
         wire.send(gvec_sum, gvec_far.at[i - 1], vec_slots[i - 1], ((r + i) % groups, t))
+    in_sum[...] = group_inw.total().astype(BF16)
+    swap_in = SlabSwap(wire, lambda at: rows(in_sum, at, share), lambda at: in_all.at[at], in_all.at[pl.ds(0, 7)])
+    swap_in.start()
     scatter_result.wait()
 
     def finish_out(i, carry):
@@ -1271,17 +1301,10 @@
     lax.fori_loop(0, seg // strip, finish_out, 0)
     stores.append(wire.local(layer_out, layer_hbm))
 
-    group_out.relay()
-    ex_sum[...] = group_exp.total().astype(BF16)
-    swap_exp = SlabSwap(wire, lambda at: rows(ex_sum, at, share), lambda at: ex_all.at[at], ex_all.at[pl.ds(0, 7)])
-    swap_exp.start()
+    out_grad[...] = group_out.total()
+    stores.append(wire.local(out_grad, out_hbm))
     shr_grad[...] = group_shr.total()
     stores.append(wire.local(shr_grad, shr_hbm))
-    in_sum[...] = group_inw.total().astype(BF16)
-    swap_in = SlabSwap(wire, lambda at: rows(in_sum, at, share), lambda at: in_all.at[at], in_all.at[pl.ds(0, 7)])
-    swap_in.start()
-    out_grad[...] = group_out.total()
-    stores.append(wire.local(out_grad, out_hbm))
     for i in range(1, groups):
         wire.arrived(gvec_far.at[i - 1], vec_slots[i - 1])
     total = gvec_sum[...]

time: 126 us -> 122 us (0.968)
  Pallas kernels: 124 us -> 120 us
    pallas_call x1, Pallas kernels: 121 us -> 118 us  [fused_shards(): pl.pallas_call(functools.partial(layer_kernel, groups, scale), out_shape=...]
where the time goes in v5:
time: 122 us
  Pallas kernels  120 us (98%)
  between operations  1.47 us (1%)
    pallas_call x1, Pallas kernels, fused_shards(): pl.pallas_call(functools.partial(layer_kernel, groups, scale), out_shape=...  118 us
    pallas_call x1, Pallas kernels, fused_shards(): pl.pallas_call(functools.partial(output_kernel, groups), out_shape=(jax.S...  2.61 us

profile of v5, /device:TPU:0, one launch (start us, length us, event | category | flops | bytes accessed | tf_op | source)
XLA Modules:
  0.0 121.6 jit_solution(16665995606415368310)
XLA Ops:
  1.3 117.5 %layer.1 = (bf16[128,1024]{1,0:T(8,128)(2,1)}, f32[128,1024]{1,0:T(8,128)}, bf16[8,32,384]{2,1,0:T(8,128)(2,1)}, f32[32,1024]{1,0:T(8,128)}, bf16[8,32,512]{2,1,...) custom-call(bf16[128,1024]{1,0:T(8,128)(2,1)} %bitcast.11, bf16[128,1024]{1,0:T(8,128)(2,1)} %bitcast.12, ...), custom_call_target="tpu_custom_call" | custom-call | tf_op jit(solution)/shard_map/layer/pallas_call | solution.py:1463
  118.8 2.6 %outputs.1 = (bf16[1,128,1024]{2,1,0:T(8,128)(2,1)}, f32[1,128,1024]{2,1,0:T(8,128)}, f32[32]{0:T(128)}, f32[32]{0:T(128)}, f32[32,3072]{1,0:T(8,128)}, /*index=...) custom-call(bf16[128,1024]{1,0:T(8,128)(2,1)} %get-tuple-element.22., ...), custom_call_target="tpu_custom_call" | custom-call | tf_op jit(solution)/shard_map/outputs/pallas_call | solution.py:1576

commit v6 on v5

--- a/solution.py
+++ b/solution.py
@@ -362,7 +362,7 @@
 F32 = jnp.float32
 BF16 = jnp.bfloat16
 MESH = pl.DeviceIdType.MESH
-SENDS, RECVS, LOCALS = 93, 137, 31
+SENDS, RECVS, LOCALS = 43, 123, 19
 SLAB = 8
 
 
@@ -434,9 +434,9 @@
         self.recvs += count
         return [self.recv_sems.at[first + i] for i in range(count)]
 
-    def batch(self, whole):
+    def batch(self, whole, far=False):
         spot = self.take()
-        self.open_sends.append((lambda: self.describe(whole, whole, spot, self.recv_sems.at[0], self.near()), None, spot, False))
+        self.open_sends.append((lambda: self.describe(whole, whole, spot, self.recv_sems.at[0], self.near()), None, spot, far))
         return spot
 
     def near(self):
@@ -495,38 +495,43 @@
         else:
             pl.when(when)(wait)
 
-    def local(self, src, dst):
-        copy = pltpu.make_async_copy(src, dst, self.local_sems.at[self.locals])
+    def local(self, src, dst, more=()):
+        sem = self.local_sems.at[self.locals]
         self.locals += 1
-        copy.start()
-        return copy
+        for one in more or ((src, dst),):
+            pltpu.make_async_copy(*one, sem).start()
+        return pltpu.make_async_copy(dst, dst, sem)
 
 
 class SlabGather:
-    def __init__(self, wire, at, half):
-        self.wire, self.at, self.half = wire, at, half
-        self.slots = wire.recv_slots(11)
+    def __init__(self, wire, at, half, several, apart):
+        self.wire, self.at, self.half, self.several, self.apart = wire, at, half, several, apart
+        self.slots = wire.recv_slots(11 if apart else 7)
+        if not apart:
+            self.slots += self.slots[6:7] * 4
 
     def start(self, whole, halves):
         wire, place, slots = self.wire, self.wire.place, self.slots
         t, r = place.t, place.r
-        wire.send(halves[0], self.half(t, 0), slots[0], (r, place.peer(4)))
-        wire.send(halves[1], self.half(t, 1), slots[3], (r, place.peer(1)))
-        wire.send(halves[1], self.half(t, 1), slots[1], (r, place.peer(4)))
-        wire.send(halves[0], self.half(t, 0), slots[2], (r, place.peer(1)))
-        wire.send(whole, self.at(t), slots[6], (r, place.peer(2)))
+        batch = wire.batch(self.several(3))
+        wire.send(halves[0], self.half(t, 0), slots[0], (r, place.peer(4)), batch=batch)
+        wire.send(halves[1], self.half(t, 1), slots[3], (r, place.peer(1)), batch=batch)
+        wire.send(halves[1], self.half(t, 1), slots[1], (r, place.peer(4)), batch=batch)
+        wire.send(halves[0], self.half(t, 0), slots[2], (r, place.peer(1)), batch=batch)
+        wire.send(whole, self.at(t), slots[6], (r, place.peer(2)), batch=batch)
 
     def relay(self):
         wire, place, slots = self.wire, self.wire.place, self.slots
         r, far, near = place.r, place.peer(4), place.peer(1)
+        self.passed = wire.batch(self.several(4))
         wire.arrived(self.half(far, 0), slots[0])
-        wire.send(self.half(far, 0), self.half(far, 0), slots[4], (r, near))
+        wire.send(self.half(far, 0), self.half(far, 0), slots[4], (r, near), batch=self.passed)
         wire.arrived(self.half(near, 1), slots[3])
-        wire.send(self.half(near, 1), self.half(near, 1), slots[5], (r, far))
+        wire.send(self.half(near, 1), self.half(near, 1), slots[5], (r, far), batch=self.passed)
         wire.arrived(self.half(far, 1), slots[1])
-        wire.send(self.at(far), self.at(far), slots[7], (r, place.peer(2)))
+        wire.send(self.at(far), self.at(far), slots[7], (r, place.peer(2)), batch=self.passed)
         wire.arrived(self.half(near, 0), slots[2])
-        wire.send(self.at(near), self.at(near), slots[8], (r, place.peer(2)))
+        wire.send(self.at(near), self.at(near), slots[8], (r, place.peer(2)), batch=self.passed)
 
     def forward(self):
         wire, place, slots = self.wire, self.wire.place, self.slots
@@ -534,7 +539,7 @@
         for h in range(2):
             block = self.half(across, h)
             wire.arrived(block, slots[4 + h])
-            wire.send(block, block, slots[9 + h], (place.r, place.peer(2)))
+            wire.send(block, block, slots[9 + h], (place.r, place.peer(2)), batch=self.passed)
 
     def wait_block(self, mask):
         wire, place, slots = self.wire, self.wire.place, self.slots
@@ -545,8 +550,7 @@
             wire.arrived(self.at(place.peer(mask)), slots[{2: 6, 6: 7, 3: 8}[mask]])
 
     def wait(self):
-        for mask in (2, 6, 3, 7):
-            self.wait_block(mask)
+        self.wire.arrived(self.several(4), self.slots[6])
 
 
 class SlabScatter:
@@ -558,12 +562,14 @@
 
     def cores(self):
         place = self.wire.place
+        batch = self.wire.batch(self.core_in)
         for i, mask in enumerate(self.order):
             self.wire.send(
                 rows(self.part, place.peer(mask ^ 2), self.block),
                 self.core_in.at[i],
                 self.core_slots[i],
                 (place.r, place.peer(2)),
+                batch=batch,
             )
 
     def half(self, mask, h):
@@ -578,13 +584,14 @@
     def chips(self):
         wire, place = self.wire, self.wire.place
         far, near = (place.r, place.peer(4)), (place.r, place.peer(1))
+        self.passed = wire.batch(self.chip_in)
         self.add_core(0)
-        wire.send(self.half(5, 0), self.chip_in.at[0], self.slots[0], far)
-        wire.send(self.half(5, 1), self.chip_in.at[1], self.slots[1], near)
+        wire.send(self.half(5, 0), self.chip_in.at[0], self.slots[0], far, batch=self.passed)
+        wire.send(self.half(5, 1), self.chip_in.at[1], self.slots[1], near, batch=self.passed)
         self.add_core(1)
-        wire.send(self.half(4, 0), self.chip_in.at[2], self.slots[2], far)
+        wire.send(self.half(4, 0), self.chip_in.at[2], self.slots[2], far, batch=self.passed)
         self.add_core(2)
-        wire.send(self.half(1, 1), self.chip_in.at[3], self.slots[3], near)
+        wire.send(self.half(1, 1), self.chip_in.at[3], self.slots[3], near, batch=self.passed)
         wire.arrived(self.core_in.at[3], self.core_slots[3])
 
     def relay(self):
@@ -593,7 +600,7 @@
         for i, (block, to) in enumerate(((self.half(1, 0), near), (self.half(4, 1), far))):
             wire.arrived(self.chip_in.at[i], self.slots[i])
             block[...] = (block[...].astype(F32) + self.chip_in[i].astype(F32)).astype(BF16)
-            wire.send(block, self.chip_in.at[4 + i], self.slots[4 + i], to)
+            wire.send(block, self.chip_in.at[4 + i], self.slots[4 + i], to, batch=self.passed)
 
     def wait(self):
         for i in range(2, 6):
@@ -628,7 +635,7 @@
 class GroupGather:
     def __init__(self, wire, at):
         self.wire, self.at = wire, at
-        self.slots = wire.recv_slots(4)
+        self.slots = [None] + wire.recv_slots(3)
         self.first = wire.recvs - 4
         r = wire.place.r
         self.inner, self.outer = (r + 1) // 2 == 1, (r + 1) // 2 != 1
@@ -663,68 +670,57 @@
 
 
 class GroupScatter:
-    def __init__(self, wire, out, into, own, passing):
-        self.wire, self.out, self.into, self.own, self.passing = wire, out, into, own, passing
+    def __init__(self, wire, out, into, own):
+        self.wire, self.out, self.into, self.own = wire, out, into, own
         self.slots = wire.recv_slots(5)
-        self.first = wire.recvs - 5
+        self.spots = {}
         r = wire.place.r
-
-        @pl.when(r == 0)
-        def _():
-            into[0] = jnp.zeros_like(into[0])
-
-        @pl.when(r == 3)
+        self.inner, self.outer = (r + 1) // 2 == 1, (r + 1) // 2 != 1
+        low = 1 - r // 2
+        self.far, self.next = (r + 1 + 2 * low) % 4, (r + 3 - 2 * low) % 4
+
+        @pl.when(self.outer)
         def _():
             into[2] = jnp.zeros_like(into[2])
 
-    def start(self, make, hold=None):
-        wire, place = self.wire, self.wire.place
-        r, t = place.r, place.t
-        inner = (r + 1) // 2 == 1
-        outer = (r + 1) // 2 != 1
-        low = 1 - r // 2
-        pair = r + 1 - 2 * (r % 2)
-        first, last = 1 + 2 * low, 3 - 2 * low
-        self.out[0] = make((r + first) % 4).astype(BF16)
-        wire.send(self.out.at[0], self.passing, self.slots[0], (pair, t), outer)
-        wire.send(self.out.at[0], self.into.at[first - 1], wire.recv_sems.at[self.first + first], (pair, t), inner)
-        self.out[1] = make((r + 2) % 4).astype(BF16)
-        wire.send(self.out.at[1], self.into.at[1], self.slots[2], ((r + 2) % 4, t), outer)
-        self.out[2] = make((r + last) % 4).astype(BF16)
-        self.last = last
-        if not hold:
-            self.start_last()
-        elif hold == "outer":
-            self.start_last(inner)
+    def put(self, k, spot, to, when):
+        if k not in self.spots:
+            self.spots[k] = self.wire.batch(self.out.at[k], far=True)
+        to = (to, self.wire.place.t)
+        self.wire.send(self.out.at[k], self.into.at[spot], self.slots[spot], to, when, self.spots[k])
+
+    def start(self, make, hold=False):
+        r = self.wire.place.r
+        for k, to in enumerate((self.far, (r + 2) % 4, self.next)):
+            self.out[k] = make(to).astype(BF16)
+            if k < 2 or not hold:
+                self.put(k, k, self.next, self.outer)
         self.own[...] = make(r)
 
-    def start_last(self, when=None):
-        wire, place = self.wire, self.wire.place
-        to = (place.r + self.last) % 4
-        slot = wire.recv_sems.at[self.first + self.last]
-        wire.send(self.out.at[2], self.into.at[self.last - 1], slot, (to, place.t), when)
+    def start_last(self):
+        self.put(2, 2, self.next, self.outer)
+
+    def add(self, k, spot):
+        self.wire.arrived(self.into.at[spot], self.slots[spot], self.inner)
+
+        @pl.when(self.inner)
+        def _():
+            self.out[k] = (self.out[k].astype(F32) + self.into[spot].astype(F32)).astype(BF16)
 
     def relay(self):
-        wire, place = self.wire, self.wire.place
-        r = place.r
-        inner = (r + 1) // 2 == 1
-        wire.arrived(self.passing, self.slots[0], inner)
-
-        @pl.when(inner)
-        def _():
-            self.out[1] = (self.out[1].astype(F32) + self.passing[...].astype(F32)).astype(BF16)
-
-        wire.send(self.out.at[1], self.into.at[1], self.slots[2], ((r + 2) % 4, place.t), inner)
+        self.add(1, 0)
+        self.put(1, 3, self.next, self.inner)
+        self.add(2, 1)
+        self.put(2, 4, self.next, self.inner)
+
+    def relay_end(self):
+        self.add(0, 3)
+        self.put(0, 4, self.far, self.inner)
 
     def total(self):
-        wire, r = self.wire, self.wire.place.r
-        wire.arrived(self.into.at[1], self.slots[2])
-        wire.arrived(self.into.at[0], self.slots[1], r != 0)
-        wire.arrived(self.into.at[2], self.slots[3], r != 3)
-        total = self.own[...]
-        for i in range(3):
-            total = total + self.into[i].astype(F32)
-        return total
+        self.wire.arrived(self.into.at[2], self.slots[2], self.inner)
+        self.wire.arrived(self.into.at[4], self.slots[4])
+        return self.own[...] + self.into[2].astype(F32) + self.into[4].astype(F32)
 
 
 def layer_kernel(
@@ -804,23 +800,19 @@
     sh_out,
     sh_in,
     sh_own,
-    sh_pass,
     ex_out,
     ex_in,
     ex_own,
-    ex_pass,
     ex_sum,
     ex_all,
     in_out,
     in_in,
     in_own,
-    in_pass,
     in_sum,
     in_all,
     ou_out,
     ou_in,
     ou_own,
-    ou_pass,
     gvec,
     gvec_exp,
     gvec_out,
@@ -858,7 +850,7 @@
         second_shift,
         shrink_bias,
     )
-    loads = [wire.local(ref, small.at[k]) for k, ref in enumerate(vectors)]
+    loads = [wire.local(None, small, [(ref, small.at[k]) for k, ref in enumerate(vectors)])]
     loads.append(wire.local(expand_bias, wide_small))
     barrier = pltpu.get_barrier_semaphore()
     for i in range(1, devices):
@@ -880,8 +872,8 @@
         wire.send(pack, packs.at[f], pack_slot, (to // 4, (to % 4) * 2 + y), batch=pack_batch)
     own_pack = wire.local(pack, packs.at[f])
 
-    in_slots = wire.recv_slots(4)
-    ex_slots = wire.recv_slots(4)
+    in_slots = [None] + wire.recv_slots(3)
+    ex_slots = [None] + wire.recv_slots(3)
 
     def in_piece(index, c):
         return win.at[pl.ds(pl.multiple_of(index * own_rows, own_rows), own_rows), pl.ds(c * head2, head2)]
@@ -896,9 +888,10 @@
         for c in range(3):
             src = w_in.at[:, pl.ds(pl.multiple_of(c * width + to * head2, head2), head2)]
             if i == 0:
-                own_in.append(wire.local(src, in_piece(f, c)))
+                own_in.append((src, in_piece(f, c)))
             else:
                 wire.send(src, in_piece(f, c), in_slots[i], (r, to), batch=in_batch)
+    own_in = wire.local(None, rows(win, f, own_rows), own_in)
 
     out_share = w_out.at[pl.ds(pl.multiple_of(y * share, share), share), :]
     own_out = wire.local(out_share, wo.at[r, t])
@@ -915,8 +908,14 @@
 
     shr_half(0)
 
-    def slab_gather(ref):
-        return SlabGather(wire, lambda at: rows(ref, at, seg), lambda at, h: rows(ref, at * 2 + h, seg // 2))
+    def slab_gather(ref, apart=True):
+        return SlabGather(
+            wire,
+            lambda at: rows(ref, at, seg),
+            lambda at, h: rows(ref, at * 2 + h, seg // 2),
+            lambda count: ref.at[pl.ds(0, count * seg), :],
+            apart,
+        )
 
     gather_tok = slab_gather(tok_all)
     gather_tok.start(tokens, [rows(tokens, h, seg // 2) for h in range(2)])
@@ -928,9 +927,10 @@
         for c in range(groups):
             src = w_exp.at[:, pl.ds(pl.multiple_of((c * SLAB + to) * chunk, chunk), chunk)]
             if i == 0:
-                own_ex.append(wire.local(src, ex_piece(f, c)))
+                own_ex.append((src, ex_piece(f, c)))
             else:
                 wire.send(src, ex_piece(f, c), ex_slots[i], (r, to), batch=ex_batch)
+    own_ex = wire.local(None, rows(wex, f, own_rows), own_ex)
 
     row_at = y * seg + lax.broadcasted_iota(jnp.int32, (seg, 1), 0)
     row_valid = row_at.astype(F32) < pack[10:11, 0:1].astype(F32)
@@ -938,16 +938,15 @@
     gls_all[pl.ds(pl.multiple_of(t * seg, seg), seg), :] = gls[...]
     gvec[...] = jnp.zeros_like(gvec)
     gvec_exp[...] = jnp.zeros_like(gvec_exp)
-    group_shr = GroupScatter(wire, sh_out, sh_in, sh_own, sh_pass)
-    group_exp = GroupScatter(wire, ex_out, ex_in, ex_own, ex_pass)
-    group_inw = GroupScatter(wire, in_out, in_in, in_own, in_pass)
-    group_out = GroupScatter(wire, ou_out, ou_in, ou_own, ou_pass)
+    group_shr = GroupScatter(wire, sh_out, sh_in, sh_own)
+    group_exp = GroupScatter(wire, ex_out, ex_in, ex_own)
+    group_inw = GroupScatter(wire, in_out, in_in, in_own)
+    group_out = GroupScatter(wire, ou_out, ou_in, ou_own)
 
     for i in range(1, 4):
         frm = r * 4 + (xc + 4 - i) % 4
         wire.arrived(rows(win, frm, own_rows), in_slots[i])
-    for copy in own_in:
-        copy.wait()
+    own_in.wait()
     own_out.wait()
     group_wo.pass_on()
     group_in = GroupGather(wire, lambda at: rows(win, at, slab_rows))
@@ -985,7 +984,13 @@
 
     gather_tok.relay()
     group_wo.wait()
-    gather_wo = SlabGather(wire, lambda at: wo.at[:, at], lambda at, h: wo.at[pl.ds(h * (groups // 2), groups // 2), at])
+    gather_wo = SlabGather(
+        wire,
+        lambda at: wo.at[:, at],
+        lambda at, h: wo.at[pl.ds(h * (groups // 2), groups // 2), at],
+        lambda count: wo.at[:, pl.ds(0, count)],
+        apart=False,
+    )
     gather_wo.start(wo.at[:, t], [wo.at[pl.ds(h * (groups // 2), groups // 2), t] for h in range(2)])
     group_in.pass_on()
     norm_block(4)
@@ -998,8 +1003,7 @@
     for i in range(1, 4):
         frm = r * 4 + (xc + 4 - i) % 4
         wire.arrived(rows(wex, frm, own_rows), ex_slots[i])
-    for copy in own_ex:
-        copy.wait()
+    own_ex.wait()
     group_ex = GroupGather(wire, lambda at: rows(wex, at, slab_rows))
     group_ex.start(rows(wex, r, slab_rows))
 
@@ -1009,7 +1013,7 @@
         norm_block(mask)
 
     gather_wo.relay()
-    gather_gls = slab_gather(gls_all)
+    gather_gls = slab_gather(gls_all, apart=False)
     gather_gls.start(gls, [rows(gls, h, seg // 2) for h in range(2)])
     group_in.wait()
     at_head = pl.ds(pl.multiple_of(t * head2, head2), head2)
@@ -1111,7 +1115,7 @@
 
     group_shr.start(
         lambda c: matmul_at(active[:, pl.ds(pl.multiple_of(c * chunk, chunk), chunk)], gls_all[...]),
-        hold="outer",
+        hold=True,
     )
     group_sh.wait()
     own_shr.wait()
@@ -1187,6 +1191,7 @@
     scatter_out = SlabScatter(wire, part_d, core_d, chip_d, seg)
     scatter_out.cores()
 
+    group_shr.relay_end()
     scatter_out.chips()
     swap_gblend.wait()
 
@@ -1229,22 +1234,20 @@
 
     group_inw.start(
         lambda c: matmul_at(first_all[:, pl.ds(pl.multiple_of(c * slab_rows, slab_rows), slab_rows)], gqkv[...]),
-        hold="all",
+        hold=True,
     )
     scatter_first.chips()
     gvec[2:3, at_head] = jnp.sum(gqkv[:, 0:head2].astype(F32), axis=0, keepdims=True)
     gvec[3:4, at_head] = jnp.sum(gqkv[:, 2 * head2 :].astype(F32), axis=0, keepdims=True)
 
     scatter_out.wait()
-    group_out.start(lambda c: scatter_out.total(c * share, share), hold="outer")
-    outer = (r + 1) // 2 != 1
-    group_inw.start_last(outer)
-    group_out.start_last(outer)
-    group_shr.start_last(outer)
+    group_out.start(lambda c: scatter_out.total(c * share, share), hold=True)
+    group_inw.start_last()
+    group_out.start_last()
     scatter_first.relay()
+    group_exp.relay_end()
     scatter_result.chips()
     group_inw.relay()
-    group_inw.start_last((r + 1) // 2 == 1)
     scatter_first.wait()
     wire.settle(feed_sends, slab_only=True)
 
@@ -1269,6 +1272,7 @@
     swap_vec = SlabSwap(wire, lambda at: gvec_out.at[at], lambda at: gvec_in.at[at], gvec_in.at[pl.ds(0, 7)])
     swap_vec.start()
 
+    group_inw.relay_end()
     scatter_result.relay()
     ex_sum[...] = group_exp.total().astype(BF16)
     swap_exp = SlabSwap(wire, lambda at: rows(ex_sum, at, share), lambda at: ex_all.at[at], ex_all.at[pl.ds(0, 7)])
@@ -1284,6 +1288,8 @@
     vec_slots = wire.recv_slots(groups - 1)
     for i in range(1, groups):
         wire.send(gvec_sum, gvec_far.at[i - 1], vec_slots[i - 1], ((r + i) % groups, t))
+    group_shr.start_last()
+    group_out.relay_end()
     in_sum[...] = group_inw.total().astype(BF16)
     swap_in = SlabSwap(wire, lambda at: rows(in_sum, at, share), lambda at: in_all.at[at], in_all.at[pl.ds(0, 7)])
     swap_in.start()
@@ -1516,25 +1522,21 @@
             pltpu.VMEM((seg, width), BF16),
             pltpu.VMEM((total_rows, head2), BF16),
             pltpu.VMEM((groups - 1, chunk, width), BF16),
-            pltpu.VMEM((groups - 1, chunk, width), BF16),
+            pltpu.VMEM((5, chunk, width), BF16),
             pltpu.VMEM((chunk, width), F32),
-            pltpu.VMEM((chunk, width), BF16),
             pltpu.VMEM((groups - 1, slab_rows, units), BF16),
-            pltpu.VMEM((groups - 1, slab_rows, units), BF16),
+            pltpu.VMEM((5, slab_rows, units), BF16),
             pltpu.VMEM((slab_rows, units), F32),
-            pltpu.VMEM((slab_rows, units), BF16),
             pltpu.VMEM((slab_rows, units), BF16),
             pltpu.VMEM((SLAB, share, units), BF16),
             pltpu.VMEM((groups - 1, slab_rows, 3 * head2), BF16),
-            pltpu.VMEM((groups - 1, slab_rows, 3 * head2), BF16),
+            pltpu.VMEM((5, slab_rows, 3 * head2), BF16),
             pltpu.VMEM((slab_rows, 3 * head2), F32),
-            pltpu.VMEM((slab_rows, 3 * head2), BF16),
             pltpu.VMEM((slab_rows, 3 * head2), BF16),
             pltpu.VMEM((SLAB, share, 3 * head2), BF16),
             pltpu.VMEM((groups - 1, share, width), BF16),
-            pltpu.VMEM((groups - 1, share, width), BF16),
+            pltpu.VMEM((5, share, width), BF16),
             pltpu.VMEM((share, width), F32),
-            pltpu.VMEM((share, width), BF16),
             pltpu.VMEM((8, width), F32),
             pltpu.VMEM((1, units), F32),
             pltpu.VMEM((SLAB, 8, 128), F32),

time: 122 us -> 120 us (0.984)
  Pallas kernels: 120 us -> 118 us
    pallas_call x1, Pallas kernels: 118 us -> 115 us  [fused_shards(): pl.pallas_call(functools.partial(layer_kernel, groups, scale), out_shape=...]
where the time goes in v6:
time: 120 us; the launch traced here: 119 us
  Pallas kernels  118 us (98%)
  between operations  1.47 us (1%)
    pallas_call x1, Pallas kernels, fused_shards(): pl.pallas_call(functools.partial(layer_kernel, groups, scale), out_shape=...  115 us
    pallas_call x1, Pallas kernels, fused_shards(): pl.pallas_call(functools.partial(output_kernel, groups), out_shape=(jax.S...  2.61 us

profile of v6, /device:TPU:0, one launch (start us, length us, event | category | flops | bytes accessed | tf_op | source)
XLA Modules:
  0.0 119.3 jit_solution(17296901538338383489)
XLA Ops:
  1.3 115.2 %layer.1 = (bf16[128,1024]{1,0:T(8,128)(2,1)}, f32[128,1024]{1,0:T(8,128)}, bf16[8,32,384]{2,1,0:T(8,128)(2,1)}, f32[32,1024]{1,0:T(8,128)}, bf16[8,32,512]{2,1,...) custom-call(bf16[128,1024]{1,0:T(8,128)(2,1)} %bitcast.11, bf16[128,1024]{1,0:T(8,128)(2,1)} %bitcast.12, ...), custom_call_target="tpu_custom_call" | custom-call | tf_op jit(solution)/shard_map/layer/pallas_call | solution.py:1469
  116.5 2.6 %outputs.1 = (bf16[1,128,1024]{2,1,0:T(8,128)(2,1)}, f32[1,128,1024]{2,1,0:T(8,128)}, f32[32]{0:T(128)}, f32[32]{0:T(128)}, f32[32,3072]{1,0:T(8,128)}, /*index=...) custom-call(bf16[128,1024]{1,0:T(8,128)(2,1)} %get-tuple-element.22., ...), custom_call_target="tpu_custom_call" | custom-call | tf_op jit(solution)/shard_map/outputs/pallas_call | solution.py:1578

commit v7 on v6

--- a/solution.py
+++ b/solution.py
@@ -362,7 +362,7 @@
 F32 = jnp.float32
 BF16 = jnp.bfloat16
 MESH = pl.DeviceIdType.MESH
-SENDS, RECVS, LOCALS = 43, 123, 19
+SENDS, RECVS, LOCALS = 42, 123, 22
 SLAB = 8
 
 
@@ -707,9 +707,11 @@
         def _():
             self.out[k] = (self.out[k].astype(F32) + self.into[spot].astype(F32)).astype(BF16)
 
-    def relay(self):
+    def relay_far(self):
         self.add(1, 0)
         self.put(1, 3, self.next, self.inner)
+
+    def relay_next(self):
         self.add(2, 1)
         self.put(2, 4, self.next, self.inner)
 
@@ -726,9 +728,9 @@
 def layer_kernel(
     groups,
     scale,
-    tokens,
-    upstream,
-    visible,
+    tokens_hbm_in,
+    upstream_hbm_in,
+    visible_hbm,
     first_gain,
     first_shift,
     query_bias,
@@ -754,6 +756,9 @@
     out_grad,
     shr_grad,
     vec_grad,
+    tokens,
+    upstream,
+    visible,
     pack,
     small,
     wide_small,
@@ -852,6 +857,9 @@
     )
     loads = [wire.local(None, small, [(ref, small.at[k]) for k, ref in enumerate(vectors)])]
     loads.append(wire.local(expand_bias, wide_small))
+    loads.append(wire.local(visible_hbm, visible))
+    early = wire.local(tokens_hbm_in, tokens)
+    late = wire.local(upstream_hbm_in, upstream)
     barrier = pltpu.get_barrier_semaphore()
     for i in range(1, devices):
         to = (me + i) % devices
@@ -917,6 +925,7 @@
             apart,
         )
 
+    early.wait()
     gather_tok = slab_gather(tok_all)
     gather_tok.start(tokens, [rows(tokens, h, seg // 2) for h in range(2)])
 
@@ -932,6 +941,7 @@
                 wire.send(src, ex_piece(f, c), ex_slots[i], (r, to), batch=ex_batch)
     own_ex = wire.local(None, rows(wex, f, own_rows), own_ex)
 
+    late.wait()
     row_at = y * seg + lax.broadcasted_iota(jnp.int32, (seg, 1), 0)
     row_valid = row_at.astype(F32) < pack[10:11, 0:1].astype(F32)
     gls[...] = jnp.where(row_valid, upstream[...].astype(F32), 0.0).astype(BF16)
@@ -1139,7 +1149,7 @@
         lambda c: matmul_at(second_all[:, pl.ds(pl.multiple_of(c * slab_rows, slab_rows), slab_rows)], ghid[...])
     )
     scatter_second.relay()
-    group_shr.relay()
+    group_shr.relay_far()
 
     def feed_out(i, carry):
         at = pl.ds(pl.multiple_of(i * tile, tile), tile)
@@ -1191,10 +1201,12 @@
     scatter_out = SlabScatter(wire, part_d, core_d, chip_d, seg)
     scatter_out.cores()
 
-    group_shr.relay_end()
+    group_shr.relay_next()
     scatter_out.chips()
     swap_gblend.wait()
 
+    group_shr.relay_end()
+    group_exp.relay_far()
     def attend_back(i, carry):
         at = pl.ds(pl.multiple_of(i * slots, slots), slots)
         q = qkv[at, 0:head2]
@@ -1221,7 +1233,7 @@
     lax.fori_loop(0, clips, attend_back, 0)
 
     scatter_out.relay()
-    group_exp.relay()
+    group_exp.relay_next()
     def project_back(i, carry):
         at = pl.ds(pl.multiple_of(i * tile, tile), tile)
         part_c[at, :] = matmul_bt(gqkv[at, :], win[...]).astype(BF16)
@@ -1247,10 +1259,14 @@
     scatter_first.relay()
     group_exp.relay_end()
     scatter_result.chips()
-    group_inw.relay()
+    group_inw.relay_far()
     scatter_first.wait()
     wire.settle(feed_sends, slab_only=True)
 
+    group_inw.relay_next()
+    group_out.relay_far()
+    group_out.relay_next()
+    group_inw.relay_end()
     def first_back(i, carry):
         first = i * strip
         at = pl.ds(pl.multiple_of(first, strip), strip)
@@ -1264,7 +1280,6 @@
     lax.fori_loop(0, seg // strip, first_back, 0)
     stores = [wire.local(tokens_grad, tokens_hbm)]
 
-    group_out.relay()
     for to in range(SLAB):
         gvec_out[to] = jnp.concatenate(
             [gvec[:, (c * SLAB + to) * share : (c * SLAB + to + 1) * share] for c in range(groups)], axis=1
@@ -1272,7 +1287,6 @@
     swap_vec = SlabSwap(wire, lambda at: gvec_out.at[at], lambda at: gvec_in.at[at], gvec_in.at[pl.ds(0, 7)])
     swap_vec.start()
 
-    group_inw.relay_end()
     scatter_result.relay()
     ex_sum[...] = group_exp.total().astype(BF16)
     swap_exp = SlabSwap(wire, lambda at: rows(ex_sum, at, share), lambda at: ex_all.at[at], ex_all.at[pl.ds(0, 7)])
@@ -1477,7 +1491,7 @@
             jax.ShapeDtypeStruct((chunk, width), F32),
             jax.ShapeDtypeStruct((16, 128), F32),
         ),
-        in_specs=[vmem, vmem, pl.BlockSpec(memory_space=pltpu.SMEM)] + [anywhere] * 13,
+        in_specs=[anywhere] * 2 + [pl.BlockSpec(memory_space=pltpu.HBM)] + [anywhere] * 13,
         out_specs=[anywhere] * 7,
         scratch_shapes=[
             pltpu.VMEM((seg, width), BF16),
@@ -1485,6 +1499,9 @@
             pltpu.VMEM((share, width), F32),
             pltpu.VMEM((chunk, width), F32),
             pltpu.VMEM((16, 128), F32),
+            pltpu.VMEM((seg, width), BF16),
+            pltpu.VMEM((seg, width), BF16),
+            pltpu.SMEM((1,), jnp.int32),
             pltpu.VMEM((16, 128), BF16),
             pltpu.VMEM((8, 1, own_rows), BF16),
             pltpu.VMEM((2, 128), BF16),

time: 120 us -> 118 us (0.983)
  Pallas kernels: 118 us -> 116 us
    pallas_call x1, Pallas kernels: 115 us -> 114 us  [fused_shards(): pl.pallas_call(functools.partial(layer_kernel, groups, scale), out_shape=...]
where the time goes in v7:
time: 118 us
  Pallas kernels  116 us (98%)
  between operations  1.47 us (1%)
    pallas_call x1, Pallas kernels, fused_shards(): pl.pallas_call(functools.partial(layer_kernel, groups, scale), out_shape=...  114 us
    pallas_call x1, Pallas kernels, fused_shards(): pl.pallas_call(functools.partial(output_kernel, groups), out_shape=(jax.S...  2.61 us

profile of v7, /device:TPU:0, one launch (start us, length us, event | category | flops | bytes accessed | tf_op | source)
XLA Modules:
  0.0 117.9 jit_solution(4073489212427599289)
XLA Ops:
  1.3 113.9 %layer.1 = (bf16[128,1024]{1,0:T(8,128)(2,1)}, f32[128,1024]{1,0:T(8,128)}, bf16[8,32,384]{2,1,0:T(8,128)(2,1)}, f32[32,1024]{1,0:T(8,128)}, bf16[8,32,512]{2,1,...) custom-call(bf16[128,1024]{1,0:T(8,128)(2,1)} %bitcast.11, bf16[128,1024]{1,0:T(8,128)(2,1)} %bitcast.12, ...), custom_call_target="tpu_custom_call" | custom-call | tf_op jit(solution)/shard_map/layer/pallas_call | solution.py:1483
  115.2 2.6 %outputs.1 = (bf16[1,128,1024]{2,1,0:T(8,128)(2,1)}, f32[1,128,1024]{2,1,0:T(8,128)}, f32[32]{0:T(128)}, f32[32]{0:T(128)}, f32[32,3072]{1,0:T(8,128)}, /*index=...) custom-call(bf16[128,1024]{1,0:T(8,128)(2,1)} %get-tuple-element.22., ...), custom_call_target="tpu_custom_call" | custom-call | tf_op jit(solution)/shard_map/outputs/pallas_call | solution.py:1595
